TPU v7x, 32 devices: a whole 2x2x4 slice. The times are simulated.
32 devices in a mesh: fsdp: 16 (over z, y, x), mp: 2 (over core).
Axes of the slice: x: 2, y: 2, z: 4, core: 2. Of those that a mesh axis runs over, the one named last changes fastest.
Arguments:
- values: bfloat16 [4096, 32], P('fsdp'), may hold values from -6 to 6
- lengths: int32 [64], P('fsdp'), may hold values from 1 to 64, 2560 in all
- w_in1: bfloat16 [64, 1280], P(None, 'fsdp'), may hold values from -0.75 to 0.75
- b_in1: bfloat16 [1280], P('fsdp'), may hold values from -3 to 3
- w_in2: bfloat16 [1280, 1280], P('fsdp'), may hold values from -0.15625 to 0.15625
- b_in2: bfloat16 [1280], P('fsdp'), may hold values from -3 to 3
- w_res: bfloat16 [64, 1280], P(None, 'fsdp'), may hold values from -0.75 to 0.75
- g_attn: bfloat16 [1280], P('fsdp'), may hold values from 0.099609375 to 1.8984375
- w_qkv: bfloat16 [1280, 3, 1280], P('fsdp', None, 'mp'), may hold values from -0.15625 to 0.15625
- w_out: bfloat16 [1280, 1280], P('mp', 'fsdp'), may hold values from -0.5 to 0.5
- g_mlp: bfloat16 [1280], P('fsdp'), may hold values from 0.099609375 to 1.8984375
- w_up: bfloat16 [1280, 1280], P('fsdp', 'mp'), may hold values from -0.15625 to 0.15625
- w_down: bfloat16 [1280, 1280], P('mp', 'fsdp'), may hold values from -0.25 to 0.25
- cotangent: bfloat16 [4096, 1280], P('fsdp'), may hold values from -6 to 6
Outputs:
- output: bfloat16 [4096, 1280], P('fsdp')
- d_values: float32 [4096, 32], P('fsdp')
- d_w_in1: float32 [64, 1280], P(None, 'fsdp')
- d_b_in1: float32 [1280], P('fsdp')
- d_w_in2: float32 [1280, 1280], P('fsdp')
- d_b_in2: float32 [1280], P('fsdp')
- d_w_res: float32 [64, 1280], P(None, 'fsdp')
- d_g_attn: float32 [1280], P('fsdp')
- d_w_qkv: float32 [1280, 3, 1280], P('fsdp', None, 'mp')
- d_w_out: float32 [1280, 1280], P('mp', 'fsdp')
- d_g_mlp: float32 [1280], P('fsdp')
- d_w_up: float32 [1280, 1280], P('fsdp', 'mp')
- d_w_down: float32 [1280, 1280], P('mp', 'fsdp')
Inputs may be any that keep to these rules, and one draw needn't show every extreme that they name: `lengths`: patches of series s; its padded slots come first.
All inputs are finite; a program needn't handle non-finite values. No bound on the sum of `lengths` on one device may be relied on, other than what follows from the above.
Results may differ from a plain program's by a relative error of at most 0.014.
Values may be sent and summed in bfloat16 or wider, within the bound.
A program may use at most 192 MiB of HBM per device.

v0:
```python
import jax
import jax.numpy as jnp
from jax import lax
from jax.sharding import PartitionSpec as P

HD = 80


def rotate(vectors, places):
    half_width = vectors.shape[-1] // 2
    frequency = 10000.0 ** (-2.0 * jnp.arange(half_width, dtype=jnp.float32) / vectors.shape[-1])
    angles = places[:, :, None, None] * frequency
    cosine = jnp.cos(angles)
    sine_val = jnp.sin(angles)
    first_half = vectors[..., :half_width]
    second_half = vectors[..., half_width:]
    return jnp.concatenate(
        [
            first_half * cosine - second_half * sine_val,
            second_half * cosine + first_half * sine_val,
        ],
        -1,
    )


def rms_norm(resid_rows, gain_vec):
    return (
        resid_rows
        * lax.rsqrt(jnp.mean(resid_rows * resid_rows, -1, keepdims=True) + 1e-06)
        * gain_vec
    )


def activate(up_rows):
    return jax.nn.gelu(up_rows, approximate=False)


def on_device(
    values,
    lengths,
    w_in1,
    b_in1,
    w_in2,
    b_in2,
    w_res,
    g_attn,
    w_qkv,
    w_out,
    g_mlp,
    w_up,
    w_down,
    cotangent,
):
    f32 = jnp.float32
    bf16 = jnp.bfloat16
    gathered = (
        lax.all_gather(w_in1, "fsdp", axis=1, tiled=True),
        lax.all_gather(b_in1, "fsdp", axis=0, tiled=True),
        lax.all_gather(w_in2, "fsdp", axis=0, tiled=True),
        lax.all_gather(b_in2, "fsdp", axis=0, tiled=True),
        lax.all_gather(w_res, "fsdp", axis=1, tiled=True),
        lax.all_gather(g_attn, "fsdp", axis=0, tiled=True),
        lax.all_gather(w_qkv, "fsdp", axis=0, tiled=True),
        lax.all_gather(w_out, "fsdp", axis=1, tiled=True),
        lax.all_gather(g_mlp, "fsdp", axis=0, tiled=True),
        lax.all_gather(w_up, "fsdp", axis=0, tiled=True),
        lax.all_gather(w_down, "fsdp", axis=1, tiled=True),
    )
    (
        full_in1,
        full_b1,
        full_in2,
        full_b2,
        full_res,
        full_gattn,
        full_qkv,
        full_out,
        full_gmlp,
        full_up,
        full_down,
    ) = gathered
    series = lengths.shape[0]
    seq_len = values.shape[0] // series
    patch_len = values.shape[1]
    slot_ids = jnp.arange(seq_len, dtype=jnp.int32)
    pad_count = seq_len - lengths
    padded = slot_ids[None, :] < pad_count[:, None]
    places = (slot_ids[None, :] - pad_count[:, None]).astype(f32)
    keep_mask = (1.0 - padded.astype(f32)).reshape(-1, 1)
    inputs = jnp.concatenate(
        [values.astype(f32) * keep_mask, jnp.broadcast_to(1.0 - keep_mask, values.shape)], 1
    ).astype(bf16)
    pre_act = jnp.dot(inputs, full_in1, preferred_element_type=f32) + full_b1.astype(f32)
    hidden = jax.nn.silu(pre_act).astype(bf16)
    resid0 = (
        jnp.dot(hidden, full_in2, preferred_element_type=f32)
        + full_b2.astype(f32)
        + jnp.dot(inputs, full_res, preferred_element_type=f32)
    )
    gain_attn = full_gattn.astype(f32)
    normed = rms_norm(resid0, gain_attn).astype(bf16)
    projected = jnp.einsum("td,dch->tch", normed, full_qkv, preferred_element_type=f32)
    local_heads = projected.shape[2] // HD
    head_shape = (series, seq_len, local_heads, HD)
    queries = rotate(projected[:, 0].reshape(head_shape), places).astype(bf16)
    key_rows = rotate(projected[:, 1].reshape(head_shape), places).astype(bf16)
    value_heads = projected[:, 2].reshape(head_shape).astype(bf16)
    causal = slot_ids[None, :] <= slot_ids[:, None]
    diagonal = slot_ids[None, :] == slot_ids[:, None]
    allowed = (causal[None] & (jnp.logical_not(padded)[:, None, :] | diagonal[None]))[:, None]
    scale = HD ** (-0.5)

    def score_block():
        raw = jnp.einsum("sqhe,skhe->shqk", queries, key_rows, preferred_element_type=f32) * scale
        return jnp.where(allowed, raw, -1e30)

    scores = score_block()
    row_max = jnp.max(scores, -1, keepdims=True)
    exponent = jnp.exp(scores - row_max)
    row_total = jnp.sum(exponent, -1, keepdims=True)
    log_total = row_max + jnp.log(row_total)
    attn_probs = (exponent / row_total).astype(bf16)
    attended = (
        jnp.einsum("shqk,skhe->sqhe", attn_probs, value_heads, preferred_element_type=f32)
        .reshape(-1, local_heads * HD)
        .astype(bf16)
    )
    branch_one = lax.psum(jnp.dot(attended, full_out, preferred_element_type=f32), "mp")
    resid1 = resid0 + branch_one
    gain_mlp = full_gmlp.astype(f32)
    normed2 = rms_norm(resid1, gain_mlp).astype(bf16)
    up_rows = jnp.dot(normed2, full_up, preferred_element_type=f32)
    mlp_hidden = activate(up_rows).astype(bf16)
    branch_two = lax.psum(
        jnp.dot(mlp_hidden, full_down, preferred_element_type=f32).astype(jnp.bfloat16), "mp"
    ).astype(jnp.float32)
    result = (resid1 + branch_two).astype(bf16)
    again = (
        lax.all_gather(w_in1, "fsdp", axis=1, tiled=True),
        lax.all_gather(b_in1, "fsdp", axis=0, tiled=True),
        lax.all_gather(w_in2, "fsdp", axis=0, tiled=True),
        lax.all_gather(b_in2, "fsdp", axis=0, tiled=True),
        lax.all_gather(w_res, "fsdp", axis=1, tiled=True),
        lax.all_gather(g_attn, "fsdp", axis=0, tiled=True),
        lax.all_gather(w_qkv, "fsdp", axis=0, tiled=True),
        lax.all_gather(w_out, "fsdp", axis=1, tiled=True),
        lax.all_gather(g_mlp, "fsdp", axis=0, tiled=True),
        lax.all_gather(w_up, "fsdp", axis=0, tiled=True),
        lax.all_gather(w_down, "fsdp", axis=1, tiled=True),
    )
    (
        back_in1,
        back_b1,
        back_in2,
        back_b2,
        back_res,
        back_gattn,
        back_qkv,
        back_out,
        back_gmlp,
        back_up,
        back_down,
    ) = again
    cot_rows = cotangent.astype(f32)
    grad_down = jnp.einsum("tf,td->fd", mlp_hidden, cotangent, preferred_element_type=f32)
    grad_hidden = jnp.einsum("td,fd->tf", cotangent, back_down, preferred_element_type=f32)
    unused_one, pull_mlp = jax.vjp(activate, up_rows)
    grad_up_rows = pull_mlp(grad_hidden)[0].astype(bf16)
    grad_up = jnp.einsum("td,tf->df", normed2, grad_up_rows, preferred_element_type=f32)
    norm_part2 = jnp.einsum("tf,df->td", grad_up_rows, back_up, preferred_element_type=f32)
    norm_grad2 = lax.psum(norm_part2, "mp")
    unused_two, pull_norm2 = jax.vjp(rms_norm, resid1, back_gmlp.astype(f32))
    resid_part1, grad_gmlp = pull_norm2(norm_grad2)
    resid1_grad = cot_rows + resid_part1
    out_grad = resid1_grad.astype(bf16)
    grad_out = jnp.einsum("th,td->hd", attended, out_grad, preferred_element_type=f32)
    attended_grad = (
        jnp.einsum("td,hd->th", out_grad, back_out, preferred_element_type=f32)
        .astype(bf16)
        .reshape(head_shape)
    )
    scores = score_block()
    probs_full = jnp.exp(scores - log_total)
    value_grad = jnp.einsum(
        "shqk,sqhe->skhe", probs_full.astype(bf16), attended_grad, preferred_element_type=f32
    )
    prob_grad = jnp.einsum(
        "sqhe,skhe->shqk", attended_grad, value_heads, preferred_element_type=f32
    )
    score_grad = (
        probs_full * (prob_grad - jnp.sum(prob_grad * probs_full, -1, keepdims=True))
    ).astype(bf16)
    query_grad = (
        jnp.einsum("shqk,skhe->sqhe", score_grad, key_rows, preferred_element_type=f32) * scale
    )
    key_grad = (
        jnp.einsum("shqk,sqhe->skhe", score_grad, queries, preferred_element_type=f32) * scale
    )
    width_local = local_heads * HD
    qkv_rows = jnp.stack(
        [
            rotate(query_grad, -places).reshape(-1, width_local),
            rotate(key_grad, -places).reshape(-1, width_local),
            value_grad.reshape(-1, width_local),
        ],
        1,
    ).astype(bf16)
    grad_qkv = jnp.einsum("td,tch->dch", normed, qkv_rows, preferred_element_type=f32)
    norm_part1 = jnp.einsum("tch,dch->td", qkv_rows, back_qkv, preferred_element_type=f32)
    norm_grad1 = lax.psum(norm_part1, "mp")
    unused_three, pull_norm1 = jax.vjp(rms_norm, resid0, back_gattn.astype(f32))
    resid_part0, grad_gattn = pull_norm1(norm_grad1)
    resid0_grad = (resid1_grad + resid_part0).astype(bf16)
    grad_in2 = jnp.einsum("th,td->hd", hidden, resid0_grad, preferred_element_type=f32)
    grad_b2 = jnp.sum(resid0_grad.astype(f32), 0)
    grad_res = jnp.einsum("tp,td->pd", inputs, resid0_grad, preferred_element_type=f32)
    hidden_grad = jnp.einsum("td,hd->th", resid0_grad, back_in2, preferred_element_type=f32)
    unused_four, pull_silu = jax.vjp(jax.nn.silu, pre_act)
    pre_grad = pull_silu(hidden_grad)[0].astype(bf16)
    grad_in1 = jnp.einsum("tp,th->ph", inputs, pre_grad, preferred_element_type=f32)
    grad_b1 = jnp.sum(pre_grad.astype(f32), 0)
    input_grad = jnp.einsum(
        "th,ph->tp", pre_grad, back_in1, preferred_element_type=f32
    ) + jnp.einsum("td,pd->tp", resid0_grad, back_res, preferred_element_type=f32)
    values_grad = input_grad[:, :patch_len] * keep_mask
    shares = tuple(
        (
            lax.psum_scatter(grad_in1, "fsdp", scatter_dimension=1, tiled=True),
            lax.psum_scatter(grad_b1, "fsdp", scatter_dimension=0, tiled=True),
            lax.psum_scatter(grad_in2, "fsdp", scatter_dimension=0, tiled=True),
            lax.psum_scatter(grad_b2, "fsdp", scatter_dimension=0, tiled=True),
            lax.psum_scatter(grad_res, "fsdp", scatter_dimension=1, tiled=True),
            lax.psum_scatter(grad_gattn, "fsdp", scatter_dimension=0, tiled=True),
            lax.psum_scatter(grad_qkv, "fsdp", scatter_dimension=0, tiled=True),
            lax.psum_scatter(grad_out, "fsdp", scatter_dimension=1, tiled=True),
            lax.psum_scatter(grad_gmlp, "fsdp", scatter_dimension=0, tiled=True),
            lax.psum_scatter(grad_up, "fsdp", scatter_dimension=0, tiled=True),
            lax.psum_scatter(grad_down, "fsdp", scatter_dimension=1, tiled=True),
        )
    )
    return (result, values_grad) + shares


def solution(mesh):
    in_specs = (
        P("fsdp", None),
        P("fsdp"),
        P(None, "fsdp"),
        P("fsdp"),
        P("fsdp", None),
        P("fsdp"),
        P(None, "fsdp"),
        P("fsdp"),
        P("fsdp", None, "mp"),
        P("mp", "fsdp"),
        P("fsdp"),
        P("fsdp", "mp"),
        P("mp", "fsdp"),
        P("fsdp", None),
    )
    out_specs = (
        P("fsdp", None),
        P("fsdp", None),
        P(None, "fsdp"),
        P("fsdp"),
        P("fsdp", None),
        P("fsdp"),
        P(None, "fsdp"),
        P("fsdp"),
        P("fsdp", None, "mp"),
        P("mp", "fsdp"),
        P("fsdp"),
        P("fsdp", "mp"),
        P("mp", "fsdp"),
    )
    return jax.shard_map(
        on_device, mesh=mesh, in_specs=in_specs, out_specs=out_specs, check_vma=False
    )
```

profile of v0, /device:TPU:0, one launch (start us, length us, event | category | flops | bytes accessed | tf_op | source)
XLA Modules:
  0.0 1253.6 jit_solution(667919393535561383)
XLA Ops:
  10.5 1.3 fusion.57
  15.8 79.4 %all-reduce.9 = (bf16[1280]{0:T(1024)(128)(2,1)S(1)}, bf16[1280]{0:T(1024)(128)(2,1)S(1)}, bf16[1280]{0:T(1024)(128)(2,1)S(1)}, bf16[1280]{0:T(1024)(128)(2,1)}) all-reduce(bf16[1280]{0:T(1024)(128)(2,1)S(1)} %dynamic-update-slice.1, bf16[1280]{0:T(1024)(128)(2,1)S(1)} %dynamic-update-slice, ...), channel_id=1, replica_groups=mesh['fsdp'=16,'mp'=2] {'fsdp'}, use_global_device_ids=true, to_apply=%add.1 | all-reduce | flops 5120 | bytes 20480
  96.0 38.8 %all-gather = bf16[16,80,64]{1,2,0:T(8,128)(2,1)S(1)} all-gather(bf16[1,80,64]{1,2,0:T(8,128)(2,1)} %bitcast.81), channel_id=1, replica_groups=mesh['fsdp'=16,'mp'=2] {'fsdp'}, dimensions={0}, use_global_device_ids=true | all-gather | bytes 174080 | tf_op jit(solution)/shard_map/all_gather | solution.py:57
  135.2 40.2 %all-gather.1 = bf16[16,80,64]{1,2,0:T(8,128)(2,1)S(1)} all-gather(bf16[1,80,64]{1,2,0:T(8,128)(2,1)S(1)} %bitcast.82), channel_id=1, replica_groups=mesh['fsdp'=16,'mp'=2] {'fsdp'}, dimensions={0}, use_global_device_ids=true | all-gather | bytes 174080 | tf_op jit(solution)/shard_map/all_gather | solution.py:61
  176.6 1.7 multiply_cosine_fusion
  178.7 1.0 copy-done.5
  179.7 3.1 convolution_add_fusion.2
  183.9 4.0 fusion.35
  187.9 1.3 copy-done.33
  189.3 1.4 convert_element_type.117
  190.7 2.2 fusion.54
  193.4 1.6 reshape_squeeze.8
  199.7 32.0 %all-gather.12.cloned.1.call-done = bf16[640,1280]{0,1:T(8,128)(2,1)} async-done(((bf16[640,80]{0,1:T(8,128)(2,1)}), bf16[640,1280]{0,1:T(8,128)(2,1)}) %all-gather.12.cloned.1.call-update) | async-done | bytes 1638416 | tf_op jit(solution)/shard_map/all_gather | solution.py:64
  231.6 3.2 fusion.59
  236.3 17.6 %all-reduce.15.cloned.1.call-done = f32[256,1280]{1,0:T(8,128)} async-done(((f32[256,1280]{1,0:T(8,128)}), f32[256,1280]{1,0:T(8,128)}) %all-reduce.15.cloned.1.call-update) | async-done | bytes 1310736 | tf_op jit(solution)/shard_map/psum | solution.py:128
  253.9 1.5 multiply_reduce_fusion.4
  255.4 60.7 %all-gather.14.cloned.1.call-done = bf16[1280,640]{1,0:T(8,128)(2,1)} async-done(((bf16[80,640]{1,0:T(8,128)(2,1)}), bf16[1280,640]{1,0:T(8,128)(2,1)}) %all-gather.14.cloned.1.call-update) | async-done | bytes 1638416 | tf_op jit(solution)/shard_map/all_gather | solution.py:66
  316.1 3.0 fusion.49
  319.1 56.9 %all-gather.16.cloned.1.call-done = bf16[640,1280]{0,1:T(8,128)(2,1)} async-done(((bf16[640,80]{0,1:T(8,128)(2,1)}), bf16[640,1280]{0,1:T(8,128)(2,1)}) %all-gather.16.cloned.1.call-update) | async-done | bytes 1638416 | tf_op jit(solution)/shard_map/all_gather | solution.py:67
  376.0 4.7 add_convert_fusion.5
  381.4 1.8 fusion.60
  383.3 1.5 multiply_convert_fusion.4
  385.5 1.5 convolution_convert_fusion
  387.1 15.1 %all-reduce.19.cloned.1.call-done = f32[256,1280]{1,0:T(8,128)} async-done(((f32[256,1280]{1,0:T(8,128)}), f32[256,1280]{1,0:T(8,128)}) %all-reduce.19.cloned.1.call-update) | async-done | bytes 1310736 | tf_op jit(solution)/shard_map/psum | solution.py:171
  402.2 1.6 multiply_reduce_fusion
  403.8 21.4 %all-reduce.17.cloned.1.call-done = bf16[256,1280]{1,0:T(8,128)(2,1)} async-done(((bf16[256,1280]{1,0:T(8,128)(2,1)}), bf16[256,1280]{1,0:T(8,128)(2,1)}) %all-reduce.17.cloned.1.call-update) | async-done | bytes 655376 | tf_op jit(solution)/shard_map/psum | solution.py:134
  425.3 3.1 fusion.3
  428.3 1.1 copy-done.2
  430.2 1.4 reshape.220
  431.6 1.8 fusion.10
  435.2 1.4 fusion
  436.7 1.6 fusion.1
  438.9 3.9 subtract_convert_fusion
  443.2 1.2 copy.68
  444.4 2.2 stack_reshape.13
  446.6 1.3 pad_maximum_fusion.2
  448.3 1.1 stack_reshape.12
  449.4 1.0 constant_dynamic-update-slice_fusion.2
  450.4 1.0 constant_dynamic-update-slice_fusion.1
  451.5 1.0 copy-done.21
  452.4 5.0 convolution_bitcast_fusion
  457.5 21.3 %all-reduce.21.cloned.1.call-done = f32[256,1280]{1,0:T(8,128)} async-done(((f32[256,1280]{1,0:T(8,128)}), f32[256,1280]{1,0:T(8,128)}) %all-reduce.21.cloned.1.call-update) | async-done | bytes 1310736 | tf_op jit(solution)/shard_map/psum | solution.py:210
  478.8 1.8 multiply_reduce_fusion.1
  482.2 1.0 copy-done.49
  483.2 1.2 convert_reduce_fusion.1
  485.3 1.2 convolution_bitcast_fusion.2
  486.6 1.2 convolution_bitcast_fusion.1
  487.9 3.4 fusion.48
  492.5 2.4 fusion.63
  495.1 1.2 copy-done.4
  496.3 3.4 fusion.29
  499.8 1.2 copy-done.7
  501.1 4.0 fusion.50
  505.1 1.1 copy-done.22
  506.3 5.4 fusion.33
  512.5 77.0 %all-reduce.8 = (f32[1280]{0:T(1024)S(1)}, f32[1280]{0:T(1024)S(1)}, f32[1280]{0:T(1024)S(1)}, f32[1280]{0:T(1024)S(1)}) all-reduce(f32[1280]{0:T(1024)S(1)} %get-tuple-element.27, f32[1280]{0:T(1024)S(1)} %get-tuple-element.25, f32[1280]{0:T(1024)S(1)} %get-tuple-element.15, ...), channel_id=3, replica_groups=mesh['fsdp'=16,'mp'=2] {'fsdp'}, use_global_device_ids=true, to_apply=%region_13.14.clone | all-reduce | flops 5120 | bytes 40960
  593.2 1.5 copy.77
  594.7 45.9 %reduce-scatter.24.cloned.1.call-done = f32[80,64]{1,0:T(8,128)} async-done(((f32[1280,64]{1,0:T(8,128)}), f32[80,64]{1,0:T(8,128)}) %reduce-scatter.24.cloned.1.call-update) | async-done | bytes 20496
  640.5 1.5 copy.79
  642.0 82.6 %reduce-scatter.18.cloned.1.call-done = f32[80,640]{1,0:T(8,128)} async-done(((f32[1280,640]{1,0:T(8,128)}), f32[80,640]{1,0:T(8,128)}) %reduce-scatter.18.cloned.1.call-update) | async-done | bytes 204816 | tf_op jit(solution)/shard_map/reduce_scatter | solution.py:237
  724.6 85.0 %reduce-scatter.20.cloned.1.call-done = f32[640,80]{0,1:T(8,128)} async-done(((f32[640,1280]{0,1:T(8,128)}), f32[640,80]{0,1:T(8,128)}) %reduce-scatter.20.cloned.1.call-update) | async-done | bytes 204816 | tf_op jit(solution)/shard_map/reduce_scatter | solution.py:238
  809.6 84.7 %reduce-scatter.16.cloned.1.call-done = f32[640,80]{0,1:T(8,128)} async-done(((f32[640,1280]{0,1:T(8,128)}), f32[640,80]{0,1:T(8,128)}) %reduce-scatter.16.cloned.1.call-update) | async-done | bytes 204816 | tf_op jit(solution)/shard_map/reduce_scatter | solution.py:235
  894.3 141.3 %reduce-scatter.12.cloned.1.call-done = f32[80,1280]{1,0:T(8,128)} async-done(((f32[1280,1280]{1,0:T(8,128)}), f32[80,1280]{1,0:T(8,128)}) %reduce-scatter.12.cloned.1.call-update) | async-done | bytes 409616 | tf_op jit(solution)/shard_map/reduce_scatter | solution.py:230
  1035.6 211.4 %reduce-scatter.14.cloned.1.call-done = f32[80,3,640]{2,0,1:T(8,128)} async-done(((f32[1280,3,640]{2,0,1:T(8,128)}), f32[80,3,640]{2,0,1:T(8,128)}) %reduce-scatter.14.cloned.1.call-update) | async-done | bytes 614416 | tf_op jit(solution)/shard_map/reduce_scatter | solution.py:234
  (186 shorter events, 30.0 us)
Async XLA Ops:
  7.2 128.0 %copy-start.41 = (bf16[64,80]{1,0:T(8,128)(2,1)S(1)}, bf16[64,80]{1,0:T(8,128)(2,1)}, u32[]{:S(2)}) copy-start(bf16[64,80]{1,0:T(8,128)(2,1)} %param.20) | copy-start | bytes 30724
  7.2 171.5 %all-gather.8.cloned.1.call-start = ((), (), s32[]{:S(2)}) async-start(), calls=%async_computation.7 | async-start | bytes 3481600 | tf_op jit(solution)/shard_map/all_gather | solution.py:59
  7.9 175.4 %all-gather.10.cloned.1.call-start = ((), (), s32[]{:S(2)}) async-start(), calls=%async_computation.8 | async-start | bytes 5222400 | tf_op jit(solution)/shard_map/all_gather | solution.py:63
  8.7 223.0 %all-gather.12.cloned.1.call-start = ((), (), s32[]{:S(2)}) async-start(), calls=%async_computation.9 | async-start | bytes 1740800 | tf_op jit(solution)/shard_map/all_gather | solution.py:64
  9.4 244.5 %all-reduce.15.cloned.1.call-start = ((), (), s32[]{:S(2)}) async-start(), calls=%async_computation.10 | async-start | bytes 2621440 | tf_op jit(solution)/shard_map/psum | solution.py:128
  10.5 164.9 %copy-start.46 = (f32[256]{0:T(256)}, f32[256]{0:T(256)S(1)}, u32[]{:S(2)}) copy-start(f32[256]{0:T(256)S(1)} %sub.90) | copy-start | bytes 3076
  95.2 88.1 %copy-start.38 = (f32[1280]{0:T(1024)}, f32[1280]{0:T(1024)S(1)}, u32[]{:S(2)}) copy-start(f32[1280]{0:T(1024)S(1)} %convert_element_type.115) | copy-start | bytes 15364
  135.2 43.5 %copy-start.31 = (bf16[1280,64]{0,1:T(8,128)(2,1)}, bf16[1280,64]{0,1:T(8,128)(2,1)S(1)}, u32[]{:S(2)}) copy-start(bf16[1280,64]{0,1:T(8,128)(2,1)S(1)} %reshape.234) | copy-start | bytes 491524
  175.8 7.0 copy-start.29
  178.3 4.6 copy-start.36
  178.7 1.1 copy-start.5
  187.9 1.3 copy-start.33
  194.9 0.9 copy-start.35
  195.8 0.9 copy-start.40
  196.8 0.8 copy-start.11
  196.8 1.0 copy-start.13
  196.8 1.1 copy-start.15
  196.8 1.4 copy-start.26
  197.9 1.0 copy-start
  199.7 35.2 %copy-start.18 = (bf16[256,640]{1,0:T(8,128)(2,1)}, bf16[256,640]{1,0:T(8,128)(2,1)S(1)}, u32[]{:S(2)}) copy-start(bf16[256,640]{1,0:T(8,128)(2,1)S(1)} %convert_element_type.122) | copy-start | bytes 983044
  234.8 1.4 copy-start.48
  234.9 81.2 %all-gather.14.cloned.1.call-start = ((), (), s32[]{:S(2)}) async-start(), calls=%async_computation.11 | async-start | bytes 1740800 | tf_op jit(solution)/shard_map/all_gather | solution.py:66
  235.5 140.5 %all-gather.16.cloned.1.call-start = ((), (), s32[]{:S(2)}) async-start(), calls=%async_computation.12 | async-start | bytes 1740800 | tf_op jit(solution)/shard_map/all_gather | solution.py:67
  236.0 166.2 %all-reduce.19.cloned.1.call-start = ((), (), s32[]{:S(2)}) async-start(), calls=%async_computation.14 | async-start | bytes 2621440 | tf_op jit(solution)/shard_map/psum | solution.py:171
  376.0 5.4 copy-start.9
  380.7 0.7 copy-start.34
  383.2 42.1 %all-reduce.17.cloned.1.call-start = ((), (), s32[]{:S(2)}) async-start(), calls=%async_computation.13 | async-start | bytes 1310720 | tf_op jit(solution)/shard_map/psum | solution.py:134
  383.3 2.2 copy-start.28
  384.7 0.7 copy-start.19
  387.0 91.7 %all-reduce.21.cloned.1.call-start = ((), (), s32[]{:S(2)}) async-start(), calls=%async_computation.15 | async-start | bytes 2621440 | tf_op jit(solution)/shard_map/psum | solution.py:210
  425.3 4.2 copy-start.8
  428.3 1.1 copy-start.2
  431.6 1.8 copy-start.1
  431.6 1.8 copy-start.17
  431.6 2.0 copy-start.27
  434.0 1.0 copy-start.14
  434.0 1.2 copy-start.16
  435.2 1.5 copy-start.12
  451.4 1.0 copy-start.21
  457.4 21.4 %copy-start.39 = (f32[1280]{0:T(1024)S(1)}, f32[1280]{0:T(1024)}, u32[]{:S(2)}) copy-start(f32[1280]{0:T(1024)} %copy-done.38) | copy-start | bytes 15364
  457.4 21.4 %copy-start.43 = (f32[256]{0:T(256)S(1)}, f32[256]{0:T(256)}, u32[]{:S(2)}) copy-start(f32[256]{0:T(256)} %copy-done.42) | copy-start | bytes 3076
  457.4 23.1 %copy-start.45 = (f32[256]{0:T(256)S(1)}, f32[256]{0:T(256)}, u32[]{:S(2)}) copy-start(f32[256]{0:T(256)} %copy-done.44) | copy-start | bytes 3076
  457.4 135.7 %reduce-scatter.22.cloned.1.call-start = ((), (), s32[]{:S(2)}) async-start(), calls=%async_computation.21 | async-start | bytes 696320
  478.8 1.8 copy-start.3
  478.8 2.1 copy-start.10
  480.9 1.3 copy-start.6
  480.9 2.3 copy-start.49
  483.2 2.1 copy-start.37
  484.4 0.9 copy-start.23
  486.6 154.0 %reduce-scatter.24.cloned.1.call-start = ((), (), s32[]{:S(2)}) async-start(), calls=%async_computation.22 | async-start | bytes 696320
  487.9 236.7 %reduce-scatter.18.cloned.1.call-start = ((), (), s32[]{:S(2)}) async-start(), calls=%async_computation.19 | async-start | bytes 3481600 | tf_op jit(solution)/shard_map/reduce_scatter | solution.py:237
  491.4 1.0 copy-start.20
  491.4 1.2 copy-start.25
  491.4 318.2 %reduce-scatter.20.cloned.1.call-start = ((), (), s32[]{:S(2)}) async-start(), calls=%async_computation.20 | async-start | bytes 3481600 | tf_op jit(solution)/shard_map/reduce_scatter | solution.py:238
  495.0 1.3 copy-start.4
  495.0 399.3 %reduce-scatter.16.cloned.1.call-start = ((), (), s32[]{:S(2)}) async-start(), calls=%async_computation.18 | async-start | bytes 3481600 | tf_op jit(solution)/shard_map/reduce_scatter | solution.py:235
  499.7 1.3 copy-start.7
  499.8 535.9 %reduce-scatter.12.cloned.1.call-start = ((), (), s32[]{:S(2)}) async-start(), calls=%async_computation.16 | async-start | bytes 6963200 | tf_op jit(solution)/shard_map/reduce_scatter | solution.py:230
  505.1 1.2 copy-start.22
  505.1 742.0 %reduce-scatter.14.cloned.1.call-start = ((), (), s32[]{:S(2)}) async-start(), calls=%async_computation.17 | async-start | bytes 10444800 | tf_op jit(solution)/shard_map/reduce_scatter | solution.py:234
  511.7 80.2 %copy-start.30 = (bf16[1280,64]{0,1:T(8,128)(2,1)S(1)}, bf16[1280,64]{0,1:T(8,128)(2,1)}, u32[]{:S(2)}) copy-start(bf16[1280,64]{0,1:T(8,128)(2,1)} %copy-done.29) | copy-start | bytes 491524
  511.7 80.5 %copy-start.24 = (bf16[256,1280]{1,0:T(8,128)(2,1)S(1)}, bf16[256,1280]{1,0:T(8,128)(2,1)}, u32[]{:S(2)}) copy-start(bf16[256,1280]{1,0:T(8,128)(2,1)} %copy-done.23) | copy-start | bytes 1966084
  511.7 80.5 %copy-start.32 = (bf16[1280,64]{0,1:T(8,128)(2,1)S(1)}, bf16[1280,64]{0,1:T(8,128)(2,1)}, u32[]{:S(2)}) copy-start(bf16[1280,64]{0,1:T(8,128)(2,1)} %copy-done.31) | copy-start | bytes 491524
  511.7 80.8 %copy-start.47 = (f32[256]{0:T(256)S(1)}, f32[256]{0:T(256)}, u32[]{:S(2)}) copy-start(f32[256]{0:T(256)} %copy-done.46) | copy-start | bytes 3076
  (2 other events, 1.2 us)
Sparse Core Ops, SparseCore 0:
  10.8 72.8 all-gather.7
  86.4 85.4 all-gather.9
  174.6 57.0 all-gather.11
  235.0 18.8 all-reduce.14
  256.8 59.2 all-gather.13
  319.0 56.9 all-gather.15
  383.3 18.8 all-reduce.18
  405.1 20.1 all-reduce.16
  457.6 21.1 all-reduce.20
  486.7 78.1 reduce-scatter.21
  567.2 73.2 reduce-scatter.23
  643.3 81.2 reduce-scatter.17
  727.5 82.0 reduce-scatter.19
  812.3 81.9 reduce-scatter.15
  897.0 138.5 reduce-scatter.11
  1038.5 208.5 reduce-scatter.13
where the time goes:
time: 1260 us; the launch traced here: 1250 us
  waiting for transfers between devices  879 us (70%)
  blocking collectives  235 us (19%)
  matrix products  57.3 us (5%)
  local copies, waits for them, and re-layouts  43.2 us (3%)
  other arithmetic  21.6 us (2%)
  between operations  15.9 us (1%)
    reduce_scatter x1, waiting for transfers between devices, on_device(): lax.psum_scatter(grad_qkv, 'fsdp', scatter_dimension=0, tiled=True)  211 us
    unnamed x2, blocking collectives  156 us
    reduce_scatter x1, waiting for transfers between devices, on_device(): lax.psum_scatter(grad_in2, 'fsdp', scatter_dimension=0, tiled=True)  141 us
    reduce_scatter x1, waiting for transfers between devices, on_device(): lax.psum_scatter(grad_down, 'fsdp', scatter_dimension=1, tiled=True)  85 us
    reduce_scatter x1, waiting for transfers between devices, on_device(): lax.psum_scatter(grad_out, 'fsdp', scatter_dimension=1, tiled=True)  84.7 us
    reduce_scatter x1, waiting for transfers between devices, on_device(): lax.psum_scatter(grad_up, 'fsdp', scatter_dimension=0, tiled=True)  82.6 us
    all_gather x1, waiting for transfers between devices, on_device(): lax.all_gather(w_up, 'fsdp', axis=0, tiled=True)  60.7 us
    all_gather x1, waiting for transfers between devices, on_device(): lax.all_gather(w_down, 'fsdp', axis=1, tiled=True)  56.9 us
  transfers between devices with their start and end apart: 16, of which 13 were waited for; matrix products, arithmetic and copies ran while one was open for 5% of the time, Pallas kernels for 0%

commit v1 on v0

--- a/solution.py
+++ b/solution.py
@@ -1,9 +1,749 @@
+import functools
+import math
+
 import jax
 import jax.numpy as jnp
 from jax import lax
+from jax.experimental import pallas as pl
+from jax.experimental.pallas import tpu as pltpu
 from jax.sharding import PartitionSpec as P
 
 HD = 80
+MESH = pl.DeviceIdType.MESH
+f32 = jnp.float32
+bf16 = jnp.bfloat16
+
+IN2, WQ, WK, WV, WOUT, WUP, WDOWN, PACK = range(8)
+NW = 7
+PL = 128
+SLOT_A, SLOT_X, SLOT_Y, SLOT_V, SLOT_V2, SLOTS = 0, 4, 8, 12, 16, 17
+VMEM_BYTES = 63 * 2**20
+
+
+def dot(left, right, left_dim, right_dim):
+    return lax.dot_general(
+        left, right, (((left_dim,), (right_dim,)), ((), ())), preferred_element_type=f32
+    )
+
+
+def fused_kernel(
+    lengths,
+    values,
+    pack,
+    in2,
+    qkv,
+    out_t,
+    up,
+    down_t,
+    cot_hbm,
+    o_out,
+    o_dval,
+    o_pack,
+    o_in2,
+    o_qkv,
+    o_wout,
+    o_up,
+    o_down,
+    W,
+    PK,
+    G,
+    GP,
+    R,
+    RP,
+    R0,
+    R1,
+    S,
+    X,
+    SB,
+    XB,
+    hid,
+    nrm,
+    nrm2,
+    q,
+    k,
+    v,
+    prob,
+    att,
+    gprime,
+    mlp,
+    cot,
+    dup,
+    dq,
+    dk,
+    dv,
+    tmp,
+    dr0,
+    rope_c,
+    rope_s,
+    bias,
+    inx,
+    gains,
+    dgs,
+    accg,
+    keep_col,
+    acc,
+    accp,
+    fin_in2,
+    fin_pack,
+    ag_send,
+    ag_recv,
+    rs_send,
+    rs_recv,
+    ex_send,
+    ex_recv,
+    lsem,
+):
+    rows, width = cot.shape
+    half = W.shape[2]
+    blk = in2.shape[0]
+    series = lengths.shape[0]
+    seq = rows // series
+    heads = half // HD
+    patch = values.shape[1]
+
+    f = lax.axis_index("fsdp")
+    m = lax.axis_index("mp")
+    x = lax.rem(f, 2)
+    y = lax.rem(lax.div(f, 2), 2)
+    z = lax.div(f, 4)
+    xn = f + 1 - 2 * x
+    yn = f + 2 - 4 * y
+    dn_ = f + 3 - 2 * x - 4 * y
+    XN, YN, UP, DN, SIB = (xn, m), (yn, m), (f + 4, m), (f - 4, m), (f, 1 - m)
+    cx, cy, cd, c0 = xn - 4 * z, yn - 4 * z, dn_ - 4 * z, f - 4 * z
+    z_inner = jnp.logical_and(z > 0, z < 3).astype(jnp.int32)
+    z_high = (z >= 2).astype(jnp.int32)
+
+    def near(i):
+        swap = (i == 0).astype(jnp.int32) - (i == 1).astype(jnp.int32)
+        low = i + z_inner * swap
+        return low + z_high * (3 - 2 * low)
+
+    def far(i):
+        return near(3 - i)
+
+    def each_plane(order, body):
+        def step(i, carry):
+            body(order(i))
+            return carry
+
+        lax.fori_loop(0, 4, step, 0)
+
+    def row_of(b):
+        return pl.ds(pl.multiple_of(b * blk, 16), blk)
+
+    def w_block(w, b):
+        return PK.at[m, row_of(b)] if w == PACK else W.at[w, row_of(b)]
+
+    def g_block(w, b):
+        return GP.at[row_of(b)] if w == PACK else G.at[w, row_of(b)]
+
+    def r_block(w, s):
+        return RP.at[s] if w == PACK else R.at[w, s]
+
+    def remote(src, dst, send, recv, dev):
+        return pltpu.make_async_remote_copy(
+            src_ref=src, dst_ref=dst, send_sem=send, recv_sem=recv, device_id=dev, device_id_type=MESH
+        )
+
+    def ag_push(w, b, dev):
+        ref = w_block(w, b)
+        remote(ref, ref, ag_send.at[w], ag_recv.at[w, b], dev).start()
+
+    def ag_await(w, b):
+        ref = w_block(w, b)
+        remote(ref, ref, ag_send.at[w], ag_recv.at[w, b], XN).wait_recv()
+
+    mcols = pl.ds(pl.multiple_of(m * half, 128), half)
+
+    def own_copy(w):
+        if w == PACK:
+            src = pack.at[m]
+        elif w == IN2:
+            src = in2.at[:, mcols]
+        elif w in (WQ, WK, WV):
+            src = qkv.at[w - WQ]
+        else:
+            src = {WOUT: out_t, WUP: up, WDOWN: down_t}[w]
+        return pltpu.make_async_copy(src, w_block(w, f), lsem.at[w])
+
+    def ag_own(w):
+        own_copy(w).wait()
+
+        @pl.when(z < 3)
+        def _():
+            ag_push(w, f, UP)
+
+        @pl.when(z > 0)
+        def _():
+            ag_push(w, f, DN)
+
+        ag_push(w, f, XN)
+        ag_push(w, f, YN)
+
+    def ag_chain(w):
+        for d in (1, 2, 3):
+
+            @pl.when(z >= d)
+            def _():
+                b = f - 4 * d
+                ag_await(w, b)
+
+                @pl.when(z < 3)
+                def _():
+                    ag_push(w, b, UP)
+
+                ag_push(w, b, XN)
+                ag_push(w, b, YN)
+
+            @pl.when(z + d <= 3)
+            def _():
+                b = f + 4 * d
+                ag_await(w, b)
+
+                @pl.when(z > 0)
+                def _():
+                    ag_push(w, b, DN)
+
+                ag_push(w, b, XN)
+                ag_push(w, b, YN)
+
+    def ag_plane(w):
+        def body(zb):
+            even = lax.rem(zb, 2) == 0
+            ag_await(w, 4 * zb + cx)
+
+            @pl.when(even)
+            def _():
+                ag_push(w, 4 * zb + cx, YN)
+
+            ag_await(w, 4 * zb + cy)
+
+            @pl.when(jnp.logical_not(even))
+            def _():
+                ag_push(w, 4 * zb + cy, XN)
+
+        each_plane(near, body)
+
+    def ag_last(w):
+        each_plane(near, lambda zb: ag_await(w, 4 * zb + cd))
+
+    def rs_push(w, src, slot, dev):
+        remote(src, r_block(w, slot), rs_send.at[w], rs_recv.at[w, slot], dev).start()
+
+    def rs_await(w, slot):
+        ref = r_block(w, slot)
+        remote(ref, ref, rs_send.at[w], rs_recv.at[w, slot], XN).wait_recv()
+
+    def rs_start(w):
+        def body(zb):
+            even = lax.rem(zb, 2) == 0
+
+            @pl.when(even)
+            def _():
+                rs_push(w, g_block(w, 4 * zb + cd), SLOT_A + zb, YN)
+                rs_push(w, g_block(w, 4 * zb + cy), SLOT_Y + zb, YN)
+
+            @pl.when(jnp.logical_not(even))
+            def _():
+                rs_push(w, g_block(w, 4 * zb + cd), SLOT_A + zb, XN)
+                rs_push(w, g_block(w, 4 * zb + cx), SLOT_X + zb, XN)
+
+        each_plane(far, body)
+
+    def rs_turn(w):
+        def body(zb):
+            even = lax.rem(zb, 2) == 0
+            rs_await(w, SLOT_A + zb)
+            ref = r_block(w, SLOT_A + zb)
+
+            @pl.when(even)
+            def _():
+                own = g_block(w, 4 * zb + cx)
+                ref[...] = (ref[...].astype(f32) + own[...].astype(f32)).astype(bf16)
+                rs_push(w, ref, SLOT_X + zb, XN)
+
+            @pl.when(jnp.logical_not(even))
+            def _():
+                own = g_block(w, 4 * zb + cy)
+                ref[...] = (ref[...].astype(f32) + own[...].astype(f32)).astype(bf16)
+                rs_push(w, ref, SLOT_Y + zb, YN)
+
+        each_plane(far, body)
+
+    def rs_chain(w, final):
+        total = accp if w == PACK else acc
+
+        def body(zb):
+            rs_await(w, SLOT_X + zb)
+            rs_await(w, SLOT_Y + zb)
+            total[...] = (
+                g_block(w, 4 * zb + c0)[...].astype(f32)
+                + r_block(w, SLOT_X + zb)[...].astype(f32)
+                + r_block(w, SLOT_Y + zb)[...].astype(f32)
+            )
+
+            def take(slot):
+                rs_await(w, slot)
+                total[...] += r_block(w, slot)[...].astype(f32)
+
+            upward = zb > z
+            downward = zb < z
+
+            @pl.when(jnp.logical_or(jnp.logical_and(upward, z > 0), jnp.logical_and(zb <= z, z < 3)))
+            def _():
+                take(SLOT_V + zb)
+
+            ref = r_block(w, SLOT_X + zb)
+
+            @pl.when(upward)
+            def _():
+                ref[...] = total[...].astype(bf16)
+
+                @pl.when(z + 1 == zb)
+                def _():
+                    rs_push(w, ref, SLOT_V2, UP)
+
+                @pl.when(z + 1 != zb)
+                def _():
+                    rs_push(w, ref, SLOT_V + zb, UP)
+
+            @pl.when(downward)
+            def _():
+                ref[...] = total[...].astype(bf16)
+                rs_push(w, ref, SLOT_V + zb, DN)
+
+            @pl.when(jnp.logical_and(zb == z, z > 0))
+            def _():
+                take(SLOT_V2)
+
+        each_plane(far, body)
+        final[...] = total[...]
+
+    def exchange(i, src, dst):
+        return remote(src, dst, ex_send.at[i], ex_recv.at[i], SIB)
+
+    def by_rows(step, body):
+        def one(i, carry):
+            body(pl.ds(pl.multiple_of(i * step, step), step))
+            return carry
+
+        lax.fori_loop(0, rows // step, one, 0)
+
+    halves = (slice(0, half), slice(half, width))
+
+    barrier = pltpu.get_barrier_semaphore()
+    for dev in (XN, YN, SIB):
+        pl.semaphore_signal(barrier, inc=1, device_id=dev, device_id_type=MESH)
+
+    @pl.when(z < 3)
+    def _():
+        pl.semaphore_signal(barrier, inc=1, device_id=UP, device_id_type=MESH)
+
+    @pl.when(z > 0)
+    def _():
+        pl.semaphore_signal(barrier, inc=1, device_id=DN, device_id_type=MESH)
+
+    order = (PACK, IN2, WQ, WK, WV, WOUT, WUP, WDOWN)
+    for w in order:
+        own_copy(w).start()
+    cot_copy = pltpu.make_async_copy(cot_hbm, cot, lsem.at[8])
+    cot_copy.start()
+    pl.semaphore_wait(barrier, 4 + z_inner)
+
+    ag_own(PACK)
+    ag_own(IN2)
+    ag_own(WQ)
+
+    lens = [lengths[s] for s in range(series)]
+
+    def pad_of(slot):
+        total = jnp.zeros(slot.shape, jnp.int32)
+        for s in range(series):
+            inside = jnp.logical_and(slot >= s * seq, slot < (s + 1) * seq)
+            total = jnp.where(inside, (s + 1) * seq - lens[s], total)
+        return total
+
+    def series_of(slot):
+        total = jnp.zeros(slot.shape, jnp.int32)
+        for s in range(1, series):
+            total = total + (slot >= s * seq).astype(jnp.int32)
+        return total
+
+    slot_col = lax.broadcasted_iota(jnp.int32, (rows, 1), 0)
+    keep_col[...] = jnp.broadcast_to((slot_col >= pad_of(slot_col)).astype(f32), keep_col.shape)
+    lane_i = lax.broadcasted_iota(jnp.int32, (rows, PL), 1)
+    keep = keep_col[...]
+    wide = jnp.concatenate([values[...].astype(f32), jnp.zeros((rows, PL - patch), f32)], 1)
+    inx[...] = jnp.where(
+        lane_i < patch,
+        wide * keep,
+        jnp.where(lane_i < 2 * patch, 1.0 - keep, (lane_i == 2 * patch).astype(f32)),
+    ).astype(bf16)
+
+    key_slot = lax.broadcasted_iota(jnp.int32, (1, rows), 1)
+    key_ok = key_slot >= pad_of(key_slot)
+    key_series = series_of(key_slot)
+
+    def bias_rows(s):
+        step = s.size
+        a = lax.broadcasted_iota(jnp.int32, (step, 1), 0) + s.start
+        a_all = jnp.broadcast_to(a, (step, rows))
+        b_all = jnp.broadcast_to(key_slot, (step, rows))
+        same = series_of(a_all) == jnp.broadcast_to(key_series, (step, rows))
+        ok = jnp.logical_or(jnp.broadcast_to(key_ok.astype(jnp.int32), (step, rows)) == 1, a_all == b_all)
+        allowed = jnp.logical_and(jnp.logical_and(same, b_all <= a_all), ok)
+        bias[s, :] = jnp.where(allowed, 0.0, -1e30)
+
+    by_rows(32, bias_rows)
+
+    lane = lax.broadcasted_iota(jnp.int32, (1, half), 1).astype(f32)
+    in_head = lane - HD * jnp.floor((lane + 0.5) / HD)
+    first = in_head < HD // 2
+    turn = jnp.where(first, in_head, in_head - HD // 2)
+    frequency = jnp.exp(turn * (-2.0 * math.log(10000.0) / HD))
+
+    def rope_rows(s):
+        step = s.size
+        slot = lax.broadcasted_iota(jnp.int32, (step, 1), 0) + s.start
+        place = (slot - pad_of(slot)).astype(f32)
+        angle = place * frequency
+        rope_c[s, :] = jnp.cos(angle)
+        sine = jnp.sin(angle)
+        rope_s[s, :] = jnp.where(first, -sine, sine)
+
+    by_rows(16, rope_rows)
+
+    def rope(t, s, inverse):
+        other = jnp.where(first, pltpu.roll(t, half - HD // 2, 1), pltpu.roll(t, HD // 2, 1))
+        turned = other * rope_s[s, :]
+        return t * rope_c[s, :] - turned if inverse else t * rope_c[s, :] + turned
+
+    ag_chain(PACK)
+    ag_own(WK)
+    ag_plane(PACK)
+    ag_last(PACK)
+    pk_copy = exchange(0, PK.at[m], PK.at[m])
+    pk_copy.start()
+    pk_copy.wait()
+    gain_lane = lax.broadcasted_iota(jnp.int32, (16, PL), 1)
+    for i in range(2):
+        pick = (gain_lane == 2 * patch + 1 + i).astype(bf16)
+        gains[i] = dot(pick, PK[1], 1, 1)[0:8]
+
+    def pre_act():
+        for cols in halves:
+            tmp[:, cols] = dot(inx[...], PK[0, cols, :], 1, 1)
+
+    pre_act()
+
+    def silu_rows(s):
+        t = tmp[s, :]
+        hid[s, :] = (t / (1.0 + jnp.exp(-t))).astype(bf16)
+
+    by_rows(16, silu_rows)
+
+    ag_chain(IN2)
+    ag_own(WV)
+    ag_chain(WQ)
+    ag_plane(IN2)
+    ag_last(IN2)
+    R0[m] = dot(hid[...], W[IN2], 1, 0) + dot(inx[...], PK[1, mcols, :], 1, 1)
+    r0_copy = exchange(1, R0.at[m], R0.at[m])
+    r0_copy.start()
+    ag_chain(WK)
+    ag_own(WOUT)
+    r0_copy.wait()
+
+    def norm_rows(load, gain, out):
+        def body(s):
+            a, b = load(s)
+            mean = (jnp.sum(a * a, -1, keepdims=True) + jnp.sum(b * b, -1, keepdims=True)) / width
+            scale = lax.rsqrt(mean + 1e-06)
+            out[s, halves[0]] = (a * scale * gain[0:1, halves[0]]).astype(bf16)
+            out[s, halves[1]] = (b * scale * gain[0:1, halves[1]]).astype(bf16)
+
+        by_rows(16, body)
+
+    norm_rows(lambda s: (R0[0, s, :], R0[1, s, :]), gains.at[0], nrm)
+
+    def project(w, out):
+        tmp[:, halves[0]] = dot(nrm[...], W[w], 1, 0)
+
+        def body(s):
+            out[s, :] = rope(tmp[s, halves[0]], s, False).astype(bf16)
+
+        by_rows(16, body)
+
+    ag_plane(WQ)
+    ag_last(WQ)
+    project(WQ, q)
+    ag_chain(WV)
+    ag_own(WUP)
+    ag_plane(WK)
+    ag_last(WK)
+    project(WK, k)
+    ag_chain(WOUT)
+    ag_own(WDOWN)
+    ag_plane(WV)
+    ag_last(WV)
+    v[...] = dot(nrm[...], W[WV], 1, 0).astype(bf16)
+
+    win = 256
+    scale = HD ** (-0.5)
+    win_lane = lax.broadcasted_iota(jnp.int32, (1, win), 1)
+
+    def head_window(h):
+        low = jnp.minimum(lax.div(h * HD, 128) * 128, half - win)
+        inside = jnp.logical_and(win_lane >= h * HD - low, win_lane < h * HD - low + HD)
+        return pl.ds(pl.multiple_of(low, 128), win), inside
+
+    def only(inside, t):
+        return jnp.where(inside, t.astype(f32), 0.0).astype(bf16)
+
+    att[...] = jnp.zeros_like(att)
+
+    def head_forward(h, carry):
+        cols, inside = head_window(h)
+        score = dot(only(inside, q[:, cols]), k[:, cols], 1, 1) * scale + bias[...]
+        exponent = jnp.exp(score - jnp.max(score, -1, keepdims=True))
+        p = exponent / jnp.sum(exponent, -1, keepdims=True)
+        prob[h] = p
+        mixed = dot(p.astype(bf16), v[:, cols], 1, 0)
+        att[:, cols] = jnp.where(inside, mixed, att[:, cols].astype(f32)).astype(bf16)
+        return carry
+
+    lax.fori_loop(0, heads, head_forward, 0)
+
+    ag_chain(WUP)
+    ag_plane(WOUT)
+    ag_last(WOUT)
+
+    def widen(dst, terms):
+        for cols in halves:
+            total = None
+            for left, w in terms:
+                part = dot(left[...], W[w, cols, :], 1, 1)
+                total = part if total is None else total + part
+            dst[:, cols] = total.astype(dst.dtype)
+
+    widen(S.at[0], [(att, WOUT)])
+    e1 = exchange(2, S.at[0], X.at[0])
+    e1.start()
+    ag_chain(WDOWN)
+    e1.wait()
+
+    def resid1_rows(s):
+        for i, cols in enumerate(halves):
+            R1[s, cols] = R0[i, s, :] + (S[0, s, cols] + X[0, s, cols])
+
+    by_rows(16, resid1_rows)
+    norm_rows(lambda s: (R1[s, halves[0]], R1[s, halves[1]]), gains.at[1], nrm2)
+
+    ag_plane(WUP)
+    ag_last(WUP)
+    tmp[:, halves[0]] = dot(nrm2[...], W[WUP], 1, 0)
+
+    def gelu_rows(s):
+        t = tmp[s, halves[0]]
+        phi = 0.5 * (1.0 + lax.erf(t * (2.0 ** -0.5)))
+        mlp[s, :] = (t * phi).astype(bf16)
+        gprime[s, :] = phi + t * jnp.exp(-0.5 * t * t) * ((2.0 * math.pi) ** -0.5)
+
+    by_rows(16, gelu_rows)
+
+    def weight_grad(w, left, right):
+        for r in halves:
+            G[w, r, :] = dot(left[:, r], right, 0, 0).astype(bf16)
+
+    cot_copy.wait()
+    weight_grad(WDOWN, cot, mlp[...])
+    rs_start(WDOWN)
+    ag_plane(WDOWN)
+    ag_last(WDOWN)
+    tmp[:, halves[0]] = dot(cot[...], W[WDOWN], 1, 0)
+
+    def dup_rows(s):
+        dup[s, :] = (tmp[s, halves[0]] * gprime[s, :]).astype(bf16)
+
+    by_rows(16, dup_rows)
+    weight_grad(WUP, nrm2, dup[...])
+    rs_start(WUP)
+    widen(SB, [(mlp, WDOWN)])
+    e2 = exchange(3, SB, XB)
+    e2.start()
+    widen(S.at[1], [(dup, WUP)])
+    e3 = exchange(4, S.at[1], X.at[1])
+    e3.start()
+    rs_turn(WDOWN)
+    e2.wait()
+
+    def output_rows(s):
+        o_out[s, :] = (R1[s, :] + (SB[s, :].astype(f32) + XB[s, :].astype(f32))).astype(bf16)
+
+    by_rows(16, output_rows)
+    e3.wait()
+
+    def norm_grad(load, partial, gain, base, out, keep_sum):
+        def body(i, carry):
+            s = pl.ds(pl.multiple_of(i * 16, 16), 16)
+            xs = load(s)
+            mean = sum(jnp.sum(t * t, -1, keepdims=True) for t in xs) / width
+            r = lax.rsqrt(mean + 1e-06)
+            n1 = [t * r for t in xs]
+            dn = [partial[0][s, c] + partial[1][s, c] for c in halves]
+            gd = [gain[0:1, c] * t for c, t in zip(halves, dn)]
+            inner = sum(jnp.sum(a * b, -1, keepdims=True) for a, b in zip(gd, n1)) / width
+            for c, a, b in zip(halves, gd, n1):
+                out(s, c, base(s, c) + r * (a - b * inner))
+            for c, a, b in zip(halves, dn, n1):
+                prod = a * b
+                accg[:, c] += prod[0:8] + prod[8:16]
+            return carry
+
+        accg[...] = jnp.zeros_like(accg)
+        lax.fori_loop(0, rows // 16, body, 0)
+        total = accg[...]
+        high = total.astype(bf16)
+        keep_sum[...] = jnp.concatenate([high.astype(f32), total - high.astype(f32)], 0).astype(bf16)
+
+    def out1(s, c, t):
+        R1[s, c] = t
+        nrm2[s, c] = t.astype(bf16)
+
+    norm_grad(
+        lambda s: [R1[s, c] for c in halves],
+        (S.at[1], X.at[1]),
+        gains.at[1],
+        lambda s, c: cot[s, c].astype(f32),
+        out1,
+        dgs.at[1],
+    )
+    weight_grad(WOUT, nrm2, att[...])
+    rs_start(WOUT)
+    att[...] = dot(nrm2[...], W[WOUT], 1, 0).astype(bf16)
+    rs_turn(WUP)
+
+    def head_backward(h, carry):
+        cols, inside = head_window(h)
+        cols2 = pl.ds(pl.multiple_of(cols.start + half, 128), win)
+        p = prob[h]
+        da = only(inside, att[:, cols])
+        dp = dot(da, v[:, cols], 1, 1)
+        inner = jnp.sum(dp * p, -1, keepdims=True)
+        ds = (p * (dp - inner)).astype(bf16)
+        dv_h = dot(p.astype(bf16), da, 0, 0)
+        dq_h = dot(ds, k[:, cols], 1, 0) * scale
+        dk_h = dot(ds, q[:, cols], 0, 0) * scale
+        dv[:, cols] = jnp.where(inside, dv_h, dv[:, cols].astype(f32)).astype(bf16)
+        tmp[:, cols] = jnp.where(inside, dq_h, tmp[:, cols])
+        tmp[:, cols2] = jnp.where(inside, dk_h, tmp[:, cols2])
+        return carry
+
+    dv[...] = jnp.zeros_like(dv)
+    tmp[...] = jnp.zeros_like(tmp)
+    lax.fori_loop(0, heads, head_backward, 0)
+
+    def unrope_rows(s):
+        dq[s, :] = rope(tmp[s, halves[0]], s, True).astype(bf16)
+        dk[s, :] = rope(tmp[s, halves[1]], s, True).astype(bf16)
+
+    by_rows(16, unrope_rows)
+    for w, g in ((WQ, dq), (WK, dk), (WV, dv)):
+        weight_grad(w, nrm, g[...])
+        rs_start(w)
+    widen(S.at[0], [(dq, WQ), (dk, WK), (dv, WV)])
+    e4 = exchange(5, S.at[0], X.at[0])
+    e4.start()
+    rs_turn(WOUT)
+    rs_chain(WDOWN, o_down)
+    e4.wait()
+
+    def out0(s, c, t):
+        dr0[s, c] = t.astype(bf16)
+
+    norm_grad(
+        lambda s: [R0[i, s, :] for i in range(2)],
+        (S.at[0], X.at[0]),
+        gains.at[0],
+        lambda s, c: R1[s, c],
+        out0,
+        dgs.at[0],
+    )
+
+    weight_grad(IN2, hid, dr0[:, mcols])
+    rs_start(IN2)
+    for c in halves:
+        S[1, :, c] = dot(dr0[:, mcols], W[IN2, c, :], 1, 1)
+    e5 = exchange(6, S.at[1], X.at[1])
+    e5.start()
+    for w in (WQ, WK, WV):
+        rs_turn(w)
+    pre_act()
+    e5.wait()
+
+    def dpre_rows(s):
+        t = tmp[s, :]
+        sig = 1.0 / (1.0 + jnp.exp(-t))
+        grad = (S[1, s, :] + X[1, s, :]) * (sig * (1.0 + t * (1.0 - sig)))
+        nrm[s, :] = grad.astype(bf16)
+
+    by_rows(16, dpre_rows)
+    dval = dot(nrm[...], PK[0], 1, 0) + dot(dr0[...], PK[1], 1, 0)
+    o_dval[...] = (dval * keep_col[...])[:, 0:patch]
+
+    @pl.when(m == 0)
+    def _():
+        for r in halves:
+            GP[r, :] = dot(nrm[:, r], inx[...], 0, 0).astype(bf16)
+
+    @pl.when(m == 1)
+    def _():
+        for r in halves:
+            total = dot(dr0[:, r], inx[...], 0, 0)
+            for i in range(2):
+                pick = (gain_lane == 2 * patch + 1 + i).astype(bf16)
+                total = total + dot(dgs[i, :, r], pick, 0, 0)
+            GP[r, :] = total.astype(bf16)
+
+    rs_start(PACK)
+    rs_chain(WUP, o_up)
+    rs_turn(IN2)
+    rs_chain(WOUT, o_wout)
+    rs_turn(PACK)
+    for i, w in enumerate((WQ, WK, WV)):
+        rs_chain(w, o_qkv.at[i])
+    rs_chain(IN2, fin_in2.at[m])
+    e6 = exchange(7, fin_in2.at[m], fin_in2.at[m])
+    e6.start()
+    rs_chain(PACK, fin_pack.at[m])
+    e7 = exchange(8, fin_pack.at[m], fin_pack.at[m])
+    e7.start()
+    e6.wait()
+    for i, c in enumerate(halves):
+        o_in2[:, c] = fin_in2[i]
+    e7.wait()
+    o_pack[...] = fin_pack[...]
+
+    def drain(w, ref_of, sem, blocks):
+        ref = ref_of(blocks)
+        remote(ref, ref, sem.at[w], sem.at[w], XN).wait_send()
+
+    for w in order:
+        if w == PACK:
+            view = lambda n: PK.at[m, pl.ds(0, n * blk)]
+            rview = lambda n: RP.at[pl.ds(0, n)]
+        else:
+            view = lambda n, w=w: W.at[w, pl.ds(0, n * blk)]
+            rview = lambda n, w=w: R.at[w, pl.ds(0, n)]
+
+        drain(w, view, ag_send, 13)
+
+        @pl.when(z_inner == 1)
+        def _():
+            drain(w, view, ag_send, 4)
+
+        drain(w, rview, rs_send, 15)
 
 
 def rotate(vectors, places):
@@ -35,7 +775,7 @@
     return jax.nn.gelu(up_rows, approximate=False)
 
 
-def on_device(
+def general_device(
     values,
     lengths,
     w_in1,
@@ -241,6 +981,159 @@
     return (result, values_grad) + shares
 
 
+def fused_device(
+    values,
+    lengths,
+    w_in1,
+    b_in1,
+    w_in2,
+    b_in2,
+    w_res,
+    g_attn,
+    w_qkv,
+    w_out,
+    g_mlp,
+    w_up,
+    w_down,
+    cotangent,
+):
+    rows, width = cotangent.shape
+    half = w_out.shape[0]
+    blk = w_in2.shape[0]
+    patch = values.shape[1]
+    tok_in = w_in1.shape[0]
+    heads = half // HD
+
+    def column(vec):
+        return vec[:, None]
+
+    def lanes(parts):
+        used = sum(p.shape[1] for p in parts)
+        return jnp.concatenate(parts + [jnp.zeros((blk, PL - used), bf16)], 1)
+
+    pack = jnp.stack(
+        [
+            lanes([w_in1.T, column(b_in1)]),
+            lanes([w_res.T, column(b_in2), column(g_attn), column(g_mlp)]),
+        ]
+    )
+    vmem = pl.BlockSpec(memory_space=pltpu.VMEM)
+    hbm = pl.BlockSpec(memory_space=pl.ANY)
+    out_shape = (
+        jax.ShapeDtypeStruct((rows, width), bf16),
+        jax.ShapeDtypeStruct((rows, patch), f32),
+        jax.ShapeDtypeStruct((2, blk, PL), f32),
+        jax.ShapeDtypeStruct((blk, width), f32),
+        jax.ShapeDtypeStruct((3, blk, half), f32),
+        jax.ShapeDtypeStruct((blk, half), f32),
+        jax.ShapeDtypeStruct((blk, half), f32),
+        jax.ShapeDtypeStruct((blk, half), f32),
+    )
+    V = pltpu.VMEM
+    scratch = [
+        V((NW, width, half), bf16),
+        V((2, width, PL), bf16),
+        V((NW, width, half), bf16),
+        V((width, PL), bf16),
+        V((NW, SLOTS, blk, half), bf16),
+        V((SLOTS, blk, PL), bf16),
+        V((2, rows, half), f32),
+        V((rows, width), f32),
+        V((2, rows, width), f32),
+        V((2, rows, width), f32),
+        V((rows, width), bf16),
+        V((rows, width), bf16),
+        V((rows, width), bf16),
+        V((rows, width), bf16),
+        V((rows, width), bf16),
+        V((rows, half), bf16),
+        V((rows, half), bf16),
+        V((rows, half), bf16),
+        V((heads, rows, rows), f32),
+        V((rows, half), bf16),
+        V((rows, half), f32),
+        V((rows, half), bf16),
+        V((rows, width), bf16),
+        V((rows, half), bf16),
+        V((rows, half), bf16),
+        V((rows, half), bf16),
+        V((rows, half), bf16),
+        V((rows, width), f32),
+        V((rows, width), bf16),
+        V((rows, half), f32),
+        V((rows, half), f32),
+        V((rows, rows), f32),
+        V((rows, PL), bf16),
+        V((2, 8, width), f32),
+        V((2, 16, width), bf16),
+        V((8, width), f32),
+        V((rows, PL), f32),
+        V((blk, half), f32),
+        V((blk, PL), f32),
+        V((2, blk, half), f32),
+        V((2, blk, PL), f32),
+        pltpu.SemaphoreType.DMA((8,)),
+        pltpu.SemaphoreType.DMA((8, 16)),
+        pltpu.SemaphoreType.DMA((8,)),
+        pltpu.SemaphoreType.DMA((8, SLOTS)),
+        pltpu.SemaphoreType.DMA((9,)),
+        pltpu.SemaphoreType.DMA((9,)),
+        pltpu.SemaphoreType.DMA((9,)),
+    ]
+    out, d_values, d_pack, d_in2, d_qkv, d_out_t, d_up, d_down_t = pl.pallas_call(
+        fused_kernel,
+        name="layer",
+        out_shape=out_shape,
+        in_specs=[pl.BlockSpec(memory_space=pltpu.SMEM), vmem] + [hbm] * 7,
+        out_specs=(vmem,) * len(out_shape),
+        scratch_shapes=scratch,
+        compiler_params=pltpu.CompilerParams(
+            collective_id=0, has_side_effects=True, vmem_limit_bytes=VMEM_BYTES
+        ),
+    )(
+        lengths,
+        values,
+        pack,
+        w_in2,
+        jnp.transpose(w_qkv, (1, 0, 2)),
+        w_out.T,
+        w_up,
+        w_down.T,
+        cotangent,
+    )
+    return (
+        out,
+        d_values,
+        d_pack[0, :, :tok_in].T,
+        d_pack[0, :, tok_in],
+        d_in2,
+        d_pack[1, :, tok_in],
+        d_pack[1, :, :tok_in].T,
+        d_pack[1, :, tok_in + 1],
+        jnp.transpose(d_qkv, (1, 0, 2)),
+        d_out_t.T,
+        d_pack[1, :, tok_in + 2],
+        d_up,
+        d_down_t.T,
+    )
+
+
+def on_device(*args):
+    blk, width = args[4].shape
+    half = args[9].shape[0]
+    shards = width // blk
+    series = args[1].shape[0]
+    fits = (
+        shards == 16
+        and 2 * half == width
+        and blk % 16 == 0
+        and half % 128 == 0
+        and args[0].shape[0] % 64 == 0
+        and series <= 8
+    )
+    return (fused_device if fits else general_device)(*args)
+
+
 def solution(mesh):
     in_specs = (
         P("fsdp", None),

time: 1260 us -> 306 us (0.24)
  waiting for transfers between devices: 879 us -> 0 us
  Pallas kernels: 0 us -> 287 us
  blocking collectives: 235 us -> 0 us
  matrix products: 57.3 us -> 0 us
  local copies, waits for them, and re-layouts: 43.2 us -> 16.5 us
  other arithmetic: 21.6 us -> 0.71 us
  between operations: 15.9 us -> 0.72 us
    reduce_scatter x5 -> x0, waiting for transfers between devices: 605 us -> none  [the longest x1 211 us: on_device(): lax.psum_scatter(grad_qkv, 'fsdp', scatter_dimension=0, tiled=True)]
    pallas_call x0 -> x1, Pallas kernels: none -> 287 us  [fused_device(): pl.pallas_call(fused_kernel, name='layer', out_shape=out_shape, in_specs=...]
    unnamed x2 -> x0, blocking collectives: 156 us -> none
    all_gather x5 -> x0, waiting for transfers between devices: 150 us -> none  [the longest x1 60.7 us: on_device(): lax.all_gather(w_up, 'fsdp', axis=0, tiled=True)]
    all_gather x2 -> x0, blocking collectives: 79 us -> none  [the longest x1 40.2 us: on_device(): lax.all_gather(w_res, 'fsdp', axis=1, tiled=True)]
    psum x4 -> x0, waiting for transfers between devices: 75.4 us -> none  [the longest x1 21.4 us: on_device(): lax.psum(jnp.dot(mlp_hidden, full_down, preferred_element_type=f32).astyp...]
    dot_general x25 -> x0, matrix products: 54.8 us -> none  [the longest x1 5.43 us: on_device(): jnp.einsum('td,tch->dch', normed, qkv_rows, preferred_element_type=f32)]
    unnamed x18 -> x0, waiting for transfers between devices: 49.2 us -> none
  transfers between devices with their start and end apart: 16 -> 0, of which waited for: 13 -> 0; matrix products, arithmetic and copies ran while one was open for 5% -> 0% of each run, Pallas kernels for 0% -> 0%
where the time goes in v1:
time: 306 us; the launch traced here: 305 us
  Pallas kernels  287 us (94%)
  local copies, waits for them, and re-layouts  16.5 us (5%)
    pallas_call x1, Pallas kernels, fused_device(): pl.pallas_call(fused_kernel, name='layer', out_shape=out_shape, in_specs=...  287 us
    unnamed x38, local copies, waits for them, and re-layouts  14.1 us

profile of v1, /device:TPU:0, one launch (start us, length us, event | category | flops | bytes accessed | tf_op | source)
XLA Modules:
  0.0 305.1 jit_solution(10070550679758291194)
XLA Ops:
  0.6 0.8 copy.39
  1.5 0.0 copy-start.9
  1.5 0.7 copy-done.9
  2.1 0.1 copy.40
  2.2 0.0 copy-start.10
  2.2 0.7 copy-done.10
  2.9 0.1 copy.41
  3.0 0.0 copy-start.11
  3.0 0.7 copy-done.11
  3.7 0.1 copy.42
  3.8 0.0 copy-start.8
  3.8 0.1 concatenate.7
  3.9 0.6 copy-done.8
  4.5 0.1 copy.37
  4.6 0.0 copy-start.12
  4.6 0.7 copy-done.12
  5.3 0.1 copy.38
  5.4 0.1 pad.4.clone
  5.5 0.1 maximum_bitcast_fusion
  5.6 0.0 copy-start.7
  5.6 0.6 pad_maximum_fusion.pack
  6.2 0.1 copy-done.7
  6.3 0.7 copy.43.values
  7.0 287.2 %layer.1 = (bf16[256,1280]{1,0:T(8,128)(2,1)}, f32[256,32]{1,0:T(8,128)}, f32[2,80,128]{2,1,0:T(8,128)}, f32[80,1280]{1,0:T(8,128)}, f32[3,80,640]{2,1,0:T(8,128...) custom-call(s32[4]{0:T(128)} %lengths.1, bf16[256,32]{1,0:T(8,128)(2,1)} %copy.43.values, ...), custom_call_target="tpu_custom_call" | custom-call | tf_op jit(solution)/shard_map/layer/pallas_call | solution.py:1083
  294.2 0.0 copy-start
  294.2 1.7 slice_reduce_fusion
  295.9 0.0 copy-done
  295.9 0.0 copy-start.6
  295.9 0.7 copy.45
  296.6 0.7 copy.46
  297.3 0.0 copy-done.6
  297.3 0.7 copy.44
  298.0 0.0 copy-start.2
  298.0 2.0 copy.53
  300.1 0.0 copy-done.2
  300.1 0.0 copy-start.1
  300.1 0.8 copy.54
  300.8 0.5 copy-done.1
  301.3 0.0 copy-start.5
  301.3 0.8 copy.55
  302.1 0.3 copy-done.5
  302.4 0.0 copy-start.4
  302.4 0.7 copy.56
  303.1 0.3 copy-done.4
  303.4 0.0 copy-start.3
  303.4 0.7 copy.57
  304.1 0.3 copy-done.3
  304.4 0.7 copy.58
  (3 shorter events, 0.0 us)
Async XLA Ops:
  1.5 0.7 copy-start.9
  2.2 0.7 copy-start.10
  3.0 0.7 copy-start.11
  3.8 0.7 copy-start.8
  4.6 0.7 copy-start.12
  5.6 0.7 copy-start.7
  294.2 1.7 copy-start
  295.9 1.4 copy-start.6
  298.0 2.0 copy-start.2
  300.1 1.2 copy-start.1
  301.3 1.1 copy-start.5
  302.4 1.0 copy-start.4
  303.4 1.0 copy-start.3

commit v2 on v0

--- a/solution.py
+++ b/solution.py
@@ -1,9 +1,955 @@
+import functools
+import math
+
 import jax
 import jax.numpy as jnp
 from jax import lax
+from jax.experimental import pallas as pl
+from jax.experimental.pallas import tpu as pltpu
 from jax.sharding import PartitionSpec as P
 
 HD = 80
+MESH = pl.DeviceIdType.MESH
+VMEM_BYTES = 63 * 2**20
+f32 = jnp.float32
+bf16 = jnp.bfloat16
+
+IN2, WQ, WK, WV, WOUT, WUP, WDOWN, PACK = range(8)
+NW = 7
+PL = 128
+PLANE_FIRST = ()
+Z_FIRST = ()
+CHAIN_LAST = tuple(w for w in range(NW) if w not in Z_FIRST)
+SLOT_A, SLOT_X, SLOT_Y, SLOT_V, SLOTS = 0, 4, 8, 12, 16
+Z_RELAY, Z_NEAR, Z_FAR, Z_A, Z_X, Z_Y, Z_SLOTS = 0, 8, 12, 16, 17, 18, 19
+
+
+def dot(left, right, left_dim, right_dim):
+    return lax.dot_general(
+        left, right, (((left_dim,), (right_dim,)), ((), ())), preferred_element_type=f32
+    )
+
+
+def layer_kernel(
+    lengths,
+    values_t,
+    w_in1,
+    w_res,
+    b_in1,
+    b_in2,
+    g_attn,
+    g_mlp,
+    in2,
+    qkv,
+    out_t,
+    up,
+    down_t,
+    cot_hbm,
+    o_out,
+    o_dval,
+    o_in1,
+    o_b1,
+    o_in2,
+    o_b2,
+    o_res,
+    o_gattn,
+    o_qkv,
+    o_wout,
+    o_gmlp,
+    o_up,
+    o_down,
+    W,
+    PK,
+    G,
+    GP,
+    R,
+    RZ,
+    RP,
+    R0,
+    R1,
+    S,
+    X,
+    SB,
+    XB,
+    hid,
+    nrm,
+    nrm2,
+    q,
+    k,
+    v,
+    prob,
+    att,
+    gprime,
+    mlp,
+    cot,
+    dup,
+    dq,
+    dk,
+    dv,
+    tmp,
+    dr0,
+    rope_c,
+    rope_s,
+    bias,
+    inx,
+    gains,
+    dgs,
+    accg,
+    keep_col,
+    fin_in2,
+    fin_pack,
+    ag_send,
+    ag_recv,
+    rs_send,
+    rs_recv,
+    ex_send,
+    ex_recv,
+    lsem,
+):
+    rows, width = cot.shape
+    half = W.shape[2]
+    blk = in2.shape[0]
+    series = lengths.shape[0]
+    seq = rows // series
+    heads = half // HD
+    patch = values_t.shape[0]
+
+    f = lax.axis_index("fsdp")
+    m = lax.axis_index("mp")
+    x = lax.rem(f, 2)
+    y = lax.rem(lax.div(f, 2), 2)
+    z = lax.div(f, 4)
+    c0 = f - 4 * z
+    cx = c0 + 1 - 2 * x
+    cy = c0 + 2 - 4 * y
+    cd = 3 - c0
+    XN, YN, SIB = (4 * z + cx, m), (4 * z + cy, m), (f, 1 - m)
+    z_high = (z >= 2).astype(jnp.int32)
+    inner = jnp.logical_and(z > 0, z < 3)
+    z_inner = inner.astype(jnp.int32)
+    z_near = z + 1 - 2 * lax.rem(z, 2)
+    z_far = 2 - z_high
+    z_even = lax.rem(z, 2) == 0
+
+    def plane(zb):
+        return (4 * zb + c0, m)
+
+    def near(i):
+        swap = (i == 0).astype(jnp.int32) - (i == 1).astype(jnp.int32)
+        low = i + z_inner * swap
+        return low + z_high * (3 - 2 * low)
+
+    def far(i):
+        return near(3 - i)
+
+    def each_plane(order, body, start=0):
+        def step(i, carry):
+            body(order(i))
+            return carry
+
+        lax.fori_loop(start, 4, step, 0)
+
+    def each_other_plane(body):
+        each_plane(near, body, 1)
+
+    def row_of(b):
+        return pl.ds(pl.multiple_of(b * blk, 16), blk)
+
+    def w_block(w, b):
+        return PK.at[m, row_of(b)] if w == PACK else W.at[w, row_of(b)]
+
+    def g_block(w, b):
+        return GP.at[row_of(b)] if w == PACK else G.at[w, row_of(b)]
+
+    def r_block(w, s):
+        if w == PACK:
+            return RP.at[s]
+        if w in Z_FIRST:
+            return RZ.at[Z_FIRST.index(w), s]
+        return R.at[CHAIN_LAST.index(w), s]
+
+    def remote(src, dst, send, recv, dev):
+        return pltpu.make_async_remote_copy(
+            src_ref=src, dst_ref=dst, send_sem=send, recv_sem=recv, device_id=dev, device_id_type=MESH
+        )
+
+    def ag_push(w, b, *devs):
+        ref = w_block(w, b)
+        for dev in devs:
+            remote(ref, ref, ag_send.at[w], ag_recv.at[w, b], dev).start()
+
+    def ag_await(w, b):
+        ref = w_block(w, b)
+        remote(ref, ref, ag_send.at[w], ag_recv.at[w, b], XN).wait_recv()
+
+    mcols = pl.ds(pl.multiple_of(m * half, 128), half)
+
+    def own_copy(w):
+        if w == IN2:
+            src = in2.at[:, mcols]
+        elif w in (WQ, WK, WV):
+            src = qkv.at[w - WQ]
+        else:
+            src = {WOUT: out_t, WUP: up, WDOWN: down_t}[w]
+        return pltpu.make_async_copy(src, w_block(w, f), lsem.at[w])
+
+    def ag_own(w):
+        if w != PACK:
+            own_copy(w).wait()
+        ag_push(w, f, XN, YN)
+        if w in PLANE_FIRST:
+            ag_push(w, f, plane(z_near), plane(z_far))
+        else:
+            each_other_plane(lambda zb: ag_push(w, f, plane(zb)))
+
+    def ag_column(w):
+        def body(zb):
+            b = 4 * zb + c0
+            ag_await(w, b)
+            ag_push(w, b, XN, YN)
+
+        each_other_plane(body)
+
+    def ag_pass(w, zb, even, *more):
+        ag_await(w, 4 * zb + cx)
+
+        @pl.when(even)
+        def _():
+            ag_push(w, 4 * zb + cx, YN)
+
+        ag_push(w, 4 * zb + cx, *more)
+        ag_await(w, 4 * zb + cy)
+
+        @pl.when(jnp.logical_not(even))
+        def _():
+            ag_push(w, 4 * zb + cy, XN)
+
+        ag_push(w, 4 * zb + cy, *more)
+
+    def ag_plane(w):
+        if w in PLANE_FIRST:
+            to = (plane(z_near), plane(z_far))
+            ag_pass(w, z, z_even, *to)
+            ag_await(w, 4 * z + cd)
+            ag_push(w, 4 * z + cd, *to)
+        else:
+            each_plane(near, lambda zb: ag_pass(w, zb, lax.rem(zb, 2) == 0))
+
+    def ag_relay(w):
+        @pl.when(inner)
+        def _():
+            for zb in (3 - z, 3 * (1 - z_high)):
+                for c in (c0, cx, cy, cd):
+                    ag_await(w, 4 * zb + c)
+                    ag_push(w, 4 * zb + c, plane(3 * z_high))
+
+    def ag_last(w):
+        if w in PLANE_FIRST:
+            for c in (c0, cx, cy, cd):
+                ag_await(w, 4 * z_near + c)
+
+            @pl.when(jnp.logical_not(inner))
+            def _():
+                for zb in (z_far, 3 - z):
+                    for c in (c0, cx, cy, cd):
+                        ag_await(w, 4 * zb + c)
+        else:
+            each_plane(near, lambda zb: ag_await(w, 4 * zb + cd))
+
+    final_of = {
+        IN2: lambda: fin_in2.at[m],
+        WQ: lambda: o_qkv.at[0],
+        WK: lambda: o_qkv.at[1],
+        WV: lambda: o_qkv.at[2],
+        WOUT: lambda: o_wout,
+        WUP: lambda: o_up,
+        WDOWN: lambda: o_down,
+        PACK: lambda: fin_pack.at[m],
+    }
+
+    def rs_push(w, src, slot, dev):
+        remote(src, r_block(w, slot), rs_send.at[w], rs_recv.at[w, slot], dev).start()
+
+    def rs_await(w, slot):
+        ref = r_block(w, slot)
+        remote(ref, ref, rs_send.at[w], rs_recv.at[w, slot], XN).wait_recv()
+
+    def add_to(ref, other):
+        ref[...] = (ref[...].astype(f32) + other[...].astype(f32)).astype(bf16)
+
+    def sum3(a, b, c):
+        return a[...].astype(f32) + b[...].astype(f32) + c[...].astype(f32)
+
+    def rs_start(w):
+        if w in Z_FIRST:
+            cs = (cd, cx, cy, c0)
+
+            @pl.when(jnp.logical_not(inner))
+            def _():
+                for zb in (3 - z, z_far):
+                    for c in cs:
+                        slot = Z_RELAY + 4 * lax.rem(zb, 2) + c
+                        rs_push(w, g_block(w, 4 * zb + c), slot, plane(1 + z_high))
+
+            for c in cs:
+                rs_push(w, g_block(w, 4 * z_near + c), Z_NEAR + c, plane(z_near))
+            return
+
+        def body(zb):
+            even = lax.rem(zb, 2) == 0
+
+            @pl.when(even)
+            def _():
+                rs_push(w, g_block(w, 4 * zb + cd), SLOT_A + zb, YN)
+                rs_push(w, g_block(w, 4 * zb + cy), SLOT_Y + zb, YN)
+
+            @pl.when(jnp.logical_not(even))
+            def _():
+                rs_push(w, g_block(w, 4 * zb + cd), SLOT_A + zb, XN)
+                rs_push(w, g_block(w, 4 * zb + cx), SLOT_X + zb, XN)
+
+        each_plane(far, body)
+
+    def turn(w, slot_a, even, own_x, own_y, slot_x, slot_y):
+        rs_await(w, slot_a)
+        ref = r_block(w, slot_a)
+
+        @pl.when(even)
+        def _():
+            add_to(ref, own_x)
+            rs_push(w, ref, slot_x, XN)
+
+        @pl.when(jnp.logical_not(even))
+        def _():
+            add_to(ref, own_y)
+            rs_push(w, ref, slot_y, YN)
+
+    def rs_turn(w):
+        if w in Z_FIRST:
+            turn(w, Z_A, z_even, r_block(w, Z_NEAR + cx), r_block(w, Z_NEAR + cy), Z_X, Z_Y)
+            return
+        each_plane(
+            far,
+            lambda zb: turn(
+                w,
+                SLOT_A + zb,
+                lax.rem(zb, 2) == 0,
+                g_block(w, 4 * zb + cx),
+                g_block(w, 4 * zb + cy),
+                SLOT_X + zb,
+                SLOT_Y + zb,
+            ),
+        )
+
+    def rs_relay(w):
+        @pl.when(inner)
+        def _():
+            for zb in (3 * (1 - z_high), z_far):
+                for c in (cd, cx, cy, c0):
+                    slot = Z_RELAY + 4 * lax.rem(zb, 2) + c
+                    rs_await(w, slot)
+                    ref = r_block(w, slot)
+                    add_to(ref, g_block(w, 4 * zb + c))
+                    rs_push(w, ref, Z_FAR + c, plane(zb))
+
+    def rs_zsum(w):
+        for c in (cd, cx, cy, c0):
+            rs_await(w, Z_NEAR + c)
+            rs_await(w, Z_FAR + c)
+            ref = r_block(w, Z_NEAR + c)
+            total = sum3(ref, r_block(w, Z_FAR + c), g_block(w, 4 * z + c))
+            if c is c0:
+                final_of[w]()[...] = total
+            else:
+                ref[...] = total.astype(bf16)
+            if c is cd:
+
+                @pl.when(z_even)
+                def _():
+                    rs_push(w, ref, Z_A, YN)
+
+                @pl.when(jnp.logical_not(z_even))
+                def _():
+                    rs_push(w, ref, Z_A, XN)
+
+            if c is cx:
+
+                @pl.when(jnp.logical_not(z_even))
+                def _():
+                    rs_push(w, ref, Z_X, XN)
+
+            if c is cy:
+
+                @pl.when(z_even)
+                def _():
+                    rs_push(w, ref, Z_Y, YN)
+
+    def plane_sum(w, zb):
+        rs_await(w, SLOT_X + zb)
+        rs_await(w, SLOT_Y + zb)
+        return sum3(g_block(w, 4 * zb + c0), r_block(w, SLOT_X + zb), r_block(w, SLOT_Y + zb))
+
+    def rs_out(w):
+        def body(zb):
+            ref = r_block(w, SLOT_X + zb)
+            ref[...] = plane_sum(w, zb).astype(bf16)
+            rs_push(w, ref, SLOT_V + z, plane(zb))
+
+        each_other_plane(body)
+        final_of[w]()[...] = plane_sum(w, z)
+
+    def rs_final(w):
+        final = final_of[w]()
+        if w in Z_FIRST:
+            rs_await(w, Z_X)
+            rs_await(w, Z_Y)
+            final[...] = sum3(final, r_block(w, Z_X), r_block(w, Z_Y))
+            return
+
+        for i in (1, 2, 3):
+            rs_await(w, SLOT_V + near(jnp.int32(i)))
+        parts = [r_block(w, SLOT_V + near(jnp.int32(i)))[...].astype(f32) for i in (1, 2, 3)]
+        final[...] = final[...] + (parts[0] + parts[1] + parts[2])
+
+    def exchange(i):
+        src, dst = {
+            0: lambda: (PK.at[m], PK.at[m]),
+            1: lambda: (R0.at[m], R0.at[m]),
+            2: lambda: (S.at[0], X.at[0]),
+            3: lambda: (SB, XB),
+            4: lambda: (S.at[1], X.at[1]),
+            5: lambda: (S.at[0], X.at[0]),
+            6: lambda: (S.at[1], X.at[1]),
+            7: lambda: (fin_in2.at[m], fin_in2.at[m]),
+            8: lambda: (fin_pack.at[m], fin_pack.at[m]),
+        }[i]()
+        return remote(src, dst, ex_send.at[i], ex_recv.at[i], SIB)
+
+    def swap_start(i):
+        exchange(i).start()
+
+    def swap_wait(i):
+        exchange(i).wait()
+
+    def by_rows(step, body, unroll=4):
+        def one(i, carry):
+            body(pl.ds(pl.multiple_of(i * step, step), step))
+            return carry
+
+        lax.fori_loop(0, rows // step, one, 0, unroll=unroll)
+
+    halves = (slice(0, half), slice(half, width))
+
+    lens = [lengths[s] for s in range(series)]
+
+    def pad_of(slot):
+        total = jnp.zeros(slot.shape, jnp.int32)
+        for s in range(series):
+            inside = jnp.logical_and(slot >= s * seq, slot < (s + 1) * seq)
+            total = jnp.where(inside, (s + 1) * seq - lens[s], total)
+        return total
+
+    def series_of(slot):
+        total = jnp.zeros(slot.shape, jnp.int32)
+        for s in range(1, series):
+            total = total + (slot >= s * seq).astype(jnp.int32)
+        return total
+
+    lane = lax.broadcasted_iota(jnp.int32, (1, half), 1).astype(f32)
+    in_head = lane - HD * jnp.floor((lane + 0.5) / HD)
+    first = in_head < HD // 2
+
+    def prepare():
+        slot_col = lax.broadcasted_iota(jnp.int32, (rows, 1), 0)
+        keep = jnp.broadcast_to((slot_col >= pad_of(slot_col)).astype(f32), keep_col.shape)
+        keep_col[...] = keep
+        lane_i = lax.broadcasted_iota(jnp.int32, (rows, PL), 1)
+        tall = jnp.concatenate([values_t[...].astype(f32), jnp.zeros((PL - patch, rows), f32)], 0)
+        inx[...] = jnp.where(
+            lane_i < patch,
+            tall.T * keep,
+            jnp.where(lane_i < 2 * patch, 1.0 - keep, (lane_i == 2 * patch).astype(f32)),
+        ).astype(bf16)
+
+        key_slot = lax.broadcasted_iota(jnp.int32, (1, rows), 1)
+        key_ok = (key_slot >= pad_of(key_slot)).astype(jnp.int32)
+        key_series = series_of(key_slot)
+
+        def bias_rows(s):
+            shape = (s.size, rows)
+            a = lax.broadcasted_iota(jnp.int32, shape, 0) + s.start
+            b = jnp.broadcast_to(key_slot, shape)
+            same = series_of(a) == jnp.broadcast_to(key_series, shape)
+            ok = jnp.logical_or(jnp.broadcast_to(key_ok, shape) == 1, a == b)
+            allowed = jnp.logical_and(jnp.logical_and(same, b <= a), ok)
+            bias[s, :] = jnp.where(allowed, 0.0, -1e30)
+
+        by_rows(32, bias_rows, 1)
+        turn_i = jnp.where(first, in_head, in_head - HD // 2)
+        frequency = jnp.exp(turn_i * (-2.0 * math.log(10000.0) / HD))
+
+        def rope_rows(s):
+            slot = lax.broadcasted_iota(jnp.int32, (s.size, 1), 0) + s.start
+            place = (slot - pad_of(slot)).astype(f32)
+            angle = place * frequency
+            rope_c[s, :] = jnp.cos(angle)
+            sine = jnp.sin(angle)
+            rope_s[s, :] = jnp.where(first, -sine, sine)
+
+        by_rows(16, rope_rows, 1)
+
+    def rope(t, s, inverse):
+        other = jnp.where(first, pltpu.roll(t, half - HD // 2, 1), pltpu.roll(t, HD // 2, 1))
+        turned = other * rope_s[s, :]
+        return t * rope_c[s, :] - turned if inverse else t * rope_c[s, :] + turned
+
+    gain_lane = lax.broadcasted_iota(jnp.int32, (16, PL), 1)
+
+    def pre_act():
+        for cols in halves:
+            tmp[:, cols] = dot(inx[...], PK[0, cols, :], 1, 1)
+
+    def token_hidden():
+        for i in range(2):
+            pick = (gain_lane == 2 * patch + 1 + i).astype(bf16)
+            gains[i] = dot(pick, PK[1], 1, 1)[0:8]
+        pre_act()
+
+        def silu_rows(s):
+            t = tmp[s, :]
+            hid[s, :] = (t / (1.0 + jnp.exp(-t))).astype(bf16)
+
+        by_rows(16, silu_rows)
+
+    def token_out():
+        R0[m] = dot(hid[...], W[IN2], 1, 0) + dot(inx[...], PK[1, mcols, :], 1, 1)
+
+    def norm_rows(load, gain, out):
+        def body(s):
+            a, b = load(s)
+            mean = (jnp.sum(a * a, -1, keepdims=True) + jnp.sum(b * b, -1, keepdims=True)) / width
+            scale = lax.rsqrt(mean + 1e-06)
+            out[s, halves[0]] = (a * scale * gain[0:1, halves[0]]).astype(bf16)
+            out[s, halves[1]] = (b * scale * gain[0:1, halves[1]]).astype(bf16)
+
+        by_rows(16, body)
+
+    def norm_first():
+        norm_rows(lambda s: (R0[0, s, :], R0[1, s, :]), gains.at[0], nrm)
+
+    def project(w, out):
+        tmp[:, halves[0]] = dot(nrm[...], W[w], 1, 0)
+
+        def body(s):
+            out[s, :] = rope(tmp[s, halves[0]], s, False).astype(bf16)
+
+        by_rows(16, body)
+
+    def project_v():
+        v[...] = dot(nrm[...], W[WV], 1, 0).astype(bf16)
+
+    win = 256
+    scale = HD ** (-0.5)
+    win_lane = lax.broadcasted_iota(jnp.int32, (1, win), 1)
+
+    def head_window(h):
+        low = jnp.minimum(lax.div(h * HD, 128) * 128, half - win)
+        inside = jnp.logical_and(win_lane >= h * HD - low, win_lane < h * HD - low + HD)
+        return pl.ds(pl.multiple_of(low, 128), win), inside
+
+    def only(inside, t):
+        return jnp.where(inside, t.astype(f32), 0.0).astype(bf16)
+
+    def attend():
+        att[...] = jnp.zeros_like(att)
+
+        def one(h, carry):
+            cols, inside = head_window(h)
+            score = dot(only(inside, q[:, cols]), k[:, cols], 1, 1) * scale + bias[...]
+            exponent = jnp.exp(score - jnp.max(score, -1, keepdims=True))
+            p = exponent / jnp.sum(exponent, -1, keepdims=True)
+            prob[h] = p
+            mixed = dot(p.astype(bf16), v[:, cols], 1, 0)
+            att[:, cols] = jnp.where(inside, mixed, att[:, cols].astype(f32)).astype(bf16)
+            return carry
+
+        lax.fori_loop(0, heads, one, 0, unroll=2)
+
+    def widen(dst, terms):
+        for cols in halves:
+            total = None
+            for left, w in terms:
+                part = dot(left[...], W[w, cols, :], 1, 1)
+                total = part if total is None else total + part
+            dst[:, cols] = total.astype(dst.dtype)
+
+    def attend_out():
+        widen(S.at[0], [(att, WOUT)])
+
+    def norm_second():
+        def body(s):
+            for i, cols in enumerate(halves):
+                R1[s, cols] = R0[i, s, :] + (S[0, s, cols] + X[0, s, cols])
+
+        by_rows(16, body)
+        norm_rows(lambda s: (R1[s, halves[0]], R1[s, halves[1]]), gains.at[1], nrm2)
+
+    def feed_up():
+        tmp[:, halves[0]] = dot(nrm2[...], W[WUP], 1, 0)
+
+        def gelu_rows(s):
+            t = tmp[s, halves[0]]
+            phi = 0.5 * (1.0 + lax.erf(t * (2.0**-0.5)))
+            mlp[s, :] = (t * phi).astype(bf16)
+            gprime[s, :] = phi + t * jnp.exp(-0.5 * t * t) * ((2.0 * math.pi) ** -0.5)
+
+        by_rows(16, gelu_rows)
+
+    def weight_grad(w, left, right):
+        for r in halves:
+            G[w, r, :] = dot(left[:, r], right, 0, 0).astype(bf16)
+
+    def grad_down():
+        cot_copy.wait()
+        weight_grad(WDOWN, cot, mlp[...])
+
+    def grad_hidden():
+        tmp[:, halves[0]] = dot(cot[...], W[WDOWN], 1, 0)
+
+        def dup_rows(s):
+            dup[s, :] = (tmp[s, halves[0]] * gprime[s, :]).astype(bf16)
+
+        by_rows(16, dup_rows)
+
+    def grad_up():
+        weight_grad(WUP, nrm2, dup[...])
+
+    def feed_down():
+        widen(SB, [(mlp, WDOWN)])
+
+    def grad_norm2():
+        widen(S.at[1], [(dup, WUP)])
+
+    def write_output():
+        def body(s):
+            o_out[s, :] = (R1[s, :] + (SB[s, :].astype(f32) + XB[s, :].astype(f32))).astype(bf16)
+
+        by_rows(16, body)
+
+    def norm_grad(load, i_part, gain, base, out, keep_sum):
+        def body(i, carry):
+            s = pl.ds(pl.multiple_of(i * 16, 16), 16)
+            xs = load(s)
+            mean = sum(jnp.sum(t * t, -1, keepdims=True) for t in xs) / width
+            r = lax.rsqrt(mean + 1e-06)
+            n1 = [t * r for t in xs]
+            dn = [S[i_part, s, c] + X[i_part, s, c] for c in halves]
+            gd = [gain[0:1, c] * t for c, t in zip(halves, dn)]
+            along = sum(jnp.sum(a * b, -1, keepdims=True) for a, b in zip(gd, n1)) / width
+            for c, a, b in zip(halves, gd, n1):
+                out(s, c, base(s, c) + r * (a - b * along))
+            for c, a, b in zip(halves, dn, n1):
+                prod = a * b
+                accg[:, c] += prod[0:8] + prod[8:16]
+            return carry
+
+        accg[...] = jnp.zeros_like(accg)
+        lax.fori_loop(0, rows // 16, body, 0, unroll=4)
+        total = accg[...]
+        high = total.astype(bf16)
+        keep_sum[...] = jnp.concatenate([high.astype(f32), total - high.astype(f32)], 0).astype(bf16)
+
+    def norm_grad2():
+        def out(s, c, t):
+            R1[s, c] = t
+            nrm2[s, c] = t.astype(bf16)
+
+        norm_grad(
+            lambda s: [R1[s, c] for c in halves],
+            1,
+            gains.at[1],
+            lambda s, c: cot[s, c].astype(f32),
+            out,
+            dgs.at[1],
+        )
+
+    def norm_grad1():
+        def out(s, c, t):
+            dr0[s, c] = t.astype(bf16)
+
+        norm_grad(
+            lambda s: [R0[i, s, :] for i in range(2)],
+            0,
+            gains.at[0],
+            lambda s, c: R1[s, c],
+            out,
+            dgs.at[0],
+        )
+
+    def grad_out():
+        weight_grad(WOUT, nrm2, att[...])
+
+    def grad_attended():
+        att[...] = dot(nrm2[...], W[WOUT], 1, 0).astype(bf16)
+
+    def attend_back():
+        dv[...] = jnp.zeros_like(dv)
+        tmp[...] = jnp.zeros_like(tmp)
+
+        def one(h, carry):
+            cols, inside = head_window(h)
+            cols2 = pl.ds(pl.multiple_of(cols.start + half, 128), win)
+            p = prob[h]
+            da = only(inside, att[:, cols])
+            dp = dot(da, v[:, cols], 1, 1)
+            ds = (p * (dp - jnp.sum(dp * p, -1, keepdims=True))).astype(bf16)
+            dv_h = dot(p.astype(bf16), da, 0, 0)
+            dq_h = dot(ds, k[:, cols], 1, 0) * scale
+            dk_h = dot(ds, q[:, cols], 0, 0) * scale
+            dv[:, cols] = jnp.where(inside, dv_h, dv[:, cols].astype(f32)).astype(bf16)
+            tmp[:, cols] = jnp.where(inside, dq_h, tmp[:, cols])
+            tmp[:, cols2] = jnp.where(inside, dk_h, tmp[:, cols2])
+            return carry
+
+        lax.fori_loop(0, heads, one, 0, unroll=2)
+
+    def unrotate():
+        def body(s):
+            dq[s, :] = rope(tmp[s, halves[0]], s, True).astype(bf16)
+            dk[s, :] = rope(tmp[s, halves[1]], s, True).astype(bf16)
+
+        by_rows(16, body)
+
+    def grad_norm1():
+        widen(S.at[0], [(dq, WQ), (dk, WK), (dv, WV)])
+
+    def grad_in2():
+        weight_grad(IN2, hid, dr0[:, mcols])
+
+    def grad_token():
+        for c in halves:
+            S[1, :, c] = dot(dr0[:, mcols], W[IN2, c, :], 1, 1)
+
+    def grad_pre():
+        def body(s):
+            t = tmp[s, :]
+            sig = 1.0 / (1.0 + jnp.exp(-t))
+            grad = (S[1, s, :] + X[1, s, :]) * (sig * (1.0 + t * (1.0 - sig)))
+            nrm[s, :] = grad.astype(bf16)
+
+        by_rows(16, body)
+
+    def grad_values():
+        total = dot(nrm[...], PK[0], 1, 0) + dot(dr0[...], PK[1], 1, 0)
+        o_dval[...] = (total * keep_col[...]).T[0:patch, :]
+
+    def grad_pack():
+        @pl.when(m == 0)
+        def _():
+            for r in halves:
+                GP[r, :] = dot(nrm[:, r], inx[...], 0, 0).astype(bf16)
+
+        @pl.when(m == 1)
+        def _():
+            for r in halves:
+                total = dot(dr0[:, r], inx[...], 0, 0)
+                for i in range(2):
+                    pick = (gain_lane == 2 * patch + 1 + i).astype(bf16)
+                    total = total + dot(dgs[i, :, r], pick, 0, 0)
+                GP[r, :] = total.astype(bf16)
+
+    def write_small():
+        for i, c in enumerate(halves):
+            o_in2[:, c] = fin_in2[i]
+        tok_in = 2 * patch
+        one, two = fin_pack[0].T, fin_pack[1].T
+        o_in1[...] = one[0:tok_in]
+        o_b1[...] = one[tok_in : tok_in + 1]
+        o_res[...] = two[0:tok_in]
+        o_b2[...] = two[tok_in : tok_in + 1]
+        o_gattn[...] = two[tok_in + 1 : tok_in + 2]
+        o_gmlp[...] = two[tok_in + 2 : tok_in + 3]
+
+    barrier = pltpu.get_barrier_semaphore()
+    for dev in (XN, YN, SIB):
+        pl.semaphore_signal(barrier, inc=1, device_id=dev, device_id_type=MESH)
+    each_other_plane(
+        lambda zb: pl.semaphore_signal(barrier, inc=1, device_id=plane(zb), device_id_type=MESH)
+    )
+    order = (IN2, WQ, WK, WV, WOUT, WUP, WDOWN)
+    for w in order:
+        own_copy(w).start()
+    cot_copy = pltpu.make_async_copy(cot_hbm, cot, lsem.at[8])
+    cot_copy.start()
+
+    @pl.when(m == 0)
+    def _():
+        pack_block(PK.at[0, row_of(f)], w_in1, [b_in1])
+
+    @pl.when(m == 1)
+    def _():
+        pack_block(PK.at[1, row_of(f)], w_res, [b_in2, g_attn, g_mlp])
+
+    pl.semaphore_wait(barrier, 6)
+
+    ag_own(PACK)
+    ag_own(IN2)
+    ag_column(PACK)
+    ag_own(WQ)
+    ag_plane(PACK)
+    ag_own(WK)
+    ag_own(WDOWN)
+    prepare()
+    ag_own(WV)
+    ag_column(IN2)
+    ag_plane(IN2)
+    ag_last(PACK)
+    ag_column(WQ)
+    swap_start(0)
+    swap_wait(0)
+    token_hidden()
+    ag_last(IN2)
+    ag_own(WUP)
+    ag_own(WOUT)
+    ag_plane(WQ)
+    ag_column(WK)
+    token_out()
+    ag_column(WV)
+    ag_plane(WV)
+    ag_plane(WK)
+    swap_start(1)
+    swap_wait(1)
+    norm_first()
+    ag_last(WQ)
+    ag_column(WOUT)
+    ag_last(WV)
+    project(WQ, q)
+    ag_column(WUP)
+    ag_plane(WOUT)
+    ag_last(WK)
+    ag_plane(WUP)
+    project_v()
+    project(WK, k)
+    ag_column(WDOWN)
+    ag_last(WOUT)
+    attend()
+    attend_out()
+    swap_start(2)
+    ag_last(WUP)
+    swap_wait(2)
+    norm_second()
+    ag_plane(WDOWN)
+    feed_up()
+    grad_down()
+    rs_start(WDOWN)
+    ag_last(WDOWN)
+    feed_down()
+    grad_hidden()
+    grad_norm2()
+    swap_start(3)
+    swap_wait(3)
+    swap_start(4)
+    grad_up()
+    rs_start(WUP)
+    write_output()
+    swap_wait(4)
+    norm_grad2()
+    grad_out()
+    rs_turn(WDOWN)
+    grad_attended()
+    rs_start(WOUT)
+    attend_back()
+    unrotate()
+    weight_grad(WQ, nrm, dq[...])
+    grad_norm1()
+    pre_act()
+    rs_out(WDOWN)
+    rs_turn(WOUT)
+    swap_start(5)
+    rs_turn(WUP)
+    swap_wait(5)
+    rs_start(WQ)
+    norm_grad1()
+    rs_out(WOUT)
+    rs_turn(WQ)
+    weight_grad(WK, nrm, dk[...])
+    grad_token()
+    grad_in2()
+    weight_grad(WV, nrm, dv[...])
+    rs_start(WK)
+    rs_out(WUP)
+    rs_turn(WK)
+    swap_start(6)
+    rs_start(IN2)
+    swap_wait(6)
+    rs_out(WQ)
+    rs_out(WK)
+    rs_final(WUP)
+    grad_pre()
+    grad_pack()
+    rs_turn(IN2)
+    rs_start(PACK)
+    rs_final(WDOWN)
+    grad_values()
+    rs_start(WV)
+    rs_turn(PACK)
+    rs_out(IN2)
+    rs_final(WK)
+    rs_final(WOUT)
+    rs_turn(WV)
+    rs_final(IN2)
+    rs_out(PACK)
+    rs_final(WQ)
+    swap_start(7)
+    rs_final(PACK)
+    rs_out(WV)
+    swap_start(8)
+    swap_wait(7)
+    swap_wait(8)
+    rs_final(WV)
+    write_small()
+
+    def drain(ref, sem):
+        remote(ref, ref, sem, sem, XN).wait_send()
+
+    for w in (PACK,) + order:
+        ref = PK.at[m] if w == PACK else W.at[w]
+        drain(ref.at[pl.ds(0, (11 if w in PLANE_FIRST else 15) * blk)], ag_send.at[w])
+        if w in PLANE_FIRST:
+
+            @pl.when(inner)
+            def _():
+                drain(ref.at[pl.ds(0, 8 * blk)], ag_send.at[w])
+
+        if w == PACK:
+            ref = RP
+        elif w in Z_FIRST:
+            ref = RZ.at[Z_FIRST.index(w)]
+        else:
+            ref = R.at[CHAIN_LAST.index(w)]
+        drain(ref.at[pl.ds(0, 15)], rs_send.at[w])
+
+
+def pack_block(dst, matrix, vectors):
+    tok_in, blk = matrix.shape
+    parts = [matrix[...].astype(f32)] + [t[...].astype(f32) for t in vectors]
+    parts.append(jnp.zeros((PL - tok_in - len(vectors), blk), f32))
+    tall = jnp.concatenate(parts, 0)
+    wide = jnp.concatenate([tall, jnp.zeros((PL, PL - blk), f32)], 1)
+    dst[...] = wide.T[0:blk].astype(bf16)
+
+
+def copy_kernel(count, *refs):
+    sources, targets, held, sems = refs[:count], refs[count : 2 * count], refs[2 * count : -1], refs[-1]
+    inward = [pltpu.make_async_copy(sources[i], held[i], sems.at[0, i]) for i in range(count)]
+    outward = [pltpu.make_async_copy(held[i], targets[i], sems.at[1, i]) for i in range(count)]
+    for c in inward:
+        c.start()
+    for a, b in zip(inward, outward):
+        a.wait()
+        b.start()
+    for c in outward:
+        c.wait()
 
 
 def rotate(vectors, places):
@@ -35,7 +981,7 @@
     return jax.nn.gelu(up_rows, approximate=False)
 
 
-def on_device(
+def general_device(
     values,
     lengths,
     w_in1,
@@ -241,6 +1187,181 @@
     return (result, values_grad) + shares
 
 
+def fused_device(
+    values,
+    lengths,
+    w_in1,
+    b_in1,
+    w_in2,
+    b_in2,
+    w_res,
+    g_attn,
+    w_qkv,
+    w_out,
+    g_mlp,
+    w_up,
+    w_down,
+    cotangent,
+):
+    rows, width = cotangent.shape
+    half = w_out.shape[0]
+    blk = w_in2.shape[0]
+    patch = values.shape[1]
+    tok_in = w_in1.shape[0]
+    heads = half // HD
+    vmem = pl.BlockSpec(memory_space=pltpu.VMEM)
+    hbm = pl.BlockSpec(memory_space=pl.ANY)
+
+    def shape(*dims, dtype=f32):
+        return jax.ShapeDtypeStruct(dims, dtype)
+
+    out_shape = (
+        shape(rows, width, dtype=bf16),
+        shape(patch, rows),
+        shape(tok_in, blk),
+        shape(1, blk),
+        shape(blk, width),
+        shape(1, blk),
+        shape(tok_in, blk),
+        shape(1, blk),
+        shape(3, blk, half),
+        shape(blk, half),
+        shape(1, blk),
+        shape(blk, half),
+        shape(blk, half),
+    )
+    V = pltpu.VMEM
+    scratch = [
+        V((NW, width, half), bf16),
+        V((2, width, PL), bf16),
+        V((NW, width, half), bf16),
+        V((width, PL), bf16),
+        V((len(CHAIN_LAST), SLOTS, blk, half), bf16),
+        V((max(1, len(Z_FIRST)), Z_SLOTS, blk, half), bf16),
+        V((SLOTS, blk, PL), bf16),
+        V((2, rows, half), f32),
+        V((rows, width), f32),
+        V((2, rows, width), f32),
+        V((2, rows, width), f32),
+        V((rows, width), bf16),
+        V((rows, width), bf16),
+        V((rows, width), bf16),
+        V((rows, width), bf16),
+        V((rows, width), bf16),
+        V((rows, half), bf16),
+        V((rows, half), bf16),
+        V((rows, half), bf16),
+        V((heads, rows, rows), f32),
+        V((rows, half), bf16),
+        V((rows, half), f32),
+        V((rows, half), bf16),
+        V((rows, width), bf16),
+        V((rows, half), bf16),
+        V((rows, half), bf16),
+        V((rows, half), bf16),
+        V((rows, half), bf16),
+        V((rows, width), f32),
+        V((rows, width), bf16),
+        V((rows, half), f32),
+        V((rows, half), f32),
+        V((rows, rows), f32),
+        V((rows, PL), bf16),
+        V((2, 8, width), f32),
+        V((2, 16, width), bf16),
+        V((8, width), f32),
+        V((rows, PL), f32),
+        V((2, blk, half), f32),
+        V((2, blk, PL), f32),
+        pltpu.SemaphoreType.DMA((8,)),
+        pltpu.SemaphoreType.DMA((8, 16)),
+        pltpu.SemaphoreType.DMA((8,)),
+        pltpu.SemaphoreType.DMA((8, Z_SLOTS)),
+        pltpu.SemaphoreType.DMA((9,)),
+        pltpu.SemaphoreType.DMA((9,)),
+        pltpu.SemaphoreType.DMA((9,)),
+    ]
+    results = pl.pallas_call(
+        layer_kernel,
+        name="layer",
+        out_shape=out_shape,
+        in_specs=[pl.BlockSpec(memory_space=pltpu.SMEM)] + [vmem] * 7 + [hbm] * 6,
+        out_specs=(vmem,) * len(out_shape),
+        scratch_shapes=scratch,
+        compiler_params=pltpu.CompilerParams(
+            collective_id=0, has_side_effects=True, vmem_limit_bytes=VMEM_BYTES
+        ),
+    )(
+        lengths,
+        values.T,
+        w_in1,
+        w_res,
+        b_in1[None],
+        b_in2[None],
+        g_attn[None],
+        g_mlp[None],
+        w_in2,
+        jnp.transpose(w_qkv, (1, 0, 2)),
+        w_out.T,
+        w_up,
+        w_down.T,
+        cotangent,
+    )
+    (
+        out,
+        d_values,
+        d_in1,
+        d_b1,
+        d_in2,
+        d_b2,
+        d_res,
+        d_gattn,
+        d_qkv,
+        d_out,
+        d_gmlp,
+        d_up,
+        d_down,
+    ) = pl.pallas_call(
+        functools.partial(copy_kernel, len(out_shape)),
+        name="hand_over",
+        out_shape=out_shape,
+        in_specs=[hbm] * len(out_shape),
+        out_specs=(hbm,) * len(out_shape),
+        scratch_shapes=[V(s.shape, s.dtype) for s in out_shape]
+        + [pltpu.SemaphoreType.DMA((2, len(out_shape)))],
+    )(*results)
+    return (
+        out,
+        d_values.T,
+        d_in1,
+        d_b1[0],
+        d_in2,
+        d_b2[0],
+        d_res,
+        d_gattn[0],
+        jnp.transpose(d_qkv, (1, 0, 2)),
+        d_out.T,
+        d_gmlp[0],
+        d_up,
+        d_down.T,
+    )
+
+
+def on_device(*args):
+    blk, width = args[4].shape
+    half = args[9].shape[0]
+    shards = width // blk
+    series = args[1].shape[0]
+    fits = (
+        shards == 16
+        and 2 * half == width
+        and blk % 16 == 0
+        and half % 128 == 0
+        and args[0].shape[0] % 64 == 0
+        and series <= 8
+    )
+    return (fused_device if fits else general_device)(*args)
+
+
 def solution(mesh):
     in_specs = (
         P("fsdp", None),

time: 1260 us -> 223 us (0.18)
  waiting for transfers between devices: 879 us -> 0 us
  blocking collectives: 235 us -> 0 us
  Pallas kernels: 0 us -> 222 us
  matrix products: 57.3 us -> 0 us
  local copies, waits for them, and re-layouts: 43.2 us -> 0 us
  other arithmetic: 21.6 us -> 0 us
  between operations: 15.9 us -> 0.82 us
    reduce_scatter x5 -> x0, waiting for transfers between devices: 605 us -> none  [the longest x1 211 us: on_device(): lax.psum_scatter(grad_qkv, 'fsdp', scatter_dimension=0, tiled=True)]
    pallas_call x0 -> x2, Pallas kernels: none -> 222 us  [the longest x1 220 us: fused_device(): pl.pallas_call(layer_kernel, name='layer', out_shape=out_shape, in_specs=...]
    unnamed x2 -> x0, blocking collectives: 156 us -> none
    all_gather x5 -> x0, waiting for transfers between devices: 150 us -> none  [the longest x1 60.7 us: on_device(): lax.all_gather(w_up, 'fsdp', axis=0, tiled=True)]
    all_gather x2 -> x0, blocking collectives: 79 us -> none  [the longest x1 40.2 us: on_device(): lax.all_gather(w_res, 'fsdp', axis=1, tiled=True)]
    psum x4 -> x0, waiting for transfers between devices: 75.4 us -> none  [the longest x1 21.4 us: on_device(): lax.psum(jnp.dot(mlp_hidden, full_down, preferred_element_type=f32).astyp...]
    dot_general x25 -> x0, matrix products: 54.8 us -> none  [the longest x1 5.43 us: on_device(): jnp.einsum('td,tch->dch', normed, qkv_rows, preferred_element_type=f32)]
    unnamed x18 -> x0, waiting for transfers between devices: 49.2 us -> none
  transfers between devices with their start and end apart: 16 -> 0, of which waited for: 13 -> 0; matrix products, arithmetic and copies ran while one was open for 5% -> 0% of each run, Pallas kernels for 0% -> 0%
where the time goes in v2:
time: 223 us
  Pallas kernels  222 us (100%)
    pallas_call x1, Pallas kernels, fused_device(): pl.pallas_call(layer_kernel, name='layer', out_shape=out_shape, in_specs=...  220 us

profile of v2, /device:TPU:0, one launch (start us, length us, event | category | flops | bytes accessed | tf_op | source)
XLA Modules:
  0.0 223.2 jit_solution(13670366073319598110)
XLA Ops:
  0.7 219.7 %layer.1 = (bf16[256,1280]{1,0:T(8,128)(2,1)}, f32[32,256]{1,0:T(8,128)}, f32[64,80]{1,0:T(8,128)}, f32[1,80]{1,0:T(1,128)}, f32[80,1280]{1,0:T(8,128)}, /*index...) custom-call(s32[4]{0:T(128)} %lengths.1, ...), custom_call_target="tpu_custom_call" | custom-call | tf_op jit(solution)/shard_map/layer/pallas_call | solution.py:1283
  220.3 2.7 %hand_over.1 = (bf16[256,1280]{1,0:T(8,128)(2,1)}, f32[32,256]{1,0:T(8,128)}, f32[64,80]{1,0:T(8,128)}, f32[1,80]{1,0:T(1,128)}, f32[80,1280]{1,0:T(8,128)}, /*i...) custom-call(bf16[256,1280]{1,0:T(8,128)(2,1)} %get-tuple-element.39., ...), custom_call_target="tpu_custom_call" | custom-call | tf_op jit(solution)/shard_map/hand_over/pallas_call | solution.py:1323

commit v3 on v2

--- a/solution.py
+++ b/solution.py
@@ -17,8 +17,8 @@
 IN2, WQ, WK, WV, WOUT, WUP, WDOWN, PACK = range(8)
 NW = 7
 PL = 128
-PLANE_FIRST = ()
-Z_FIRST = ()
+PLANE_FIRST = (WUP,)
+Z_FIRST = (WUP,)
 CHAIN_LAST = tuple(w for w in range(NW) if w not in Z_FIRST)
 SLOT_A, SLOT_X, SLOT_Y, SLOT_V, SLOTS = 0, 4, 8, 12, 16
 Z_RELAY, Z_NEAR, Z_FAR, Z_A, Z_X, Z_Y, Z_SLOTS = 0, 8, 12, 16, 17, 18, 19
@@ -793,119 +793,120 @@
     pl.semaphore_wait(barrier, 6)
 
     ag_own(PACK)
+    ag_own(WQ)
+    ag_own(WK)
+    ag_own(WOUT)
     ag_own(IN2)
+    ag_own(WUP)
     ag_column(PACK)
-    ag_own(WQ)
+    ag_column(WQ)
+    ag_own(WV)
     ag_plane(PACK)
-    ag_own(WK)
+    ag_column(WK)
+    ag_last(PACK)
+    swap_start(0)
+    ag_plane(WQ)
+    prepare()
+    ag_plane(WK)
+    swap_wait(0)
+    ag_column(IN2)
+    token_hidden()
+    ag_plane(IN2)
     ag_own(WDOWN)
-    prepare()
-    ag_own(WV)
-    ag_column(IN2)
-    ag_plane(IN2)
-    ag_last(PACK)
-    ag_column(WQ)
-    swap_start(0)
-    swap_wait(0)
-    token_hidden()
+    ag_last(WK)
+    ag_plane(WUP)
+    ag_column(WV)
     ag_last(IN2)
-    ag_own(WUP)
-    ag_own(WOUT)
-    ag_plane(WQ)
-    ag_column(WK)
+    ag_column(WOUT)
     token_out()
-    ag_column(WV)
+    ag_last(WQ)
     ag_plane(WV)
-    ag_plane(WK)
     swap_start(1)
     swap_wait(1)
     norm_first()
-    ag_last(WQ)
-    ag_column(WOUT)
+    project(WK, k)
+    ag_plane(WOUT)
+    project(WQ, q)
+    ag_relay(WUP)
+    ag_column(WDOWN)
     ag_last(WV)
-    project(WQ, q)
-    ag_column(WUP)
-    ag_plane(WOUT)
-    ag_last(WK)
-    ag_plane(WUP)
     project_v()
-    project(WK, k)
-    ag_column(WDOWN)
+    attend()
     ag_last(WOUT)
-    attend()
     attend_out()
     swap_start(2)
-    ag_last(WUP)
+    ag_plane(WDOWN)
     swap_wait(2)
     norm_second()
-    ag_plane(WDOWN)
+    ag_last(WUP)
     feed_up()
+    ag_last(WDOWN)
     grad_down()
     rs_start(WDOWN)
-    ag_last(WDOWN)
     feed_down()
+    swap_start(3)
     grad_hidden()
     grad_norm2()
-    swap_start(3)
+    swap_start(4)
     swap_wait(3)
-    swap_start(4)
     grad_up()
     rs_start(WUP)
     write_output()
     swap_wait(4)
     norm_grad2()
     grad_out()
+    rs_start(WOUT)
     rs_turn(WDOWN)
     grad_attended()
-    rs_start(WOUT)
     attend_back()
     unrotate()
+    rs_turn(WOUT)
     weight_grad(WQ, nrm, dq[...])
+    weight_grad(WK, nrm, dk[...])
+    rs_start(WK)
+    rs_relay(WUP)
+    rs_out(WOUT)
     grad_norm1()
+    swap_start(5)
+    rs_start(WQ)
+    rs_turn(WQ)
+    rs_out(WDOWN)
+    swap_wait(5)
     pre_act()
-    rs_out(WDOWN)
-    rs_turn(WOUT)
-    swap_start(5)
-    rs_turn(WUP)
-    swap_wait(5)
-    rs_start(WQ)
     norm_grad1()
-    rs_out(WOUT)
-    rs_turn(WQ)
-    weight_grad(WK, nrm, dk[...])
+    rs_turn(WK)
+    rs_final(WOUT)
+    grad_in2()
+    rs_start(IN2)
     grad_token()
-    grad_in2()
+    swap_start(6)
+    swap_wait(6)
+    rs_out(WK)
+    rs_turn(IN2)
+    rs_out(WQ)
     weight_grad(WV, nrm, dv[...])
-    rs_start(WK)
-    rs_out(WUP)
-    rs_turn(WK)
-    swap_start(6)
-    rs_start(IN2)
-    swap_wait(6)
-    rs_out(WQ)
-    rs_out(WK)
-    rs_final(WUP)
+    rs_start(WV)
     grad_pre()
     grad_pack()
-    rs_turn(IN2)
     rs_start(PACK)
+    rs_out(IN2)
+    rs_final(WQ)
+    rs_turn(PACK)
+    rs_turn(WV)
+    grad_values()
+    rs_out(PACK)
+    rs_zsum(WUP)
+    rs_out(WV)
+    rs_final(IN2)
+    swap_start(7)
+    rs_turn(WUP)
+    rs_final(PACK)
+    rs_final(WK)
+    swap_wait(7)
+    swap_start(8)
     rs_final(WDOWN)
-    grad_values()
-    rs_start(WV)
-    rs_turn(PACK)
-    rs_out(IN2)
-    rs_final(WK)
-    rs_final(WOUT)
-    rs_turn(WV)
-    rs_final(IN2)
-    rs_out(PACK)
-    rs_final(WQ)
-    swap_start(7)
-    rs_final(PACK)
-    rs_out(WV)
-    swap_start(8)
-    swap_wait(7)
     swap_wait(8)
+    rs_final(WUP)
     rs_final(WV)
     write_small()
 

time: 223 us -> 202 us (0.906)
  Pallas kernels: 222 us -> 201 us
    pallas_call x1, Pallas kernels: 220 us -> 198 us  [fused_device(): pl.pallas_call(layer_kernel, name='layer', out_shape=out_shape, in_specs=...]
where the time goes in v3:
time: 202 us
  Pallas kernels  201 us (100%)
    pallas_call x1, Pallas kernels, fused_device(): pl.pallas_call(layer_kernel, name='layer', out_shape=out_shape, in_specs=...  198 us

profile of v3, /device:TPU:0, one launch (start us, length us, event | category | flops | bytes accessed | tf_op | source)
XLA Modules:
  0.0 201.8 jit_solution(13035443405150911135)
XLA Ops:
  0.7 198.3 %layer.1 = (bf16[256,1280]{1,0:T(8,128)(2,1)}, f32[32,256]{1,0:T(8,128)}, f32[64,80]{1,0:T(8,128)}, f32[1,80]{1,0:T(1,128)}, f32[80,1280]{1,0:T(8,128)}, /*index...) custom-call(s32[4]{0:T(128)} %lengths.1, ...), custom_call_target="tpu_custom_call" | custom-call | tf_op jit(solution)/shard_map/layer/pallas_call | solution.py:1284
  198.9 2.7 %hand_over.1 = (bf16[256,1280]{1,0:T(8,128)(2,1)}, f32[32,256]{1,0:T(8,128)}, f32[64,80]{1,0:T(8,128)}, f32[1,80]{1,0:T(1,128)}, f32[80,1280]{1,0:T(8,128)}, /*i...) custom-call(bf16[256,1280]{1,0:T(8,128)(2,1)} %get-tuple-element.39., ...), custom_call_target="tpu_custom_call" | custom-call | tf_op jit(solution)/shard_map/hand_over/pallas_call | solution.py:1324

commit v4 on v2

--- a/solution.py
+++ b/solution.py
@@ -14,12 +14,21 @@
 f32 = jnp.float32
 bf16 = jnp.bfloat16
 
-IN2, WQ, WK, WV, WOUT, WUP, WDOWN, PACK = range(8)
+IN2, WQ, WK, WV, WOUT, WUP, WDOWN, PACK, XTRA = range(9)
 NW = 7
 PL = 128
-PLANE_FIRST = ()
-Z_FIRST = ()
-CHAIN_LAST = tuple(w for w in range(NW) if w not in Z_FIRST)
+SPLIT, CUT = WQ, 384
+ITEMS = (PACK, IN2, WQ, WK, WV, WOUT, WUP, WDOWN) + (() if SPLIT is None else (XTRA,))
+PLANE_FIRST = (WUP, XTRA)
+Z_FIRST = (WUP, XTRA)
+
+
+def cols_of(w, half):
+    if SPLIT is None or w not in (SPLIT, XTRA):
+        return 0, PL if w == PACK else half
+    return (0, CUT) if w == SPLIT else (CUT, half)
+
+
 SLOT_A, SLOT_X, SLOT_Y, SLOT_V, SLOTS = 0, 4, 8, 12, 16
 Z_RELAY, Z_NEAR, Z_FAR, Z_A, Z_X, Z_Y, Z_SLOTS = 0, 8, 12, 16, 17, 18, 19
 
@@ -62,9 +71,7 @@
     PK,
     G,
     GP,
-    R,
-    RZ,
-    RP,
+    recv,
     R0,
     R1,
     S,
@@ -96,8 +103,11 @@
     dgs,
     accg,
     keep_col,
+    fin,
     fin_in2,
     fin_pack,
+    out_rows,
+    in2_rows,
     ag_send,
     ag_recv,
     rs_send,
@@ -105,6 +115,7 @@
     ex_send,
     ex_recv,
     lsem,
+    out_sem,
 ):
     rows, width = cot.shape
     half = W.shape[2]
@@ -139,9 +150,6 @@
         low = i + z_inner * swap
         return low + z_high * (3 - 2 * low)
 
-    def far(i):
-        return near(3 - i)
-
     def each_plane(order, body, start=0):
         def step(i, carry):
             body(order(i))
@@ -152,21 +160,29 @@
     def each_other_plane(body):
         each_plane(near, body, 1)
 
+    nearest = [near(jnp.int32(i)) for i in range(4)]
+
     def row_of(b):
         return pl.ds(pl.multiple_of(b * blk, 16), blk)
 
+    def whole(w):
+        return SPLIT if w == XTRA else w
+
+    def part(ref, w, *index):
+        low, high = cols_of(w, half)
+        return ref.at[(*index, slice(low, high))]
+
+    def w_rows(w, r):
+        return PK.at[m, r] if w == PACK else part(W, w, whole(w), r)
+
     def w_block(w, b):
-        return PK.at[m, row_of(b)] if w == PACK else W.at[w, row_of(b)]
+        return w_rows(w, row_of(b))
 
     def g_block(w, b):
-        return GP.at[row_of(b)] if w == PACK else G.at[w, row_of(b)]
+        return GP.at[row_of(b)] if w == PACK else part(G, w, whole(w), row_of(b))
 
     def r_block(w, s):
-        if w == PACK:
-            return RP.at[s]
-        if w in Z_FIRST:
-            return RZ.at[Z_FIRST.index(w), s]
-        return R.at[CHAIN_LAST.index(w), s]
+        return recv[w].at[s]
 
     def remote(src, dst, send, recv, dev):
         return pltpu.make_async_remote_copy(
@@ -187,61 +203,67 @@
     def own_copy(w):
         if w == IN2:
             src = in2.at[:, mcols]
-        elif w in (WQ, WK, WV):
-            src = qkv.at[w - WQ]
+        elif whole(w) in (WQ, WK, WV):
+            src = part(qkv, w, whole(w) - WQ, slice(None))
         else:
-            src = {WOUT: out_t, WUP: up, WDOWN: down_t}[w]
+            src = part({WOUT: out_t, WUP: up, WDOWN: down_t}[whole(w)], w, slice(None))
         return pltpu.make_async_copy(src, w_block(w, f), lsem.at[w])
 
-    def ag_own(w):
-        if w != PACK:
-            own_copy(w).wait()
+    def ag_ready(w):
+        own_copy(w).wait()
+
+    def ag_own_xy(w):
         ag_push(w, f, XN, YN)
+
+    def ag_own_z(w):
         if w in PLANE_FIRST:
             ag_push(w, f, plane(z_near), plane(z_far))
         else:
             each_other_plane(lambda zb: ag_push(w, f, plane(zb)))
 
-    def ag_column(w):
-        def body(zb):
-            b = 4 * zb + c0
-            ag_await(w, b)
-            ag_push(w, b, XN, YN)
-
-        each_other_plane(body)
-
-    def ag_pass(w, zb, even, *more):
+    def ag_column(w, i):
+        b = 4 * nearest[i] + c0
+        ag_await(w, b)
+        ag_push(w, b, XN, YN)
+
+    def ag_from_x(w, zb, even):
         ag_await(w, 4 * zb + cx)
 
         @pl.when(even)
         def _():
             ag_push(w, 4 * zb + cx, YN)
 
-        ag_push(w, 4 * zb + cx, *more)
+    def ag_from_y(w, zb, even):
         ag_await(w, 4 * zb + cy)
 
         @pl.when(jnp.logical_not(even))
         def _():
             ag_push(w, 4 * zb + cy, XN)
 
-        ag_push(w, 4 * zb + cy, *more)
-
-    def ag_plane(w):
-        if w in PLANE_FIRST:
-            to = (plane(z_near), plane(z_far))
-            ag_pass(w, z, z_even, *to)
-            ag_await(w, 4 * z + cd)
-            ag_push(w, 4 * z + cd, *to)
-        else:
-            each_plane(near, lambda zb: ag_pass(w, zb, lax.rem(zb, 2) == 0))
-
-    def ag_relay(w):
+    def ag_plane(w, i):
+        even = lax.rem(nearest[i], 2) == 0
+        ag_from_x(w, nearest[i], even)
+        ag_from_y(w, nearest[i], even)
+
+    def ag_first_x(w):
+        ag_from_x(w, z, z_even)
+        ag_push(w, 4 * z + cx, plane(z_near), plane(z_far))
+
+    def ag_first_y(w):
+        ag_from_y(w, z, z_even)
+        ag_push(w, 4 * z + cy, plane(z_near), plane(z_far))
+
+    def ag_first_d(w):
+        ag_await(w, 4 * z + cd)
+        ag_push(w, 4 * z + cd, plane(z_near), plane(z_far))
+
+    def ag_relay(w, i):
         @pl.when(inner)
         def _():
-            for zb in (3 - z, 3 * (1 - z_high)):
-                for c in (c0, cx, cy, cd):
-                    ag_await(w, 4 * zb + c)
-                    ag_push(w, 4 * zb + c, plane(3 * z_high))
+            zb = (3 - z, 3 * (1 - z_high))[i]
+            for c in (c0, cx, cy, cd):
+                ag_await(w, 4 * zb + c)
+                ag_push(w, 4 * zb + c, plane(3 * z_high))
 
     def ag_last(w):
         if w in PLANE_FIRST:
@@ -256,16 +278,18 @@
         else:
             each_plane(near, lambda zb: ag_await(w, 4 * zb + cd))
 
-    final_of = {
-        IN2: lambda: fin_in2.at[m],
-        WQ: lambda: o_qkv.at[0],
-        WK: lambda: o_qkv.at[1],
-        WV: lambda: o_qkv.at[2],
-        WOUT: lambda: o_wout,
-        WUP: lambda: o_up,
-        WDOWN: lambda: o_down,
-        PACK: lambda: fin_pack.at[m],
-    }
+    def final_of(w):
+        if w == PACK:
+            return fin_pack.at[m]
+        if w == IN2:
+            return fin_in2.at[m]
+        return part(fin, w, whole(w) - WQ, slice(None))
+
+    targets = [o_qkv.at[0], o_qkv.at[1], o_qkv.at[2], o_wout, o_up, o_down]
+
+    def hand_out(w):
+        target = part(targets[whole(w) - WQ], w, slice(None))
+        return pltpu.make_async_copy(final_of(w), target, out_sem.at[w])
 
     def rs_push(w, src, slot, dev):
         remote(src, r_block(w, slot), rs_send.at[w], rs_recv.at[w, slot], dev).start()
@@ -280,35 +304,19 @@
     def sum3(a, b, c):
         return a[...].astype(f32) + b[...].astype(f32) + c[...].astype(f32)
 
-    def rs_start(w):
-        if w in Z_FIRST:
-            cs = (cd, cx, cy, c0)
-
-            @pl.when(jnp.logical_not(inner))
-            def _():
-                for zb in (3 - z, z_far):
-                    for c in cs:
-                        slot = Z_RELAY + 4 * lax.rem(zb, 2) + c
-                        rs_push(w, g_block(w, 4 * zb + c), slot, plane(1 + z_high))
-
-            for c in cs:
-                rs_push(w, g_block(w, 4 * z_near + c), Z_NEAR + c, plane(z_near))
-            return
-
-        def body(zb):
-            even = lax.rem(zb, 2) == 0
-
-            @pl.when(even)
-            def _():
-                rs_push(w, g_block(w, 4 * zb + cd), SLOT_A + zb, YN)
-                rs_push(w, g_block(w, 4 * zb + cy), SLOT_Y + zb, YN)
-
-            @pl.when(jnp.logical_not(even))
-            def _():
-                rs_push(w, g_block(w, 4 * zb + cd), SLOT_A + zb, XN)
-                rs_push(w, g_block(w, 4 * zb + cx), SLOT_X + zb, XN)
-
-        each_plane(far, body)
+    def rs_start(w, i):
+        zb = nearest[3 - i]
+        even = lax.rem(zb, 2) == 0
+
+        @pl.when(even)
+        def _():
+            rs_push(w, g_block(w, 4 * zb + cd), SLOT_A + zb, YN)
+            rs_push(w, g_block(w, 4 * zb + cy), SLOT_Y + zb, YN)
+
+        @pl.when(jnp.logical_not(even))
+        def _():
+            rs_push(w, g_block(w, 4 * zb + cd), SLOT_A + zb, XN)
+            rs_push(w, g_block(w, 4 * zb + cx), SLOT_X + zb, XN)
 
     def turn(w, slot_a, even, own_x, own_y, slot_x, slot_y):
         rs_await(w, slot_a)
@@ -324,92 +332,84 @@
             add_to(ref, own_y)
             rs_push(w, ref, slot_y, YN)
 
-    def rs_turn(w):
-        if w in Z_FIRST:
-            turn(w, Z_A, z_even, r_block(w, Z_NEAR + cx), r_block(w, Z_NEAR + cy), Z_X, Z_Y)
-            return
-        each_plane(
-            far,
-            lambda zb: turn(
-                w,
-                SLOT_A + zb,
-                lax.rem(zb, 2) == 0,
-                g_block(w, 4 * zb + cx),
-                g_block(w, 4 * zb + cy),
-                SLOT_X + zb,
-                SLOT_Y + zb,
-            ),
-        )
-
-    def rs_relay(w):
+    def rs_turn(w, i):
+        zb = nearest[3 - i]
+        own_x, own_y = g_block(w, 4 * zb + cx), g_block(w, 4 * zb + cy)
+        turn(w, SLOT_A + zb, lax.rem(zb, 2) == 0, own_x, own_y, SLOT_X + zb, SLOT_Y + zb)
+
+    def rs_out(w, i):
+        zb = nearest[i]
+        rs_await(w, SLOT_X + zb)
+        rs_await(w, SLOT_Y + zb)
+        ref = r_block(w, SLOT_X + zb)
+        total = sum3(g_block(w, 4 * zb + c0), ref, r_block(w, SLOT_Y + zb))
+        if i == 0:
+            final_of(w)[...] = total
+        else:
+            ref[...] = total.astype(bf16)
+            rs_push(w, ref, SLOT_V + z, plane(zb))
+
+    def rs_first_far(w, i):
+        @pl.when(jnp.logical_not(inner))
+        def _():
+            zb = (3 - z, z_far)[i]
+            for c in (cd, cx, cy, c0):
+                slot = Z_RELAY + 4 * lax.rem(zb, 2) + c
+                rs_push(w, g_block(w, 4 * zb + c), slot, plane(1 + z_high))
+
+    def rs_first_near(w):
+        for c in (cd, cx, cy, c0):
+            rs_push(w, g_block(w, 4 * z_near + c), Z_NEAR + c, plane(z_near))
+
+    def rs_relay(w, i):
         @pl.when(inner)
         def _():
-            for zb in (3 * (1 - z_high), z_far):
-                for c in (cd, cx, cy, c0):
-                    slot = Z_RELAY + 4 * lax.rem(zb, 2) + c
-                    rs_await(w, slot)
-                    ref = r_block(w, slot)
-                    add_to(ref, g_block(w, 4 * zb + c))
-                    rs_push(w, ref, Z_FAR + c, plane(zb))
-
-    def rs_zsum(w):
-        for c in (cd, cx, cy, c0):
-            rs_await(w, Z_NEAR + c)
-            rs_await(w, Z_FAR + c)
-            ref = r_block(w, Z_NEAR + c)
-            total = sum3(ref, r_block(w, Z_FAR + c), g_block(w, 4 * z + c))
-            if c is c0:
-                final_of[w]()[...] = total
-            else:
-                ref[...] = total.astype(bf16)
-            if c is cd:
-
-                @pl.when(z_even)
-                def _():
-                    rs_push(w, ref, Z_A, YN)
-
-                @pl.when(jnp.logical_not(z_even))
-                def _():
-                    rs_push(w, ref, Z_A, XN)
-
-            if c is cx:
-
-                @pl.when(jnp.logical_not(z_even))
-                def _():
-                    rs_push(w, ref, Z_X, XN)
-
-            if c is cy:
-
-                @pl.when(z_even)
-                def _():
-                    rs_push(w, ref, Z_Y, YN)
-
-    def plane_sum(w, zb):
-        rs_await(w, SLOT_X + zb)
-        rs_await(w, SLOT_Y + zb)
-        return sum3(g_block(w, 4 * zb + c0), r_block(w, SLOT_X + zb), r_block(w, SLOT_Y + zb))
-
-    def rs_out(w):
-        def body(zb):
-            ref = r_block(w, SLOT_X + zb)
-            ref[...] = plane_sum(w, zb).astype(bf16)
-            rs_push(w, ref, SLOT_V + z, plane(zb))
-
-        each_other_plane(body)
-        final_of[w]()[...] = plane_sum(w, z)
+            zb = (3 * (1 - z_high), z_far)[i]
+            for c in (cd, cx, cy, c0):
+                slot = Z_RELAY + 4 * lax.rem(zb, 2) + c
+                rs_await(w, slot)
+                ref = r_block(w, slot)
+                add_to(ref, g_block(w, 4 * zb + c))
+                rs_push(w, ref, Z_FAR + c, plane(zb))
+
+    def rs_zsum(w, i):
+        c = (cd, cx, cy, c0)[i]
+        rs_await(w, Z_NEAR + c)
+        rs_await(w, Z_FAR + c)
+        ref = r_block(w, Z_NEAR + c)
+        total = sum3(ref, r_block(w, Z_FAR + c), g_block(w, 4 * z + c))
+        if i == 3:
+            final_of(w)[...] = total
+            return
+        ref[...] = total.astype(bf16)
+        if i in (0, 2):
+
+            @pl.when(z_even)
+            def _():
+                rs_push(w, ref, Z_A if i == 0 else Z_Y, YN)
+
+        if i in (0, 1):
+
+            @pl.when(jnp.logical_not(z_even))
+            def _():
+                rs_push(w, ref, Z_A if i == 0 else Z_X, XN)
+
+    def rs_first_turn(w):
+        turn(w, Z_A, z_even, r_block(w, Z_NEAR + cx), r_block(w, Z_NEAR + cy), Z_X, Z_Y)
 
     def rs_final(w):
-        final = final_of[w]()
+        final = final_of(w)
         if w in Z_FIRST:
             rs_await(w, Z_X)
             rs_await(w, Z_Y)
             final[...] = sum3(final, r_block(w, Z_X), r_block(w, Z_Y))
-            return
-
-        for i in (1, 2, 3):
-            rs_await(w, SLOT_V + near(jnp.int32(i)))
-        parts = [r_block(w, SLOT_V + near(jnp.int32(i)))[...].astype(f32) for i in (1, 2, 3)]
-        final[...] = final[...] + (parts[0] + parts[1] + parts[2])
+        else:
+            for i in (1, 2, 3):
+                rs_await(w, SLOT_V + nearest[i])
+            parts = [r_block(w, SLOT_V + nearest[i])[...].astype(f32) for i in (1, 2, 3)]
+            final[...] = final[...] + (parts[0] + parts[1] + parts[2])
+        if w not in (IN2, PACK):
+            hand_out(w).start()
 
     def exchange(i):
         src, dst = {
@@ -630,11 +630,15 @@
     def grad_norm2():
         widen(S.at[1], [(dup, WUP)])
 
+    out_copy = pltpu.make_async_copy(out_rows, o_out, out_sem.at[PACK])
+    in2_copy = pltpu.make_async_copy(in2_rows, o_in2, out_sem.at[IN2])
+
     def write_output():
         def body(s):
-            o_out[s, :] = (R1[s, :] + (SB[s, :].astype(f32) + XB[s, :].astype(f32))).astype(bf16)
+            out_rows[s, :] = (R1[s, :] + (SB[s, :].astype(f32) + XB[s, :].astype(f32))).astype(bf16)
 
         by_rows(16, body)
+        out_copy.start()
 
     def norm_grad(load, i_part, gain, base, out, keep_sum):
         def body(i, carry):
@@ -758,9 +762,12 @@
                     total = total + dot(dgs[i, :, r], pick, 0, 0)
                 GP[r, :] = total.astype(bf16)
 
+    def write_in2():
+        for i, c in enumerate(halves):
+            in2_rows[:, c] = fin_in2[i]
+        in2_copy.start()
+
     def write_small():
-        for i, c in enumerate(halves):
-            o_in2[:, c] = fin_in2[i]
         tok_in = 2 * patch
         one, two = fin_pack[0].T, fin_pack[1].T
         o_in1[...] = one[0:tok_in]
@@ -776,10 +783,10 @@
     each_other_plane(
         lambda zb: pl.semaphore_signal(barrier, inc=1, device_id=plane(zb), device_id_type=MESH)
     )
-    order = (IN2, WQ, WK, WV, WOUT, WUP, WDOWN)
+    order = ITEMS[1:]
     for w in order:
         own_copy(w).start()
-    cot_copy = pltpu.make_async_copy(cot_hbm, cot, lsem.at[8])
+    cot_copy = pltpu.make_async_copy(cot_hbm, cot, lsem.at[PACK])
     cot_copy.start()
 
     @pl.when(m == 0)
@@ -792,142 +799,285 @@
 
     pl.semaphore_wait(barrier, 6)
 
-    ag_own(PACK)
-    ag_own(IN2)
-    ag_column(PACK)
-    ag_own(WQ)
-    ag_plane(PACK)
-    ag_own(WK)
-    ag_own(WDOWN)
+    ag_own_z(PACK)
+    ag_ready(WV)
+    ag_own_xy(WV)
+    ag_ready(WQ)
+    ag_own_z(WQ)
+    ag_own_xy(PACK)
+    ag_ready(IN2)
+    ag_own_z(IN2)
+    ag_column(PACK, 1)
+    ag_ready(WK)
+    ag_own_xy(WK)
+    ag_ready(XTRA)
+    ag_own_z(XTRA)
+    ag_column(WQ, 1)
+    ag_own_xy(XTRA)
+    ag_column(WQ, 2)
+    ag_plane(PACK, 0)
+    ag_column(PACK, 3)
+    ag_column(WQ, 3)
+    ag_first_y(XTRA)
+    ag_column(IN2, 1)
+    ag_plane(PACK, 3)
+    ag_column(PACK, 2)
+    ag_own_z(WK)
+    ag_ready(WUP)
+    ag_own_xy(WUP)
+    ag_column(IN2, 3)
+    ag_column(IN2, 2)
+    ag_ready(WDOWN)
+    ag_own_xy(WDOWN)
+    ag_ready(WOUT)
+    ag_own_z(WOUT)
+    ag_own_xy(WOUT)
+    ag_column(WK, 1)
     prepare()
-    ag_own(WV)
-    ag_column(IN2)
-    ag_plane(IN2)
+    ag_plane(IN2, 1)
+    ag_plane(PACK, 1)
+    ag_plane(PACK, 2)
+    ag_first_x(XTRA)
+    ag_column(WK, 2)
+    ag_plane(IN2, 3)
     ag_last(PACK)
-    ag_column(WQ)
+    ag_column(WK, 3)
+    ag_plane(WK, 0)
+    ag_own_xy(IN2)
+    ag_plane(IN2, 2)
+    ag_own_xy(WQ)
+    ag_plane(WQ, 2)
+    ag_first_d(XTRA)
+    ag_plane(WK, 2)
+    ag_plane(WQ, 1)
     swap_start(0)
+    ag_plane(WOUT, 0)
+    ag_plane(IN2, 0)
+    ag_column(WOUT, 1)
+    ag_relay(XTRA, 0)
+    ag_own_z(WV)
+    ag_plane(WQ, 3)
+    ag_plane(WK, 1)
+    ag_plane(WK, 3)
+    ag_relay(XTRA, 1)
+    ag_own_z(WDOWN)
+    ag_column(WV, 1)
+    ag_column(WOUT, 2)
+    ag_plane(WV, 1)
+    ag_first_x(WUP)
+    ag_first_y(WUP)
+    ag_plane(WQ, 0)
+    ag_column(WV, 3)
+    ag_column(WV, 2)
+    ag_own_z(WUP)
+    ag_last(WK)
+    ag_plane(WOUT, 2)
     swap_wait(0)
     token_hidden()
+    ag_plane(WV, 0)
+    ag_first_d(WUP)
+    ag_plane(WOUT, 1)
     ag_last(IN2)
-    ag_own(WUP)
-    ag_own(WOUT)
-    ag_plane(WQ)
-    ag_column(WK)
     token_out()
-    ag_column(WV)
-    ag_plane(WV)
-    ag_plane(WK)
     swap_start(1)
+    ag_last(XTRA)
     swap_wait(1)
+    ag_last(WQ)
+    ag_column(WOUT, 3)
     norm_first()
-    ag_last(WQ)
-    ag_column(WOUT)
+    ag_plane(WV, 3)
+    ag_plane(WV, 2)
+    project(WK, k)
+    ag_column(WDOWN, 3)
+    project(WQ, q)
+    ag_plane(WOUT, 3)
+    ag_relay(WUP, 0)
+    ag_column(WDOWN, 2)
+    ag_column(WDOWN, 1)
+    ag_plane(WDOWN, 0)
     ag_last(WV)
-    project(WQ, q)
-    ag_column(WUP)
-    ag_plane(WOUT)
-    ag_last(WK)
-    ag_plane(WUP)
     project_v()
-    project(WK, k)
-    ag_column(WDOWN)
+    attend()
     ag_last(WOUT)
-    attend()
     attend_out()
     swap_start(2)
-    ag_last(WUP)
+    ag_plane(WDOWN, 3)
+    ag_plane(WDOWN, 2)
+    ag_relay(WUP, 1)
+    ag_plane(WDOWN, 1)
     swap_wait(2)
     norm_second()
-    ag_plane(WDOWN)
+    ag_last(WUP)
     feed_up()
     grad_down()
-    rs_start(WDOWN)
+    rs_start(WDOWN, 0)
+    rs_start(WDOWN, 1)
     ag_last(WDOWN)
+    grad_hidden()
     feed_down()
-    grad_hidden()
+    swap_start(3)
+    grad_up()
+    rs_first_far(WUP, 0)
     grad_norm2()
-    swap_start(3)
+    swap_start(4)
+    rs_start(WDOWN, 3)
+    rs_turn(WDOWN, 0)
+    rs_first_far(WUP, 1)
+    rs_turn(WDOWN, 1)
     swap_wait(3)
-    swap_start(4)
-    grad_up()
-    rs_start(WUP)
     write_output()
+    rs_first_near(WUP)
+    rs_start(WDOWN, 2)
     swap_wait(4)
     norm_grad2()
     grad_out()
-    rs_turn(WDOWN)
     grad_attended()
-    rs_start(WOUT)
+    rs_start(WOUT, 1)
+    rs_start(WOUT, 0)
     attend_back()
+    rs_start(WOUT, 3)
+    weight_grad(WV, nrm, dv[...])
+    rs_start(WV, 1)
+    rs_start(WV, 2)
     unrotate()
+    rs_relay(WUP, 0)
+    weight_grad(WK, nrm, dk[...])
+    rs_turn(WOUT, 1)
+    rs_start(WV, 0)
+    rs_start(WK, 1)
+    grad_norm1()
+    rs_relay(WUP, 1)
+    swap_start(5)
     weight_grad(WQ, nrm, dq[...])
-    grad_norm1()
+    rs_start(WK, 3)
     pre_act()
-    rs_out(WDOWN)
-    rs_turn(WOUT)
-    swap_start(5)
-    rs_turn(WUP)
+    rs_turn(WV, 0)
+    rs_out(WDOWN, 3)
+    rs_out(WOUT, 2)
+    rs_start(WK, 0)
     swap_wait(5)
-    rs_start(WQ)
     norm_grad1()
-    rs_out(WOUT)
-    rs_turn(WQ)
-    weight_grad(WK, nrm, dk[...])
+    rs_turn(WV, 1)
+    rs_start(WOUT, 2)
+    rs_turn(WV, 2)
     grad_token()
     grad_in2()
-    weight_grad(WV, nrm, dv[...])
-    rs_start(WK)
-    rs_out(WUP)
-    rs_turn(WK)
+    rs_first_far(XTRA, 0)
+    rs_start(IN2, 2)
+    rs_turn(WK, 1)
     swap_start(6)
-    rs_start(IN2)
+    rs_start(IN2, 3)
+    rs_start(WQ, 2)
     swap_wait(6)
-    rs_out(WQ)
-    rs_out(WK)
+    rs_out(WDOWN, 2)
+    grad_pre()
+    rs_out(WV, 3)
+    rs_turn(WOUT, 2)
+    rs_first_near(XTRA)
+    rs_start(IN2, 1)
+    rs_out(WV, 2)
+    grad_pack()
+    rs_first_far(XTRA, 1)
+    rs_out(WV, 1)
+    rs_turn(WDOWN, 2)
+    rs_start(IN2, 0)
+    rs_turn(IN2, 1)
+    rs_turn(WK, 0)
+    rs_turn(WK, 3)
+    rs_start(WV, 3)
+    rs_relay(XTRA, 0)
+    rs_start(PACK, 3)
+    rs_turn(IN2, 3)
+    rs_out(WK, 3)
+    rs_turn(IN2, 0)
+    rs_start(PACK, 1)
+    rs_start(PACK, 2)
+    rs_start(PACK, 0)
+    rs_out(WOUT, 1)
+    rs_relay(XTRA, 1)
+    rs_turn(WOUT, 0)
+    rs_out(IN2, 2)
+    rs_turn(IN2, 2)
+    rs_turn(WOUT, 3)
+    rs_out(WDOWN, 1)
+    rs_turn(WV, 3)
+    rs_zsum(XTRA, 0)
+    rs_turn(PACK, 0)
+    rs_turn(PACK, 2)
+    rs_start(WQ, 1)
+    rs_turn(PACK, 3)
+    rs_out(IN2, 3)
+    rs_turn(WDOWN, 3)
+    rs_out(IN2, 1)
+    rs_turn(PACK, 1)
+    rs_start(WK, 2)
+    rs_turn(WQ, 2)
+    rs_zsum(XTRA, 3)
+    rs_turn(WQ, 1)
+    rs_start(WQ, 3)
+    rs_out(WOUT, 3)
+    rs_zsum(WUP, 3)
+    rs_out(WV, 0)
+    rs_out(WK, 2)
+    rs_out(WOUT, 0)
+    rs_turn(WK, 2)
+    rs_out(IN2, 0)
+    rs_out(PACK, 0)
+    rs_out(WQ, 1)
+    rs_out(PACK, 3)
+    rs_start(WQ, 0)
+    rs_final(IN2)
+    rs_final(WV)
+    rs_zsum(WUP, 0)
+    rs_out(PACK, 2)
+    rs_turn(WQ, 3)
+    rs_out(PACK, 1)
+    rs_final(WOUT)
+    rs_turn(WQ, 0)
+    swap_start(7)
+    rs_out(WK, 0)
+    rs_zsum(WUP, 1)
+    rs_out(WQ, 2)
+    rs_zsum(WUP, 2)
+    rs_out(WDOWN, 0)
+    rs_out(WK, 1)
+    rs_first_turn(WUP)
+    rs_zsum(XTRA, 1)
+    rs_out(WQ, 3)
+    rs_zsum(XTRA, 2)
+    rs_first_turn(XTRA)
+    rs_final(PACK)
+    swap_start(8)
+    rs_final(WK)
+    rs_final(WDOWN)
+    swap_wait(7)
+    write_in2()
+    rs_out(WQ, 0)
+    rs_final(XTRA)
+    grad_values()
     rs_final(WUP)
-    grad_pre()
-    grad_pack()
-    rs_turn(IN2)
-    rs_start(PACK)
-    rs_final(WDOWN)
-    grad_values()
-    rs_start(WV)
-    rs_turn(PACK)
-    rs_out(IN2)
-    rs_final(WK)
-    rs_final(WOUT)
-    rs_turn(WV)
-    rs_final(IN2)
-    rs_out(PACK)
     rs_final(WQ)
-    swap_start(7)
-    rs_final(PACK)
-    rs_out(WV)
-    swap_start(8)
-    swap_wait(7)
     swap_wait(8)
-    rs_final(WV)
     write_small()
+
+    for w in ITEMS:
+        if w not in (IN2, PACK):
+            hand_out(w).wait()
+    out_copy.wait()
+    in2_copy.wait()
 
     def drain(ref, sem):
         remote(ref, ref, sem, sem, XN).wait_send()
 
-    for w in (PACK,) + order:
-        ref = PK.at[m] if w == PACK else W.at[w]
-        drain(ref.at[pl.ds(0, (11 if w in PLANE_FIRST else 15) * blk)], ag_send.at[w])
+    for w in ITEMS:
+        drain(w_rows(w, pl.ds(0, (11 if w in PLANE_FIRST else 15) * blk)), ag_send.at[w])
         if w in PLANE_FIRST:
 
             @pl.when(inner)
             def _():
-                drain(ref.at[pl.ds(0, 8 * blk)], ag_send.at[w])
-
-        if w == PACK:
-            ref = RP
-        elif w in Z_FIRST:
-            ref = RZ.at[Z_FIRST.index(w)]
-        else:
-            ref = R.at[CHAIN_LAST.index(w)]
-        drain(ref.at[pl.ds(0, 15)], rs_send.at[w])
+                drain(w_rows(w, pl.ds(0, 8 * blk)), ag_send.at[w])
+
+        drain(recv[w].at[pl.ds(0, 15)], rs_send.at[w])
 
 
 def pack_block(dst, matrix, vectors):
@@ -1236,9 +1386,10 @@
         V((2, width, PL), bf16),
         V((NW, width, half), bf16),
         V((width, PL), bf16),
-        V((len(CHAIN_LAST), SLOTS, blk, half), bf16),
-        V((max(1, len(Z_FIRST)), Z_SLOTS, blk, half), bf16),
-        V((SLOTS, blk, PL), bf16),
+        {
+            w: V((Z_SLOTS if w in Z_FIRST else SLOTS, blk, cols_of(w, half)[1] - cols_of(w, half)[0]), bf16)
+            for w in ITEMS
+        },
         V((2, rows, half), f32),
         V((rows, width), f32),
         V((2, rows, width), f32),
@@ -1270,12 +1421,16 @@
         V((2, 16, width), bf16),
         V((8, width), f32),
         V((rows, PL), f32),
+        V((NW - 1, blk, half), f32),
         V((2, blk, half), f32),
         V((2, blk, PL), f32),
-        pltpu.SemaphoreType.DMA((8,)),
-        pltpu.SemaphoreType.DMA((8, 16)),
-        pltpu.SemaphoreType.DMA((8,)),
-        pltpu.SemaphoreType.DMA((8, Z_SLOTS)),
+        V((rows, width), bf16),
+        V((blk, width), f32),
+        pltpu.SemaphoreType.DMA((9,)),
+        pltpu.SemaphoreType.DMA((9, 16)),
+        pltpu.SemaphoreType.DMA((9,)),
+        pltpu.SemaphoreType.DMA((9, Z_SLOTS)),
+        pltpu.SemaphoreType.DMA((9,)),
         pltpu.SemaphoreType.DMA((9,)),
         pltpu.SemaphoreType.DMA((9,)),
         pltpu.SemaphoreType.DMA((9,)),
@@ -1285,7 +1440,7 @@
         name="layer",
         out_shape=out_shape,
         in_specs=[pl.BlockSpec(memory_space=pltpu.SMEM)] + [vmem] * 7 + [hbm] * 6,
-        out_specs=(vmem,) * len(out_shape),
+        out_specs=(hbm,) + (vmem,) * 3 + (hbm,) + (vmem,) * 3 + (hbm,) * 2 + (vmem,) + (hbm,) * 2,
         scratch_shapes=scratch,
         compiler_params=pltpu.CompilerParams(
             collective_id=0, has_side_effects=True, vmem_limit_bytes=VMEM_BYTES

time: 223 us -> 198 us (0.89)
  Pallas kernels: 222 us -> 197 us
    pallas_call x1, Pallas kernels: 220 us -> 194 us  [fused_device(): pl.pallas_call(layer_kernel, name='layer', out_shape=out_shape, in_specs=...]
where the time goes in v4:
time: 198 us; the launch traced here: 197 us
  Pallas kernels  197 us (99%)
    pallas_call x1, Pallas kernels, fused_device(): pl.pallas_call(layer_kernel, name='layer', out_shape=out_shape, in_specs=...  194 us

profile of v4, /device:TPU:0, one launch (start us, length us, event | category | flops | bytes accessed | tf_op | source)
XLA Modules:
  0.0 197.3 jit_solution(5735069975652237798)
XLA Ops:
  0.7 193.8 %layer.1 = (bf16[256,1280]{1,0:T(8,128)(2,1)}, f32[32,256]{1,0:T(8,128)}, f32[64,80]{1,0:T(8,128)}, f32[1,80]{1,0:T(1,128)}, f32[80,1280]{1,0:T(8,128)}, /*index...) custom-call(s32[4]{0:T(128)} %lengths.1, ...), custom_call_target="tpu_custom_call" | custom-call | tf_op jit(solution)/shard_map/layer/pallas_call | solution.py:1438
  194.4 2.7 %hand_over.1 = (bf16[256,1280]{1,0:T(8,128)(2,1)}, f32[32,256]{1,0:T(8,128)}, f32[64,80]{1,0:T(8,128)}, f32[1,80]{1,0:T(1,128)}, f32[80,1280]{1,0:T(8,128)}, /*i...) custom-call(bf16[256,1280]{1,0:T(8,128)(2,1)} %get-tuple-element.39., ...), custom_call_target="tpu_custom_call" | custom-call | tf_op jit(solution)/shard_map/hand_over/pallas_call | solution.py:1478

commit v5 on v4

--- a/solution.py
+++ b/solution.py
@@ -40,14 +40,7 @@
 
 
 def layer_kernel(
-    lengths,
-    values_t,
-    w_in1,
-    w_res,
-    b_in1,
-    b_in2,
-    g_attn,
-    g_mlp,
+    small_hbm,
     in2,
     qkv,
     out_t,
@@ -67,6 +60,7 @@
     o_gmlp,
     o_up,
     o_down,
+    small,
     W,
     PK,
     G,
@@ -116,7 +110,9 @@
     ex_recv,
     lsem,
     out_sem,
+    small_sem,
 ):
+    lengths, values_t, w_in1, w_res, b_in1, b_in2, g_attn, g_mlp = small
     rows, width = cot.shape
     half = W.shape[2]
     blk = in2.shape[0]
@@ -141,6 +137,7 @@
     z_near = z + 1 - 2 * lax.rem(z, 2)
     z_far = 2 - z_high
     z_even = lax.rem(z, 2) == 0
+    z_odd = jnp.logical_not(z_even)
 
     def plane(zb):
         return (4 * zb + c0, m)
@@ -245,12 +242,15 @@
         ag_from_x(w, nearest[i], even)
         ag_from_y(w, nearest[i], even)
 
+    def turns_y(w):
+        return z_odd if w in (XTRA, PACK) else z_even
+
     def ag_first_x(w):
-        ag_from_x(w, z, z_even)
+        ag_from_x(w, z, turns_y(w))
         ag_push(w, 4 * z + cx, plane(z_near), plane(z_far))
 
     def ag_first_y(w):
-        ag_from_y(w, z, z_even)
+        ag_from_y(w, z, turns_y(w))
         ag_push(w, 4 * z + cy, plane(z_near), plane(z_far))
 
     def ag_first_d(w):
@@ -384,18 +384,18 @@
         ref[...] = total.astype(bf16)
         if i in (0, 2):
 
+            @pl.when(z_odd)
+            def _():
+                rs_push(w, ref, Z_A if i == 0 else Z_Y, YN)
+
+        if i in (0, 1):
+
             @pl.when(z_even)
             def _():
-                rs_push(w, ref, Z_A if i == 0 else Z_Y, YN)
-
-        if i in (0, 1):
-
-            @pl.when(jnp.logical_not(z_even))
-            def _():
                 rs_push(w, ref, Z_A if i == 0 else Z_X, XN)
 
     def rs_first_turn(w):
-        turn(w, Z_A, z_even, r_block(w, Z_NEAR + cx), r_block(w, Z_NEAR + cy), Z_X, Z_Y)
+        turn(w, Z_A, z_odd, r_block(w, Z_NEAR + cx), r_block(w, Z_NEAR + cy), Z_X, Z_Y)
 
     def rs_final(w):
         final = final_of(w)
@@ -440,9 +440,8 @@
 
     halves = (slice(0, half), slice(half, width))
 
-    lens = [lengths[s] for s in range(series)]
-
     def pad_of(slot):
+        lens = [lengths[s] for s in range(series)]
         total = jnp.zeros(slot.shape, jnp.int32)
         for s in range(series):
             inside = jnp.logical_and(slot >= s * seq, slot < (s + 1) * seq)
@@ -459,7 +458,13 @@
     in_head = lane - HD * jnp.floor((lane + 0.5) / HD)
     first = in_head < HD // 2
 
+    small_copies = [
+        pltpu.make_async_copy(src, dst, small_sem.at[i]) for i, (src, dst) in enumerate(zip(small_hbm, small))
+    ]
+
     def prepare():
+        for c in small_copies[:2]:
+            c.wait()
         slot_col = lax.broadcasted_iota(jnp.int32, (rows, 1), 0)
         keep = jnp.broadcast_to((slot_col >= pad_of(slot_col)).astype(f32), keep_col.shape)
         keep_col[...] = keep
@@ -783,12 +788,17 @@
     each_other_plane(
         lambda zb: pl.semaphore_signal(barrier, inc=1, device_id=plane(zb), device_id_type=MESH)
     )
+    for c in small_copies[2:] + small_copies[:2]:
+        c.start()
     order = ITEMS[1:]
     for w in order:
         own_copy(w).start()
     cot_copy = pltpu.make_async_copy(cot_hbm, cot, lsem.at[PACK])
     cot_copy.start()
 
+    for c in small_copies[2:]:
+        c.wait()
+
     @pl.when(m == 0)
     def _():
         pack_block(PK.at[0, row_of(f)], w_in1, [b_in1])
@@ -799,264 +809,264 @@
 
     pl.semaphore_wait(barrier, 6)
 
+    ag_ready(IN2)
+    ag_own_xy(IN2)
+    ag_ready(XTRA)
+    ag_own_xy(XTRA)
+    ag_ready(WOUT)
+    ag_own_xy(WOUT)
+    ag_own_z(IN2)
+    ag_column(IN2, 1)
+    ag_first_x(XTRA)
+    ag_ready(WQ)
+    ag_own_xy(WQ)
+    ag_ready(WUP)
+    ag_own_xy(WUP)
+    ag_own_xy(PACK)
+    prepare()
     ag_own_z(PACK)
+    ag_column(IN2, 2)
+    ag_column(IN2, 3)
+    ag_ready(WK)
+    ag_own_z(WK)
+    ag_own_z(WQ)
+    ag_column(PACK, 1)
+    ag_own_xy(WK)
+    ag_plane(PACK, 0)
+    ag_plane(IN2, 1)
+    ag_column(WK, 2)
+    ag_first_y(XTRA)
     ag_ready(WV)
     ag_own_xy(WV)
-    ag_ready(WQ)
-    ag_own_z(WQ)
-    ag_own_xy(PACK)
-    ag_ready(IN2)
-    ag_own_z(IN2)
-    ag_column(PACK, 1)
-    ag_ready(WK)
-    ag_own_xy(WK)
-    ag_ready(XTRA)
+    ag_own_z(WV)
+    ag_column(PACK, 2)
     ag_own_z(XTRA)
+    ag_plane(IN2, 0)
+    ag_plane(IN2, 2)
+    ag_first_d(XTRA)
+    ag_column(PACK, 3)
+    ag_plane(WK, 0)
+    ag_own_z(WOUT)
     ag_column(WQ, 1)
-    ag_own_xy(XTRA)
     ag_column(WQ, 2)
-    ag_plane(PACK, 0)
-    ag_column(PACK, 3)
-    ag_column(WQ, 3)
-    ag_first_y(XTRA)
-    ag_column(IN2, 1)
+    ag_plane(IN2, 3)
+    ag_own_z(WUP)
+    ag_column(WK, 1)
+    ag_plane(WQ, 1)
     ag_plane(PACK, 3)
-    ag_column(PACK, 2)
-    ag_own_z(WK)
-    ag_ready(WUP)
-    ag_own_xy(WUP)
-    ag_column(IN2, 3)
-    ag_column(IN2, 2)
-    ag_ready(WDOWN)
-    ag_own_xy(WDOWN)
-    ag_ready(WOUT)
-    ag_own_z(WOUT)
-    ag_own_xy(WOUT)
-    ag_column(WK, 1)
-    prepare()
-    ag_plane(IN2, 1)
     ag_plane(PACK, 1)
     ag_plane(PACK, 2)
-    ag_first_x(XTRA)
-    ag_column(WK, 2)
-    ag_plane(IN2, 3)
+    ag_column(WV, 1)
+    ag_plane(WK, 2)
     ag_last(PACK)
+    ag_column(WV, 2)
     ag_column(WK, 3)
-    ag_plane(WK, 0)
-    ag_own_xy(IN2)
-    ag_plane(IN2, 2)
-    ag_own_xy(WQ)
+    ag_column(WQ, 3)
+    ag_relay(XTRA, 1)
+    ag_column(WV, 3)
+    ag_last(IN2)
+    ag_plane(WV, 1)
     ag_plane(WQ, 2)
-    ag_first_d(XTRA)
-    ag_plane(WK, 2)
-    ag_plane(WQ, 1)
     swap_start(0)
-    ag_plane(WOUT, 0)
-    ag_plane(IN2, 0)
+    ag_plane(WK, 1)
+    ag_plane(WV, 0)
     ag_column(WOUT, 1)
     ag_relay(XTRA, 0)
-    ag_own_z(WV)
-    ag_plane(WQ, 3)
-    ag_plane(WK, 1)
+    swap_wait(0)
+    ag_plane(WV, 3)
     ag_plane(WK, 3)
-    ag_relay(XTRA, 1)
+    ag_plane(WQ, 0)
+    ag_plane(WV, 2)
+    ag_last(XTRA)
+    token_hidden()
+    ag_ready(WDOWN)
     ag_own_z(WDOWN)
-    ag_column(WV, 1)
-    ag_column(WOUT, 2)
-    ag_plane(WV, 1)
     ag_first_x(WUP)
     ag_first_y(WUP)
-    ag_plane(WQ, 0)
-    ag_column(WV, 3)
-    ag_column(WV, 2)
-    ag_own_z(WUP)
+    ag_plane(WQ, 3)
+    token_out()
+    ag_column(WOUT, 2)
+    ag_column(WOUT, 3)
+    swap_start(1)
     ag_last(WK)
-    ag_plane(WOUT, 2)
-    swap_wait(0)
-    token_hidden()
-    ag_plane(WV, 0)
-    ag_first_d(WUP)
-    ag_plane(WOUT, 1)
-    ag_last(IN2)
-    token_out()
-    swap_start(1)
-    ag_last(XTRA)
     swap_wait(1)
     ag_last(WQ)
-    ag_column(WOUT, 3)
+    ag_plane(WOUT, 1)
     norm_first()
-    ag_plane(WV, 3)
-    ag_plane(WV, 2)
+    ag_first_d(WUP)
+    ag_last(WV)
+    ag_own_xy(WDOWN)
+    ag_plane(WOUT, 0)
     project(WK, k)
+    ag_column(WDOWN, 2)
+    project_v()
+    ag_plane(WOUT, 3)
+    ag_plane(WOUT, 2)
+    project(WQ, q)
+    ag_relay(WUP, 0)
+    ag_column(WDOWN, 1)
     ag_column(WDOWN, 3)
-    project(WQ, q)
-    ag_plane(WOUT, 3)
-    ag_relay(WUP, 0)
-    ag_column(WDOWN, 2)
-    ag_column(WDOWN, 1)
-    ag_plane(WDOWN, 0)
-    ag_last(WV)
-    project_v()
     attend()
     ag_last(WOUT)
+    ag_plane(WDOWN, 0)
     attend_out()
+    ag_plane(WDOWN, 2)
     swap_start(2)
+    ag_plane(WDOWN, 1)
+    ag_relay(WUP, 1)
     ag_plane(WDOWN, 3)
-    ag_plane(WDOWN, 2)
-    ag_relay(WUP, 1)
-    ag_plane(WDOWN, 1)
     swap_wait(2)
     norm_second()
     ag_last(WUP)
     feed_up()
     grad_down()
     rs_start(WDOWN, 0)
-    rs_start(WDOWN, 1)
     ag_last(WDOWN)
     grad_hidden()
+    rs_start(WDOWN, 1)
+    grad_up()
     feed_down()
     swap_start(3)
-    grad_up()
+    rs_start(WDOWN, 2)
     rs_first_far(WUP, 0)
     grad_norm2()
+    rs_first_far(WUP, 1)
+    rs_turn(WDOWN, 0)
     swap_start(4)
+    swap_wait(3)
+    rs_turn(WDOWN, 1)
+    rs_first_near(WUP)
+    write_output()
     rs_start(WDOWN, 3)
-    rs_turn(WDOWN, 0)
-    rs_first_far(WUP, 1)
-    rs_turn(WDOWN, 1)
-    swap_wait(3)
-    write_output()
-    rs_first_near(WUP)
-    rs_start(WDOWN, 2)
     swap_wait(4)
     norm_grad2()
     grad_out()
     grad_attended()
+    rs_start(WOUT, 2)
+    rs_turn(WDOWN, 2)
+    rs_start(WOUT, 0)
+    rs_out(WDOWN, 2)
     rs_start(WOUT, 1)
-    rs_start(WOUT, 0)
     attend_back()
-    rs_start(WOUT, 3)
+    rs_relay(WUP, 0)
+    unrotate()
+    weight_grad(WQ, nrm, dq[...])
+    weight_grad(WK, nrm, dk[...])
+    rs_start(WK, 1)
     weight_grad(WV, nrm, dv[...])
-    rs_start(WV, 1)
-    rs_start(WV, 2)
-    unrotate()
-    rs_relay(WUP, 0)
-    weight_grad(WK, nrm, dk[...])
-    rs_turn(WOUT, 1)
+    rs_out(WDOWN, 3)
+    rs_start(WK, 0)
+    grad_norm1()
+    rs_turn(WOUT, 0)
+    swap_start(5)
+    rs_start(WQ, 1)
+    rs_relay(WUP, 1)
     rs_start(WV, 0)
-    rs_start(WK, 1)
-    grad_norm1()
-    rs_relay(WUP, 1)
-    swap_start(5)
-    weight_grad(WQ, nrm, dq[...])
-    rs_start(WK, 3)
+    rs_turn(WK, 0)
+    rs_first_far(XTRA, 0)
+    swap_wait(5)
+    rs_start(WQ, 0)
+    rs_turn(WK, 1)
+    norm_grad1()
+    grad_in2()
+    rs_start(IN2, 1)
+    rs_start(IN2, 0)
+    grad_token()
+    rs_first_far(XTRA, 1)
+    rs_out(WOUT, 3)
+    rs_start(IN2, 3)
+    rs_start(IN2, 2)
+    rs_start(WV, 3)
     pre_act()
-    rs_turn(WV, 0)
-    rs_out(WDOWN, 3)
-    rs_out(WOUT, 2)
-    rs_start(WK, 0)
-    swap_wait(5)
-    norm_grad1()
-    rs_turn(WV, 1)
-    rs_start(WOUT, 2)
-    rs_turn(WV, 2)
-    grad_token()
-    grad_in2()
-    rs_first_far(XTRA, 0)
-    rs_start(IN2, 2)
-    rs_turn(WK, 1)
     swap_start(6)
-    rs_start(IN2, 3)
     rs_start(WQ, 2)
+    rs_turn(WQ, 0)
     swap_wait(6)
-    rs_out(WDOWN, 2)
     grad_pre()
-    rs_out(WV, 3)
-    rs_turn(WOUT, 2)
     rs_first_near(XTRA)
-    rs_start(IN2, 1)
-    rs_out(WV, 2)
     grad_pack()
-    rs_first_far(XTRA, 1)
-    rs_out(WV, 1)
-    rs_turn(WDOWN, 2)
-    rs_start(IN2, 0)
-    rs_turn(IN2, 1)
-    rs_turn(WK, 0)
-    rs_turn(WK, 3)
-    rs_start(WV, 3)
+    rs_out(WK, 3)
+    rs_start(PACK, 0)
     rs_relay(XTRA, 0)
     rs_start(PACK, 3)
+    grad_values()
+    rs_turn(IN2, 0)
+    rs_turn(IN2, 2)
+    rs_relay(XTRA, 1)
+    rs_start(WV, 2)
+    rs_turn(IN2, 1)
+    rs_out(IN2, 3)
+    rs_turn(PACK, 3)
+    rs_out(WK, 2)
+    rs_turn(WQ, 2)
+    rs_start(WK, 2)
+    rs_turn(WQ, 1)
+    rs_zsum(WUP, 3)
+    rs_turn(WV, 2)
+    rs_turn(WV, 0)
+    rs_out(WQ, 1)
+    rs_out(IN2, 2)
+    rs_start(PACK, 1)
+    rs_start(WQ, 3)
+    rs_turn(PACK, 0)
+    rs_zsum(XTRA, 0)
+    rs_start(PACK, 2)
+    rs_turn(WOUT, 2)
+    rs_out(IN2, 1)
     rs_turn(IN2, 3)
-    rs_out(WK, 3)
-    rs_turn(IN2, 0)
-    rs_start(PACK, 1)
-    rs_start(PACK, 2)
-    rs_start(PACK, 0)
+    rs_zsum(XTRA, 3)
+    rs_out(WQ, 3)
+    rs_turn(PACK, 1)
+    rs_zsum(XTRA, 2)
+    rs_turn(PACK, 2)
+    rs_zsum(WUP, 0)
+    rs_turn(WDOWN, 3)
+    rs_start(WV, 1)
+    rs_out(WDOWN, 1)
+    rs_out(PACK, 3)
+    rs_out(WV, 3)
+    rs_out(WQ, 2)
+    rs_turn(WK, 2)
+    rs_out(PACK, 1)
+    rs_turn(WV, 3)
+    rs_out(IN2, 0)
+    rs_turn(WQ, 3)
+    rs_start(WK, 3)
+    rs_out(PACK, 2)
+    rs_turn(WV, 1)
+    rs_out(WK, 1)
+    rs_zsum(XTRA, 1)
+    rs_out(WV, 1)
+    rs_zsum(WUP, 1)
+    rs_zsum(WUP, 2)
+    rs_turn(WOUT, 1)
+    rs_out(WDOWN, 0)
+    rs_start(WOUT, 3)
+    rs_final(IN2)
+    rs_first_turn(WUP)
+    rs_out(WV, 2)
+    rs_out(WQ, 0)
+    rs_final(WDOWN)
     rs_out(WOUT, 1)
-    rs_relay(XTRA, 1)
-    rs_turn(WOUT, 0)
-    rs_out(IN2, 2)
-    rs_turn(IN2, 2)
+    rs_out(WV, 0)
+    rs_turn(WK, 3)
     rs_turn(WOUT, 3)
-    rs_out(WDOWN, 1)
-    rs_turn(WV, 3)
-    rs_zsum(XTRA, 0)
-    rs_turn(PACK, 0)
-    rs_turn(PACK, 2)
-    rs_start(WQ, 1)
-    rs_turn(PACK, 3)
-    rs_out(IN2, 3)
-    rs_turn(WDOWN, 3)
-    rs_out(IN2, 1)
-    rs_turn(PACK, 1)
-    rs_start(WK, 2)
-    rs_turn(WQ, 2)
-    rs_zsum(XTRA, 3)
-    rs_turn(WQ, 1)
-    rs_start(WQ, 3)
-    rs_out(WOUT, 3)
-    rs_zsum(WUP, 3)
-    rs_out(WV, 0)
-    rs_out(WK, 2)
+    rs_out(WOUT, 2)
+    swap_start(7)
+    rs_final(WV)
+    rs_out(PACK, 0)
+    rs_final(PACK)
+    rs_first_turn(XTRA)
+    swap_start(8)
+    rs_out(WK, 0)
+    rs_final(WQ)
+    rs_final(WUP)
+    rs_final(WK)
+    rs_final(XTRA)
     rs_out(WOUT, 0)
-    rs_turn(WK, 2)
-    rs_out(IN2, 0)
-    rs_out(PACK, 0)
-    rs_out(WQ, 1)
-    rs_out(PACK, 3)
-    rs_start(WQ, 0)
-    rs_final(IN2)
-    rs_final(WV)
-    rs_zsum(WUP, 0)
-    rs_out(PACK, 2)
-    rs_turn(WQ, 3)
-    rs_out(PACK, 1)
     rs_final(WOUT)
-    rs_turn(WQ, 0)
-    swap_start(7)
-    rs_out(WK, 0)
-    rs_zsum(WUP, 1)
-    rs_out(WQ, 2)
-    rs_zsum(WUP, 2)
-    rs_out(WDOWN, 0)
-    rs_out(WK, 1)
-    rs_first_turn(WUP)
-    rs_zsum(XTRA, 1)
-    rs_out(WQ, 3)
-    rs_zsum(XTRA, 2)
-    rs_first_turn(XTRA)
-    rs_final(PACK)
-    swap_start(8)
-    rs_final(WK)
-    rs_final(WDOWN)
     swap_wait(7)
     write_in2()
-    rs_out(WQ, 0)
-    rs_final(XTRA)
-    grad_values()
-    rs_final(WUP)
-    rs_final(WQ)
     swap_wait(8)
     write_small()
 
@@ -1381,7 +1391,18 @@
         shape(blk, half),
     )
     V = pltpu.VMEM
+    small = [
+        lengths,
+        values.T,
+        w_in1,
+        w_res,
+        b_in1[None],
+        b_in2[None],
+        g_attn[None],
+        g_mlp[None],
+    ]
     scratch = [
+        [pltpu.SMEM(lengths.shape, lengths.dtype)] + [V(a.shape, a.dtype) for a in small[1:]],
         V((NW, width, half), bf16),
         V((2, width, PL), bf16),
         V((NW, width, half), bf16),
@@ -1434,26 +1455,20 @@
         pltpu.SemaphoreType.DMA((9,)),
         pltpu.SemaphoreType.DMA((9,)),
         pltpu.SemaphoreType.DMA((9,)),
+        pltpu.SemaphoreType.DMA((len(small),)),
     ]
     results = pl.pallas_call(
         layer_kernel,
         name="layer",
         out_shape=out_shape,
-        in_specs=[pl.BlockSpec(memory_space=pltpu.SMEM)] + [vmem] * 7 + [hbm] * 6,
+        in_specs=[[hbm] * len(small)] + [hbm] * 6,
         out_specs=(hbm,) + (vmem,) * 3 + (hbm,) + (vmem,) * 3 + (hbm,) * 2 + (vmem,) + (hbm,) * 2,
         scratch_shapes=scratch,
         compiler_params=pltpu.CompilerParams(
             collective_id=0, has_side_effects=True, vmem_limit_bytes=VMEM_BYTES
         ),
     )(
-        lengths,
-        values.T,
-        w_in1,
-        w_res,
-        b_in1[None],
-        b_in2[None],
-        g_attn[None],
-        g_mlp[None],
+        small,
         w_in2,
         jnp.transpose(w_qkv, (1, 0, 2)),
         w_out.T,

time: 198 us -> 190 us (0.960)
  Pallas kernels: 197 us -> 187 us
    pallas_call x1, Pallas kernels: 194 us -> 184 us  [fused_device(): pl.pallas_call(layer_kernel, name='layer', out_shape=out_shape, in_specs=...]
where the time goes in v5:
time: 190 us; the launch traced here: 188 us
  Pallas kernels  187 us (98%)
    pallas_call x1, Pallas kernels, fused_device(): pl.pallas_call(layer_kernel, name='layer', out_shape=out_shape, in_specs=...  184 us

profile of v5, /device:TPU:0, one launch (start us, length us, event | category | flops | bytes accessed | tf_op | source)
XLA Modules:
  0.0 187.8 jit_solution(15213231099987561997)
XLA Ops:
  0.7 184.2 %layer.1 = (bf16[256,1280]{1,0:T(8,128)(2,1)}, f32[32,256]{1,0:T(8,128)}, f32[64,80]{1,0:T(8,128)}, f32[1,80]{1,0:T(1,128)}, f32[80,1280]{1,0:T(8,128)}, /*index...) custom-call(s32[4]{0:T(128)} %small_hbm_0_.1, ...), custom_call_target="tpu_custom_call" | custom-call | tf_op jit(solution)/shard_map/layer/pallas_call | solution.py:1460
  184.9 2.7 %hand_over.1 = (bf16[256,1280]{1,0:T(8,128)(2,1)}, f32[32,256]{1,0:T(8,128)}, f32[64,80]{1,0:T(8,128)}, f32[1,80]{1,0:T(1,128)}, f32[80,1280]{1,0:T(8,128)}, /*i...) custom-call(bf16[256,1280]{1,0:T(8,128)(2,1)} %get-tuple-element.39., ...), custom_call_target="tpu_custom_call" | custom-call | tf_op jit(solution)/shard_map/hand_over/pallas_call | solution.py:1493

commit v6 on v5

--- a/solution.py
+++ b/solution.py
@@ -809,265 +809,265 @@
 
     pl.semaphore_wait(barrier, 6)
 
+    ag_own_z(PACK)
+    ag_ready(WQ)
+    ag_own_z(WQ)
     ag_ready(IN2)
     ag_own_xy(IN2)
+    ag_own_z(IN2)
     ag_ready(XTRA)
     ag_own_xy(XTRA)
+    ag_ready(WV)
+    ag_own_xy(WV)
+    ag_own_xy(PACK)
+    ag_ready(WK)
+    ag_own_xy(WK)
+    ag_column(PACK, 3)
+    ag_column(WQ, 1)
     ag_ready(WOUT)
     ag_own_xy(WOUT)
-    ag_own_z(IN2)
-    ag_column(IN2, 1)
-    ag_first_x(XTRA)
-    ag_ready(WQ)
-    ag_own_xy(WQ)
+    ag_own_z(WK)
+    ag_own_z(WV)
+    ag_column(WQ, 2)
     ag_ready(WUP)
     ag_own_xy(WUP)
-    ag_own_xy(PACK)
+    ag_column(PACK, 2)
+    ag_column(PACK, 1)
+    ag_plane(IN2, 0)
+    ag_plane(PACK, 0)
     prepare()
-    ag_own_z(PACK)
+    ag_first_y(XTRA)
+    ag_plane(PACK, 3)
+    ag_plane(PACK, 2)
+    ag_first_x(XTRA)
+    ag_own_z(XTRA)
+    ag_plane(PACK, 1)
+    ag_column(IN2, 3)
+    ag_first_d(XTRA)
+    ag_column(WK, 1)
+    ag_plane(WK, 0)
+    ag_own_xy(WQ)
+    ag_own_z(WOUT)
+    ag_last(PACK)
+    ag_column(IN2, 1)
     ag_column(IN2, 2)
-    ag_column(IN2, 3)
-    ag_ready(WK)
-    ag_own_z(WK)
-    ag_own_z(WQ)
-    ag_column(PACK, 1)
-    ag_own_xy(WK)
-    ag_plane(PACK, 0)
-    ag_plane(IN2, 1)
-    ag_column(WK, 2)
-    ag_first_y(XTRA)
-    ag_ready(WV)
-    ag_own_xy(WV)
-    ag_own_z(WV)
-    ag_column(PACK, 2)
-    ag_own_z(XTRA)
-    ag_plane(IN2, 0)
-    ag_plane(IN2, 2)
-    ag_first_d(XTRA)
-    ag_column(PACK, 3)
-    ag_plane(WK, 0)
-    ag_own_z(WOUT)
-    ag_column(WQ, 1)
-    ag_column(WQ, 2)
     ag_plane(IN2, 3)
-    ag_own_z(WUP)
-    ag_column(WK, 1)
-    ag_plane(WQ, 1)
-    ag_plane(PACK, 3)
-    ag_plane(PACK, 1)
-    ag_plane(PACK, 2)
-    ag_column(WV, 1)
-    ag_plane(WK, 2)
-    ag_last(PACK)
-    ag_column(WV, 2)
-    ag_column(WK, 3)
-    ag_column(WQ, 3)
-    ag_relay(XTRA, 1)
-    ag_column(WV, 3)
-    ag_last(IN2)
-    ag_plane(WV, 1)
-    ag_plane(WQ, 2)
-    swap_start(0)
     ag_plane(WK, 1)
     ag_plane(WV, 0)
-    ag_column(WOUT, 1)
-    ag_relay(XTRA, 0)
-    swap_wait(0)
-    ag_plane(WV, 3)
-    ag_plane(WK, 3)
-    ag_plane(WQ, 0)
-    ag_plane(WV, 2)
-    ag_last(XTRA)
-    token_hidden()
+    ag_column(WV, 1)
+    ag_column(WQ, 3)
+    ag_own_z(WUP)
+    ag_plane(IN2, 1)
+    ag_plane(IN2, 2)
+    swap_start(0)
+    ag_column(WK, 2)
+    ag_plane(WV, 1)
     ag_ready(WDOWN)
     ag_own_z(WDOWN)
+    ag_plane(WQ, 2)
+    ag_plane(WQ, 0)
+    ag_last(IN2)
+    ag_plane(WQ, 3)
+    ag_relay(XTRA, 1)
     ag_first_x(WUP)
+    ag_column(WV, 2)
+    ag_column(WOUT, 1)
     ag_first_y(WUP)
-    ag_plane(WQ, 3)
+    swap_wait(0)
+    token_hidden()
     token_out()
-    ag_column(WOUT, 2)
+    ag_column(WV, 3)
+    ag_column(WK, 3)
+    swap_start(1)
+    ag_plane(WQ, 1)
+    ag_plane(WV, 2)
+    swap_wait(1)
+    ag_relay(XTRA, 0)
+    ag_plane(WV, 3)
     ag_column(WOUT, 3)
-    swap_start(1)
-    ag_last(WK)
-    swap_wait(1)
+    norm_first()
+    ag_plane(WK, 3)
     ag_last(WQ)
+    ag_plane(WK, 2)
     ag_plane(WOUT, 1)
-    norm_first()
     ag_first_d(WUP)
     ag_last(WV)
+    ag_column(WDOWN, 1)
     ag_own_xy(WDOWN)
+    ag_last(XTRA)
+    project_v()
+    ag_column(WOUT, 2)
+    ag_column(WDOWN, 3)
+    ag_relay(WUP, 1)
+    ag_plane(WOUT, 3)
+    ag_last(WK)
     ag_plane(WOUT, 0)
     project(WK, k)
+    project(WQ, q)
+    attend()
+    ag_plane(WOUT, 2)
     ag_column(WDOWN, 2)
-    project_v()
-    ag_plane(WOUT, 3)
-    ag_plane(WOUT, 2)
-    project(WQ, q)
     ag_relay(WUP, 0)
-    ag_column(WDOWN, 1)
-    ag_column(WDOWN, 3)
-    attend()
     ag_last(WOUT)
-    ag_plane(WDOWN, 0)
     attend_out()
-    ag_plane(WDOWN, 2)
     swap_start(2)
     ag_plane(WDOWN, 1)
-    ag_relay(WUP, 1)
+    ag_plane(WDOWN, 0)
+    ag_plane(WDOWN, 2)
     ag_plane(WDOWN, 3)
     swap_wait(2)
     norm_second()
     ag_last(WUP)
     feed_up()
     grad_down()
+    rs_start(WDOWN, 1)
     rs_start(WDOWN, 0)
     ag_last(WDOWN)
     grad_hidden()
-    rs_start(WDOWN, 1)
+    feed_down()
     grad_up()
-    feed_down()
+    rs_first_far(WUP, 1)
     swap_start(3)
-    rs_start(WDOWN, 2)
-    rs_first_far(WUP, 0)
     grad_norm2()
-    rs_first_far(WUP, 1)
+    rs_turn(WDOWN, 1)
     rs_turn(WDOWN, 0)
+    rs_start(WDOWN, 3)
     swap_start(4)
     swap_wait(3)
-    rs_turn(WDOWN, 1)
-    rs_first_near(WUP)
     write_output()
-    rs_start(WDOWN, 3)
+    rs_start(WDOWN, 2)
     swap_wait(4)
+    rs_out(WDOWN, 3)
+    rs_out(WDOWN, 2)
     norm_grad2()
     grad_out()
+    rs_start(WOUT, 1)
+    rs_start(WOUT, 0)
+    rs_first_far(WUP, 0)
     grad_attended()
+    rs_first_near(WUP)
     rs_start(WOUT, 2)
+    rs_relay(WUP, 1)
     rs_turn(WDOWN, 2)
-    rs_start(WOUT, 0)
-    rs_out(WDOWN, 2)
-    rs_start(WOUT, 1)
     attend_back()
+    unrotate()
+    rs_turn(WOUT, 1)
+    weight_grad(WV, nrm, dv[...])
+    rs_start(WOUT, 3)
+    weight_grad(WQ, nrm, dq[...])
+    rs_start(WQ, 2)
+    grad_norm1()
+    rs_first_far(XTRA, 1)
+    rs_turn(WOUT, 0)
+    rs_start(WQ, 1)
+    weight_grad(WK, nrm, dk[...])
+    pre_act()
+    rs_start(WK, 0)
+    swap_start(5)
+    rs_first_far(XTRA, 0)
+    rs_start(WK, 1)
     rs_relay(WUP, 0)
-    unrotate()
-    weight_grad(WQ, nrm, dq[...])
-    weight_grad(WK, nrm, dk[...])
-    rs_start(WK, 1)
-    weight_grad(WV, nrm, dv[...])
-    rs_out(WDOWN, 3)
-    rs_start(WK, 0)
-    grad_norm1()
-    rs_turn(WOUT, 0)
-    swap_start(5)
-    rs_start(WQ, 1)
-    rs_relay(WUP, 1)
-    rs_start(WV, 0)
-    rs_turn(WK, 0)
-    rs_first_far(XTRA, 0)
+    rs_start(WQ, 0)
+    rs_out(WOUT, 3)
+    rs_out(WOUT, 2)
     swap_wait(5)
-    rs_start(WQ, 0)
-    rs_turn(WK, 1)
     norm_grad1()
     grad_in2()
+    grad_token()
     rs_start(IN2, 1)
-    rs_start(IN2, 0)
-    grad_token()
-    rs_first_far(XTRA, 1)
-    rs_out(WOUT, 3)
-    rs_start(IN2, 3)
+    rs_start(WV, 0)
+    swap_start(6)
     rs_start(IN2, 2)
-    rs_start(WV, 3)
-    pre_act()
-    swap_start(6)
-    rs_start(WQ, 2)
-    rs_turn(WQ, 0)
+    rs_turn(IN2, 1)
+    rs_start(WK, 2)
+    rs_turn(WK, 1)
+    rs_turn(WV, 0)
+    rs_turn(WOUT, 2)
     swap_wait(6)
     grad_pre()
+    rs_start(IN2, 0)
     rs_first_near(XTRA)
     grad_pack()
-    rs_out(WK, 3)
+    rs_start(IN2, 3)
+    rs_turn(WK, 0)
+    rs_relay(XTRA, 1)
+    rs_relay(XTRA, 0)
+    rs_turn(IN2, 2)
+    rs_start(PACK, 2)
+    rs_out(WDOWN, 1)
+    rs_turn(WK, 2)
+    rs_start(PACK, 3)
+    rs_turn(WQ, 1)
     rs_start(PACK, 0)
-    rs_relay(XTRA, 0)
-    rs_start(PACK, 3)
-    grad_values()
-    rs_turn(IN2, 0)
-    rs_turn(IN2, 2)
-    rs_relay(XTRA, 1)
-    rs_start(WV, 2)
-    rs_turn(IN2, 1)
-    rs_out(IN2, 3)
-    rs_turn(PACK, 3)
-    rs_out(WK, 2)
-    rs_turn(WQ, 2)
-    rs_start(WK, 2)
-    rs_turn(WQ, 1)
-    rs_zsum(WUP, 3)
-    rs_turn(WV, 2)
-    rs_turn(WV, 0)
-    rs_out(WQ, 1)
     rs_out(IN2, 2)
     rs_start(PACK, 1)
+    rs_out(WV, 3)
+    rs_start(WV, 3)
+    grad_values()
+    rs_out(WK, 2)
+    rs_start(WV, 1)
+    rs_turn(IN2, 3)
+    rs_turn(PACK, 2)
+    rs_turn(PACK, 1)
+    rs_out(WK, 3)
+    rs_out(IN2, 1)
+    rs_start(WV, 2)
+    rs_out(IN2, 0)
+    rs_out(WOUT, 1)
+    rs_turn(WOUT, 3)
+    rs_turn(WV, 1)
+    rs_turn(IN2, 0)
+    rs_turn(PACK, 3)
+    rs_out(PACK, 1)
+    rs_turn(PACK, 0)
+    rs_out(PACK, 2)
+    rs_turn(WQ, 0)
+    rs_zsum(XTRA, 0)
+    rs_start(WK, 3)
+    rs_turn(WQ, 2)
+    rs_out(PACK, 3)
+    rs_zsum(XTRA, 3)
+    rs_zsum(XTRA, 2)
     rs_start(WQ, 3)
-    rs_turn(PACK, 0)
-    rs_zsum(XTRA, 0)
-    rs_start(PACK, 2)
-    rs_turn(WOUT, 2)
-    rs_out(IN2, 1)
-    rs_turn(IN2, 3)
-    rs_zsum(XTRA, 3)
+    rs_turn(WV, 2)
+    rs_turn(WDOWN, 3)
+    rs_out(IN2, 3)
+    rs_out(WV, 2)
+    rs_turn(WK, 3)
+    rs_zsum(WUP, 0)
+    rs_zsum(XTRA, 1)
+    rs_turn(WV, 3)
+    rs_out(WK, 1)
+    rs_out(WOUT, 0)
+    rs_out(WDOWN, 0)
     rs_out(WQ, 3)
-    rs_turn(PACK, 1)
-    rs_zsum(XTRA, 2)
-    rs_turn(PACK, 2)
-    rs_zsum(WUP, 0)
-    rs_turn(WDOWN, 3)
-    rs_start(WV, 1)
-    rs_out(WDOWN, 1)
-    rs_out(PACK, 3)
-    rs_out(WV, 3)
-    rs_out(WQ, 2)
-    rs_turn(WK, 2)
-    rs_out(PACK, 1)
-    rs_turn(WV, 3)
-    rs_out(IN2, 0)
     rs_turn(WQ, 3)
-    rs_start(WK, 3)
-    rs_out(PACK, 2)
-    rs_turn(WV, 1)
-    rs_out(WK, 1)
-    rs_zsum(XTRA, 1)
-    rs_out(WV, 1)
+    rs_final(WOUT)
+    rs_out(PACK, 0)
+    rs_zsum(WUP, 3)
+    rs_first_turn(XTRA)
+    rs_out(WQ, 1)
     rs_zsum(WUP, 1)
     rs_zsum(WUP, 2)
-    rs_turn(WOUT, 1)
-    rs_out(WDOWN, 0)
-    rs_start(WOUT, 3)
     rs_final(IN2)
+    rs_out(WK, 0)
+    swap_start(7)
+    rs_final(PACK)
+    rs_out(WV, 1)
     rs_first_turn(WUP)
-    rs_out(WV, 2)
+    rs_out(WQ, 2)
+    rs_final(XTRA)
+    rs_final(WDOWN)
+    swap_start(8)
+    rs_out(WV, 0)
     rs_out(WQ, 0)
-    rs_final(WDOWN)
-    rs_out(WOUT, 1)
-    rs_out(WV, 0)
-    rs_turn(WK, 3)
-    rs_turn(WOUT, 3)
-    rs_out(WOUT, 2)
-    swap_start(7)
     rs_final(WV)
-    rs_out(PACK, 0)
-    rs_final(PACK)
-    rs_first_turn(XTRA)
-    swap_start(8)
-    rs_out(WK, 0)
-    rs_final(WQ)
+    rs_final(WK)
     rs_final(WUP)
-    rs_final(WK)
-    rs_final(XTRA)
-    rs_out(WOUT, 0)
-    rs_final(WOUT)
     swap_wait(7)
     write_in2()
     swap_wait(8)
+    rs_final(WQ)
     write_small()
 
     for w in ITEMS:

time: 190 us -> 184 us (0.968)
  Pallas kernels: 187 us -> 183 us
    pallas_call x1, Pallas kernels: 184 us -> 180 us  [fused_device(): pl.pallas_call(layer_kernel, name='layer', out_shape=out_shape, in_specs=...]
where the time goes in v6:
time: 184 us; the launch traced here: 183 us
  Pallas kernels  183 us (99%)
    pallas_call x1, Pallas kernels, fused_device(): pl.pallas_call(layer_kernel, name='layer', out_shape=out_shape, in_specs=...  180 us

profile of v6, /device:TPU:0, one launch (start us, length us, event | category | flops | bytes accessed | tf_op | source)
XLA Modules:
  0.0 183.5 jit_solution(5306145989257538196)
XLA Ops:
  0.7 179.9 %layer.1 = (bf16[256,1280]{1,0:T(8,128)(2,1)}, f32[32,256]{1,0:T(8,128)}, f32[64,80]{1,0:T(8,128)}, f32[1,80]{1,0:T(1,128)}, f32[80,1280]{1,0:T(8,128)}, /*index...) custom-call(s32[4]{0:T(128)} %small_hbm_0_.1, ...), custom_call_target="tpu_custom_call" | custom-call | tf_op jit(solution)/shard_map/layer/pallas_call | solution.py:1460
  180.6 2.7 %hand_over.1 = (bf16[256,1280]{1,0:T(8,128)(2,1)}, f32[32,256]{1,0:T(8,128)}, f32[64,80]{1,0:T(8,128)}, f32[1,80]{1,0:T(1,128)}, f32[80,1280]{1,0:T(8,128)}, /*i...) custom-call(bf16[256,1280]{1,0:T(8,128)(2,1)} %get-tuple-element.39., ...), custom_call_target="tpu_custom_call" | custom-call | tf_op jit(solution)/shard_map/hand_over/pallas_call | solution.py:1493

commit v7 on v6

--- a/solution.py
+++ b/solution.py
@@ -136,7 +136,7 @@
     z_inner = inner.astype(jnp.int32)
     z_near = z + 1 - 2 * lax.rem(z, 2)
     z_far = 2 - z_high
-    z_even = lax.rem(z, 2) == 0
+    z_even = lax.rem(z + m, 2) == 0
     z_odd = jnp.logical_not(z_even)
 
     def plane(zb):
@@ -238,7 +238,7 @@
             ag_push(w, 4 * zb + cy, XN)
 
     def ag_plane(w, i):
-        even = lax.rem(nearest[i], 2) == 0
+        even = lax.rem(nearest[i] + m, 2) == 0
         ag_from_x(w, nearest[i], even)
         ag_from_y(w, nearest[i], even)
 
@@ -306,7 +306,7 @@
 
     def rs_start(w, i):
         zb = nearest[3 - i]
-        even = lax.rem(zb, 2) == 0
+        even = lax.rem(zb + m, 2) == 0
 
         @pl.when(even)
         def _():
@@ -335,7 +335,7 @@
     def rs_turn(w, i):
         zb = nearest[3 - i]
         own_x, own_y = g_block(w, 4 * zb + cx), g_block(w, 4 * zb + cy)
-        turn(w, SLOT_A + zb, lax.rem(zb, 2) == 0, own_x, own_y, SLOT_X + zb, SLOT_Y + zb)
+        turn(w, SLOT_A + zb, lax.rem(zb + m, 2) == 0, own_x, own_y, SLOT_X + zb, SLOT_Y + zb)
 
     def rs_out(w, i):
         zb = nearest[i]
@@ -810,263 +810,263 @@
     pl.semaphore_wait(barrier, 6)
 
     ag_own_z(PACK)
+    ag_ready(WUP)
+    ag_own_xy(WUP)
     ag_ready(WQ)
     ag_own_z(WQ)
+    ag_ready(WK)
+    ag_own_xy(WK)
+    ag_column(PACK, 3)
+    ag_ready(WOUT)
+    ag_own_xy(WOUT)
     ag_ready(IN2)
-    ag_own_xy(IN2)
     ag_own_z(IN2)
-    ag_ready(XTRA)
-    ag_own_xy(XTRA)
     ag_ready(WV)
     ag_own_xy(WV)
     ag_own_xy(PACK)
-    ag_ready(WK)
-    ag_own_xy(WK)
-    ag_column(PACK, 3)
+    ag_column(PACK, 1)
+    ag_column(IN2, 1)
+    ag_plane(WK, 0)
+    prepare()
+    ag_column(WQ, 3)
+    ag_column(WQ, 2)
+    ag_own_z(WV)
+    ag_ready(XTRA)
+    ag_own_xy(XTRA)
+    ag_plane(PACK, 0)
+    ag_column(PACK, 2)
+    ag_plane(PACK, 3)
+    ag_plane(IN2, 1)
+    ag_column(IN2, 3)
+    ag_plane(PACK, 1)
+    ag_own_z(WK)
+    ag_first_x(XTRA)
+    ag_plane(PACK, 2)
+    ag_column(IN2, 2)
+    ag_own_z(XTRA)
+    ag_first_y(XTRA)
+    ag_own_xy(WQ)
+    ag_column(WK, 1)
+    ag_last(PACK)
+    ag_own_xy(IN2)
+    ag_column(WV, 1)
     ag_column(WQ, 1)
-    ag_ready(WOUT)
-    ag_own_xy(WOUT)
-    ag_own_z(WK)
-    ag_own_z(WV)
-    ag_column(WQ, 2)
-    ag_ready(WUP)
-    ag_own_xy(WUP)
-    ag_column(PACK, 2)
-    ag_column(PACK, 1)
+    ag_column(WV, 2)
+    ag_plane(IN2, 2)
+    ag_plane(WK, 1)
+    ag_column(WV, 3)
+    ag_first_d(XTRA)
+    ag_own_z(WOUT)
     ag_plane(IN2, 0)
-    ag_plane(PACK, 0)
-    prepare()
-    ag_first_y(XTRA)
-    ag_plane(PACK, 3)
-    ag_plane(PACK, 2)
-    ag_first_x(XTRA)
-    ag_own_z(XTRA)
-    ag_plane(PACK, 1)
-    ag_column(IN2, 3)
-    ag_first_d(XTRA)
-    ag_column(WK, 1)
-    ag_plane(WK, 0)
-    ag_own_xy(WQ)
-    ag_own_z(WOUT)
-    ag_last(PACK)
-    ag_column(IN2, 1)
-    ag_column(IN2, 2)
-    ag_plane(IN2, 3)
-    ag_plane(WK, 1)
-    ag_plane(WV, 0)
-    ag_column(WV, 1)
-    ag_column(WQ, 3)
-    ag_own_z(WUP)
-    ag_plane(IN2, 1)
-    ag_plane(IN2, 2)
-    swap_start(0)
-    ag_column(WK, 2)
-    ag_plane(WV, 1)
+    ag_column(WK, 3)
     ag_ready(WDOWN)
     ag_own_z(WDOWN)
-    ag_plane(WQ, 2)
+    ag_plane(IN2, 3)
+    ag_relay(XTRA, 1)
+    ag_plane(WV, 0)
+    ag_first_y(WUP)
+    ag_plane(WV, 2)
+    swap_start(0)
+    swap_wait(0)
+    ag_own_z(WUP)
+    ag_first_x(WUP)
+    ag_column(WK, 2)
+    token_hidden()
+    ag_last(IN2)
     ag_plane(WQ, 0)
-    ag_last(IN2)
-    ag_plane(WQ, 3)
-    ag_relay(XTRA, 1)
-    ag_first_x(WUP)
-    ag_column(WV, 2)
-    ag_column(WOUT, 1)
-    ag_first_y(WUP)
-    swap_wait(0)
-    token_hidden()
     token_out()
-    ag_column(WV, 3)
-    ag_column(WK, 3)
     swap_start(1)
     ag_plane(WQ, 1)
-    ag_plane(WV, 2)
+    ag_plane(WV, 1)
+    ag_plane(WV, 3)
+    ag_first_d(WUP)
+    ag_plane(WK, 3)
+    ag_column(WOUT, 1)
+    ag_plane(WK, 2)
+    ag_plane(WQ, 2)
     swap_wait(1)
+    ag_plane(WQ, 3)
+    norm_first()
+    ag_last(WV)
+    ag_column(WOUT, 2)
+    ag_column(WDOWN, 1)
+    ag_column(WOUT, 3)
+    ag_plane(WOUT, 0)
+    ag_own_xy(WDOWN)
     ag_relay(XTRA, 0)
-    ag_plane(WV, 3)
-    ag_column(WOUT, 3)
-    norm_first()
-    ag_plane(WK, 3)
+    project_v()
+    ag_last(WK)
+    ag_last(XTRA)
+    ag_plane(WOUT, 1)
+    project(WK, k)
     ag_last(WQ)
-    ag_plane(WK, 2)
-    ag_plane(WOUT, 1)
-    ag_first_d(WUP)
-    ag_last(WV)
-    ag_column(WDOWN, 1)
-    ag_own_xy(WDOWN)
-    ag_last(XTRA)
-    project_v()
-    ag_column(WOUT, 2)
-    ag_column(WDOWN, 3)
+    ag_column(WDOWN, 2)
+    project(WQ, q)
+    ag_plane(WOUT, 2)
     ag_relay(WUP, 1)
     ag_plane(WOUT, 3)
-    ag_last(WK)
-    ag_plane(WOUT, 0)
-    project(WK, k)
-    project(WQ, q)
     attend()
-    ag_plane(WOUT, 2)
-    ag_column(WDOWN, 2)
+    ag_column(WDOWN, 3)
     ag_relay(WUP, 0)
     ag_last(WOUT)
     attend_out()
     swap_start(2)
     ag_plane(WDOWN, 1)
-    ag_plane(WDOWN, 0)
     ag_plane(WDOWN, 2)
     ag_plane(WDOWN, 3)
+    ag_plane(WDOWN, 0)
     swap_wait(2)
     norm_second()
     ag_last(WUP)
     feed_up()
     grad_down()
+    rs_start(WDOWN, 0)
     rs_start(WDOWN, 1)
-    rs_start(WDOWN, 0)
     ag_last(WDOWN)
     grad_hidden()
-    feed_down()
     grad_up()
     rs_first_far(WUP, 1)
+    feed_down()
     swap_start(3)
     grad_norm2()
+    swap_start(4)
     rs_turn(WDOWN, 1)
     rs_turn(WDOWN, 0)
     rs_start(WDOWN, 3)
-    swap_start(4)
+    rs_start(WDOWN, 2)
     swap_wait(3)
     write_output()
-    rs_start(WDOWN, 2)
     swap_wait(4)
-    rs_out(WDOWN, 3)
+    norm_grad2()
     rs_out(WDOWN, 2)
-    norm_grad2()
     grad_out()
     rs_start(WOUT, 1)
+    rs_first_far(WUP, 0)
     rs_start(WOUT, 0)
-    rs_first_far(WUP, 0)
+    rs_out(WDOWN, 3)
+    rs_start(WOUT, 3)
     grad_attended()
+    attend_back()
     rs_first_near(WUP)
     rs_start(WOUT, 2)
     rs_relay(WUP, 1)
-    rs_turn(WDOWN, 2)
-    attend_back()
     unrotate()
+    weight_grad(WK, nrm, dk[...])
+    rs_start(WK, 1)
+    grad_norm1()
     rs_turn(WOUT, 1)
-    weight_grad(WV, nrm, dv[...])
-    rs_start(WOUT, 3)
+    swap_start(5)
     weight_grad(WQ, nrm, dq[...])
-    rs_start(WQ, 2)
-    grad_norm1()
+    pre_act()
     rs_first_far(XTRA, 1)
     rs_turn(WOUT, 0)
-    rs_start(WQ, 1)
-    weight_grad(WK, nrm, dk[...])
-    pre_act()
-    rs_start(WK, 0)
-    swap_start(5)
-    rs_first_far(XTRA, 0)
-    rs_start(WK, 1)
-    rs_relay(WUP, 0)
-    rs_start(WQ, 0)
-    rs_out(WOUT, 3)
-    rs_out(WOUT, 2)
+    weight_grad(WV, nrm, dv[...])
+    rs_start(WQ, 2)
+    rs_first_near(XTRA)
     swap_wait(5)
     norm_grad1()
+    rs_start(WV, 0)
+    rs_start(WQ, 1)
+    rs_relay(WUP, 0)
+    grad_token()
+    swap_start(6)
     grad_in2()
-    grad_token()
     rs_start(IN2, 1)
-    rs_start(WV, 0)
-    swap_start(6)
+    rs_first_far(XTRA, 0)
+    rs_turn(WK, 1)
     rs_start(IN2, 2)
+    rs_turn(WOUT, 2)
+    rs_turn(WV, 0)
+    swap_wait(6)
+    rs_start(WV, 1)
+    rs_start(WQ, 0)
+    grad_pre()
+    rs_out(WOUT, 3)
+    rs_turn(WQ, 2)
+    rs_out(WOUT, 2)
+    grad_pack()
     rs_turn(IN2, 1)
     rs_start(WK, 2)
-    rs_turn(WK, 1)
-    rs_turn(WV, 0)
-    rs_turn(WOUT, 2)
-    swap_wait(6)
-    grad_pre()
+    rs_turn(WDOWN, 3)
+    rs_turn(WDOWN, 2)
+    rs_start(PACK, 1)
+    rs_relay(XTRA, 1)
+    rs_start(WK, 0)
+    rs_out(IN2, 2)
+    rs_turn(IN2, 2)
+    rs_start(PACK, 3)
+    rs_start(PACK, 0)
     rs_start(IN2, 0)
-    rs_first_near(XTRA)
-    grad_pack()
+    rs_start(PACK, 2)
+    rs_out(WV, 3)
+    rs_turn(WOUT, 3)
+    rs_out(WDOWN, 1)
+    rs_out(WK, 2)
+    rs_turn(WK, 2)
+    rs_turn(WK, 0)
+    rs_out(WOUT, 1)
     rs_start(IN2, 3)
-    rs_turn(WK, 0)
-    rs_relay(XTRA, 1)
+    rs_turn(IN2, 0)
+    rs_turn(WV, 1)
     rs_relay(XTRA, 0)
-    rs_turn(IN2, 2)
-    rs_start(PACK, 2)
-    rs_out(WDOWN, 1)
-    rs_turn(WK, 2)
-    rs_start(PACK, 3)
+    rs_zsum(WUP, 0)
+    rs_turn(PACK, 1)
+    rs_start(WV, 3)
+    rs_out(IN2, 1)
+    rs_turn(PACK, 0)
+    rs_out(WOUT, 0)
+    grad_values()
+    rs_start(WV, 2)
+    rs_turn(PACK, 2)
+    rs_turn(PACK, 3)
+    rs_final(WOUT)
+    rs_out(IN2, 3)
+    rs_out(WK, 1)
+    rs_start(WK, 3)
+    rs_out(WK, 3)
+    rs_turn(WQ, 0)
+    rs_turn(WV, 3)
+    rs_out(PACK, 3)
+    rs_zsum(XTRA, 0)
+    rs_turn(IN2, 3)
+    rs_out(PACK, 2)
+    rs_turn(WV, 2)
     rs_turn(WQ, 1)
-    rs_start(PACK, 0)
-    rs_out(IN2, 2)
-    rs_start(PACK, 1)
-    rs_out(WV, 3)
-    rs_start(WV, 3)
-    grad_values()
-    rs_out(WK, 2)
-    rs_start(WV, 1)
-    rs_turn(IN2, 3)
-    rs_turn(PACK, 2)
-    rs_turn(PACK, 1)
-    rs_out(WK, 3)
-    rs_out(IN2, 1)
-    rs_start(WV, 2)
+    rs_out(PACK, 1)
+    rs_turn(WK, 3)
+    rs_zsum(XTRA, 1)
+    rs_zsum(WUP, 3)
+    rs_zsum(XTRA, 3)
+    rs_out(PACK, 0)
+    rs_out(WV, 2)
+    rs_start(WQ, 3)
+    rs_zsum(WUP, 1)
+    rs_out(WDOWN, 0)
+    rs_final(WDOWN)
+    rs_out(WQ, 1)
+    rs_out(WV, 0)
     rs_out(IN2, 0)
-    rs_out(WOUT, 1)
-    rs_turn(WOUT, 3)
-    rs_turn(WV, 1)
-    rs_turn(IN2, 0)
-    rs_turn(PACK, 3)
-    rs_out(PACK, 1)
-    rs_turn(PACK, 0)
-    rs_out(PACK, 2)
-    rs_turn(WQ, 0)
-    rs_zsum(XTRA, 0)
-    rs_start(WK, 3)
-    rs_turn(WQ, 2)
-    rs_out(PACK, 3)
-    rs_zsum(XTRA, 3)
+    rs_out(WQ, 3)
+    rs_final(IN2)
+    swap_start(7)
     rs_zsum(XTRA, 2)
-    rs_start(WQ, 3)
-    rs_turn(WV, 2)
-    rs_turn(WDOWN, 3)
-    rs_out(IN2, 3)
-    rs_out(WV, 2)
-    rs_turn(WK, 3)
-    rs_zsum(WUP, 0)
-    rs_zsum(XTRA, 1)
-    rs_turn(WV, 3)
-    rs_out(WK, 1)
-    rs_out(WOUT, 0)
-    rs_out(WDOWN, 0)
-    rs_out(WQ, 3)
+    rs_out(WV, 1)
+    rs_zsum(WUP, 2)
+    rs_first_turn(WUP)
+    rs_final(PACK)
+    rs_first_turn(XTRA)
+    swap_start(8)
+    rs_out(WQ, 2)
     rs_turn(WQ, 3)
-    rs_final(WOUT)
-    rs_out(PACK, 0)
-    rs_zsum(WUP, 3)
-    rs_first_turn(XTRA)
-    rs_out(WQ, 1)
-    rs_zsum(WUP, 1)
-    rs_zsum(WUP, 2)
-    rs_final(IN2)
     rs_out(WK, 0)
-    swap_start(7)
-    rs_final(PACK)
-    rs_out(WV, 1)
-    rs_first_turn(WUP)
-    rs_out(WQ, 2)
-    rs_final(XTRA)
-    rs_final(WDOWN)
-    swap_start(8)
-    rs_out(WV, 0)
-    rs_out(WQ, 0)
     rs_final(WV)
     rs_final(WK)
-    rs_final(WUP)
     swap_wait(7)
     write_in2()
     swap_wait(8)
+    rs_final(WUP)
+    rs_final(XTRA)
+    rs_out(WQ, 0)
     rs_final(WQ)
     write_small()
 

time: 184 us -> 183 us (level)
  no operation moved by 1% of the time
where the time goes in v7:
time: 183 us
  Pallas kernels  182 us (99%)
    pallas_call x1, Pallas kernels, fused_device(): pl.pallas_call(layer_kernel, name='layer', out_shape=out_shape, in_specs=...  179 us

profile of v7, /device:TPU:0, one launch (start us, length us, event | category | flops | bytes accessed | tf_op | source)
XLA Modules:
  0.0 182.8 jit_solution(13869315653385719886)
XLA Ops:
  0.7 179.2 %layer.1 = (bf16[256,1280]{1,0:T(8,128)(2,1)}, f32[32,256]{1,0:T(8,128)}, f32[64,80]{1,0:T(8,128)}, f32[1,80]{1,0:T(1,128)}, f32[80,1280]{1,0:T(8,128)}, /*index...) custom-call(s32[4]{0:T(128)} %small_hbm_0_.1, ...), custom_call_target="tpu_custom_call" | custom-call | tf_op jit(solution)/shard_map/layer/pallas_call | solution.py:1460
  179.9 2.7 %hand_over.1 = (bf16[256,1280]{1,0:T(8,128)(2,1)}, f32[32,256]{1,0:T(8,128)}, f32[64,80]{1,0:T(8,128)}, f32[1,80]{1,0:T(1,128)}, f32[80,1280]{1,0:T(8,128)}, /*i...) custom-call(bf16[256,1280]{1,0:T(8,128)(2,1)} %get-tuple-element.39., ...), custom_call_target="tpu_custom_call" | custom-call | tf_op jit(solution)/shard_map/hand_over/pallas_call | solution.py:1493
